TPU v7x, 128 devices: a whole 4x4x4 slice. The times are simulated.
128 devices in a mesh: grp: 4 (over x), tile: 32 (over z, y, core).
Axes of the slice: x: 4, y: 4, z: 4, core: 2. Of those that a mesh axis runs over, the one named last changes fastest.
Arguments:
- rhs_fiber: float32 [8192, 256], P(('grp', 'tile')), may hold values from -6 to 6
- rhs_body: float32 [400, 4608], P('grp', 'tile'), may hold values from -6 to 6
- fiber_ops: bfloat16 [8192, 256, 256], P(('grp', 'tile')), may hold values from -0.375 to 0.375
- body_op: bfloat16 [4608, 4608], P('tile'), may hold values from -0.09375 to 0.09375
- positions: float32 [3, 524288], P(None, ('grp', 'tile')), may hold values from 0 to 1
- send_order: int32 [128, 4096], P(('grp', 'tile')), may hold values from 0 to 4095, each once within a row
- leaf_order: int32 [128, 4096], P(('grp', 'tile')), may hold values from 0 to 4095, each once within a row
- neighbours: int32 [4096, 2], P(('grp', 'tile')), may hold values 0 or 1
- attach_nucleus: int32 [8192], P(('grp', 'tile')), may hold values from 0 to 99
- attach_node: int32 [8192], P(('grp', 'tile')), may hold values from 0 to 1535
Outputs:
- sol_fiber: float32 [8192, 256], P(('grp', 'tile'))
- sol_body: float32 [400, 4608], P('grp', 'tile')
Inputs may be any that keep to these rules, and one draw needn't show every extreme that they name: `send_order`: each row is a permutation of the device's 4096 node positions, so each device sends exactly 4096 / 32 nodes to every device of its group. `leaf_order`: each row is a permutation of the device's 4096 received slots.
All inputs are finite; a program needn't handle non-finite values. No bound on the sum of `neighbours` on one device may be relied on, other than what follows from the above.
Results may differ from a plain program's by a relative error of at most 0.002.
Values may be sent and summed in bfloat16 or wider, within the bound.
No kernel may reach another device: no remote copies, remote signals or barrier semaphores. Data moves between devices by JAX's collectives and lax.ppermute only.
A program may use at most 128 MiB of HBM per device.

v0:
```python
import math

import jax
import jax.numpy as jnp
from jax import lax
from jax.sharding import PartitionSpec as P

FNODES = 64
BNODES = 1536
LEAF_PTS = 128
ITERS = 3


kappa_coef = 0.5
eps_square = 0.0025
stokes_coef = 1.0 / (16.0 * math.pi)


def padded(array, sides, width):
    for axis, dim in sides:
        devices, length = (lax.axis_size(axis), array.shape[dim])
        up = [(i, (i + 1) % devices) for i in range(devices - 1)]
        down = [(j, i) for i, j in up]
        last = lax.slice_in_dim(array, length - width, length, axis=dim)
        leading = lax.slice_in_dim(array, 0, width, axis=dim)
        before = lax.ppermute(last, axis, up)
        after = lax.ppermute(leading, axis, down)
        array = jnp.concatenate([before, array, after], axis=dim)
    return array


def stokes_block(target_pos, source_pos, source_force):
    delta_pos = target_pos[:, :, :, None] - source_pos[:, :, None, :]
    dist_square = jnp.sum(delta_pos * delta_pos, axis=1)
    along_force = jnp.sum(delta_pos * source_force[:, :, None, :], axis=1)
    inv_root = lax.rsqrt(dist_square + eps_square)
    inv_cube = inv_root * inv_root * inv_root
    terms = (
        source_force[:, :, None, :] * (dist_square + 2.0 * eps_square)[:, None]
        + delta_pos * along_force[:, None]
    ) * inv_cube[:, None]
    return stokes_coef * jnp.sum(terms, axis=3)


def window_velocity(
    leaf_pos, pos_left, pos_right, leaf_force, force_left, force_right, leaf_masks, block_size
):
    source_pos = jnp.concatenate([pos_left, leaf_pos, pos_right], axis=2)
    source_force = jnp.concatenate(
        [
            force_left * leaf_masks[:, 0, None, None],
            leaf_force,
            force_right * leaf_masks[:, 1, None, None],
        ],
        axis=2,
    )
    leaf_count = leaf_pos.shape[0]

    def shaped(array):
        return array.reshape((leaf_count // block_size, block_size) + array.shape[1:])

    def one_block(pieces):
        return stokes_block(pieces[0], pieces[1], pieces[2])

    result = lax.map(one_block, (shaped(leaf_pos), shaped(source_pos), shaped(source_force)))
    return result.reshape(leaf_pos.shape)


def inner_product(first, second):
    return jnp.sum(first[0] * second[0]) + jnp.sum(first[1] * second[1])


def local(
    rhs_fiber,
    rhs_body,
    fiber_ops,
    body_op,
    positions,
    send_order,
    leaf_order,
    neighbours,
    attach_nucleus,
    attach_node,
):
    send_index = send_order[0]
    leaf_index = leaf_order[0]
    node_count = positions.shape[1]
    leaf_count = node_count // LEAF_PTS
    block_size = math.gcd(leaf_count, 16)
    fiber_count = rhs_fiber.shape[0]
    nucleus_count = rhs_body.shape[0]
    leaf_masks = neighbours.astype(jnp.float32)
    end_cols = jnp.arange(3, dtype=jnp.int32) * FNODES
    nucleus_cols = (jnp.arange(3, dtype=jnp.int32) * BNODES)[None, :] + attach_node[:, None]

    def to_leaves(flat):
        return flat.reshape(3, leaf_count, LEAF_PTS).transpose(1, 0, 2)

    pos_recv = lax.all_to_all(
        jnp.take(positions, send_index, axis=1), "tile", split_axis=1, concat_axis=1, tiled=True
    )
    leaf_pos = to_leaves(jnp.take(pos_recv, leaf_index, axis=1))
    pos_rim = padded(leaf_pos, (("tile", 0),), 1)
    start_norm = jnp.sqrt(
        lax.psum(inner_product((rhs_fiber, rhs_body), (rhs_fiber, rhs_body)), ("grp", "tile"))
    )
    basis = [(rhs_fiber / start_norm, rhs_body / start_norm)]
    hessen = jnp.zeros((ITERS + 1, ITERS), jnp.float32)
    for j in range(ITERS):
        fiber_vec = basis[j][0]
        nucleus_vec = basis[j][1]
        fiber_bf = fiber_vec.astype(jnp.bfloat16)
        nucleus_bf = nucleus_vec.astype(jnp.bfloat16)
        fiber_out = fiber_vec + jnp.einsum(
            "fij,fj->fi", fiber_ops, fiber_bf, preferred_element_type=jnp.float32
        )
        nucleus_full = lax.all_gather(nucleus_bf, "tile", axis=1, tiled=True)
        nucleus_out = nucleus_vec + lax.dot_general(
            nucleus_full, body_op, (((1,), (1,)), ((), ())), preferred_element_type=jnp.float32
        )
        fiber_out = fiber_out.at[:, end_cols].add(
            -kappa_coef * nucleus_full[attach_nucleus[:, None], nucleus_cols].astype(jnp.float32)
        )
        fiber_ends = fiber_vec[:, end_cols]
        attach_term = (
            jnp.zeros((nucleus_count, 3 * BNODES), jnp.float32)
            .at[attach_nucleus[:, None], nucleus_cols]
            .add(fiber_ends)
        )
        nucleus_out = nucleus_out - kappa_coef * lax.psum_scatter(
            attach_term.astype(jnp.bfloat16), "tile", scatter_dimension=1, tiled=True
        ).astype(jnp.float32)
        forces = (
            fiber_vec[:, : 3 * FNODES]
            .reshape(fiber_count, 3, FNODES)
            .transpose(1, 0, 2)
            .reshape(3, node_count)
        )
        sent_forces = jnp.take(forces, send_index, axis=1)
        force_recv = lax.all_to_all(sent_forces, "tile", split_axis=1, concat_axis=1, tiled=True)
        leaf_force = to_leaves(jnp.take(force_recv, leaf_index, axis=1))
        force_rim = padded(leaf_force.astype(jnp.bfloat16), (("tile", 0),), 1).astype(
            leaf_force.dtype
        )
        force_left = force_rim[:-2]
        force_right = force_rim[2:]
        velocity = window_velocity(
            leaf_pos,
            pos_rim[:-2],
            pos_rim[2:],
            leaf_force,
            force_left,
            force_right,
            leaf_masks,
            block_size,
        )
        flat_vel = velocity.transpose(1, 0, 2).reshape(3, node_count)
        in_slots = jnp.zeros((3, node_count), jnp.float32).at[:, leaf_index].set(flat_vel)
        returned = lax.all_to_all(in_slots, "tile", split_axis=1, concat_axis=1, tiled=True)
        node_vel = jnp.zeros((3, node_count), jnp.float32).at[:, send_index].set(returned)
        hydro_term = (
            node_vel.reshape(3, fiber_count, FNODES)
            .transpose(1, 0, 2)
            .reshape(fiber_count, 3 * FNODES)
        )
        fiber_out = fiber_out + jnp.concatenate(
            [hydro_term, jnp.zeros((fiber_count, FNODES), jnp.float32)], axis=1
        )
        image = (fiber_out, nucleus_out)
        local_dots = [inner_product(image, vector) for vector in basis]
        coeffs = lax.psum(jnp.stack(local_dots), ("grp", "tile"))
        fiber_w, nucleus_w = image
        for i in range(j + 1):
            fiber_w = fiber_w - coeffs[i] * basis[i][0]
            nucleus_w = nucleus_w - coeffs[i] * basis[i][1]
        new_length = jnp.sqrt(
            lax.psum(inner_product((fiber_w, nucleus_w), (fiber_w, nucleus_w)), ("grp", "tile"))
        )
        for i in range(j + 1):
            hessen = hessen.at[i, j].set(coeffs[i])
        hessen = hessen.at[j + 1, j].set(new_length)
        if j + 1 < ITERS:
            basis.append((fiber_w / new_length, nucleus_w / new_length))
    gram = jnp.dot(hessen.T, hessen, precision=lax.Precision.HIGHEST)
    target = start_norm * hessen[0, :]
    factor = jnp.linalg.cholesky(gram)
    weights = jax.scipy.linalg.cho_solve((factor, True), target)
    sol_fiber = jnp.zeros_like(rhs_fiber)
    sol_body = jnp.zeros_like(rhs_body)
    for j in range(ITERS):
        sol_fiber = sol_fiber + weights[j] * basis[j][0]
        sol_body = sol_body + weights[j] * basis[j][1]
    return (sol_fiber, sol_body)


def solution(mesh):
    placed = (
        P(("grp", "tile"), None),
        P("grp", "tile"),
        P(("grp", "tile"), None, None),
        P("tile", None),
        P(None, ("grp", "tile")),
        P(("grp", "tile"), None),
        P(("grp", "tile"), None),
        P(("grp", "tile"), None),
        P(("grp", "tile")),
        P(("grp", "tile")),
    )
    return jax.shard_map(
        local,
        mesh=mesh,
        in_specs=placed,
        out_specs=(P(("grp", "tile"), None), P("grp", "tile")),
        check_vma=False,
    )
```

profile of v0, /device:TPU:1, one launch (start us, length us, event | category | flops | bytes accessed | tf_op | source)
XLA Modules:
  0.0 1122.8 jit_solution(4118333626098370897)
XLA Ops:
  16.8 68.6 %psum.49 = f32[]{:T(128)} all-reduce(f32[]{:T(128)S(6)} %add.304), channel_id=1, replica_groups=mesh['grp'=4,'tile'=32] {'grp','tile'}, use_global_device_ids=true, to_apply=%region_2.3 | all-reduce | flops 1 | bytes 8 | tf_op jit(solution)/shard_map/psum | solution.py:105
  89.0 15.7 %gather_fusion.8 = f32[4096,3]{1,0:T(8,128)} fusion(f32[3,4096]{0,1:T(8,128)} %copy.374, s32[4096]{0:T(1024)S(1)} %fusion.38), kind=kCustom, calls=%fused_computation.2.clone | custom fusion | bytes 114688 | tf_op jit(solution)/shard_map/jit(_take)/gather | solution.py:100
  104.7 15.7 %gather_fusion.6 = f32[4096,3]{1,0:T(8,128)} fusion(f32[3,4096]{0,1:T(8,128)} %bitcast.258, s32[4096]{0:T(1024)S(1)} %fusion.38), kind=kCustom, calls=%fused_computation.clone | custom fusion | bytes 114688 | tf_op jit(solution)/shard_map/jit(_take)/gather | solution.py:139
  120.3 3.8 broadcast_select_fusion.5
  127.0 5.0 all-to-all-start.1
  134.1 10.4 scatter_fusion.1
  148.3 25.6 %all_gather.9 = bf16[100,4608]{0,1:T(8,128)(2,1)S(1)} all-gather(bf16[100,144]{0,1:T(8,128)(2,1)S(1)} %fusion.50), channel_id=1, replica_groups=mesh['grp'=4,'tile'=32] {'tile'}, dimensions={1}, use_global_device_ids=true | all-gather | bytes 950400 | tf_op jit(solution)/shard_map/all_gather | solution.py:117
  176.7 5.7 fusion.15
  185.8 5.5 all-to-all-start
  194.1 15.7 %gather_fusion.9 = f32[4096,3]{1,0:T(8,128)} fusion(f32[3,4096]{0,1:T(8,128)} %bitcast.261, s32[4096]{0:T(1024)S(1)} %fusion.39), kind=kCustom, calls=%fused_computation.3.clone | custom fusion | bytes 114688 | tf_op jit(solution)/shard_map/jit(_take)/gather | solution.py:102
  211.8 15.7 %gather_fusion.7 = f32[4096,3]{1,0:T(8,128)} fusion(f32[3,4096]{0,1:T(8,128)} %bitcast.262, s32[4096]{0:T(1024)S(1)} %fusion.39), kind=kCustom, calls=%fused_computation.1.clone | custom fusion | bytes 114688 | tf_op jit(solution)/shard_map/jit(_take)/gather | solution.py:141
  227.4 3.9 broadcast_select_fusion.4
  235.6 3.5 collective-permute-start
  245.5 3.6 collective-permute-start.2
  250.0 14.8 %while.39 = (s32[]{:T(128)}, f32[2,16,3,128]{3,2,1,0:T(4,128)S(1)}, f32[2,16,3,384]{3,1,0,2:T(8,128)S(1)}, f32[2,16,3,128]{3,2,1,0:T(4,128)S(1)}, f32[2,16,3,384]{3,2,1,0:T(4,128)S(1)}, /*index=5*/s32[]{:T(128)}) while((s32[]{:T(128)}, f32[2,16,3,128]{3,2,1,0:T(4,128)S(1)}, f32[2,16,3,384]{3,1,0,2:T(8,128)S(1)}, ...), condition=%wide.region_7.9_spmd, body=%wide.region_3.8_spmd.sunk | while | flops 27525120 | bytes 26091612 | solution.py:65
  250.2 3.3 fusion.77
  254.1 3.3 fusion.78
  257.6 3.3 fusion.77
  261.5 3.3 fusion.78
  266.9 12.3 %scatter_custom_fusion = f32[3,4096]{0,1:T(8,128)} fusion(s32[4096]{0:T(1024)S(1)} %bitcast.302, f32[4096,3]{1,0:T(8,128)} %bitcast.266, f32[]{:T(128)} %constant.361.clone.1), kind=kCustom, calls=%fused_computation.103 | custom fusion | bytes 49664 | tf_op jit(solution)/shard_map/scatter | solution.py:158
  282.0 12.1 %all-to-all-start.2 = ((f32[3,32,128]{2,0,1:T(4,128)}), f32[3,32,128]{2,0,1:T(4,128)S(1)}, u32[]{:S(2)}, u32[]{:S(2)}) async-start(f32[3,32,128]{2,0,1:T(4,128)} %copy.382), calls=%async_computation.2 | async-start | bytes 131072 | tf_op jit(solution)/shard_map/all_to_all | solution.py:159
  295.1 6.4 all-to-all-done.2
  303.5 12.3 %scatter_custom_fusion.1 = f32[3,4096]{0,1:T(8,128)} fusion(s32[4096]{0:T(1024)S(1)} %bitcast.299, f32[4096,3]{1,0:T(8,128)} %copy.383, f32[]{:T(128)} %constant.361.clone.1), kind=kCustom, calls=%fused_computation.101 | custom fusion | bytes 49664 | tf_op jit(solution)/shard_map/scatter | solution.py:160
  323.2 63.2 %psum.50 = f32[1]{0:T(128)} all-reduce(f32[1]{0:T(128)} %bitcast.55), channel_id=1, replica_groups=mesh['grp'=4,'tile'=32] {'grp','tile'}, use_global_device_ids=true, to_apply=%region_15.17 | all-reduce | flops 1 | bytes 8 | tf_op jit(solution)/shard_map/psum | solution.py:171
  390.2 63.0 %psum.51 = f32[]{:T(128)} all-reduce(f32[]{:T(128)S(6)} %add.317), channel_id=1, replica_groups=mesh['grp'=4,'tile'=32] {'grp','tile'}, use_global_device_ids=true, to_apply=%region_18.20 | all-reduce | flops 1 | bytes 8 | tf_op jit(solution)/shard_map/psum | solution.py:177
  457.5 15.7 %gather_fusion.10 = f32[4096,3]{1,0:T(8,128)} fusion(f32[3,4096]{0,1:T(8,128)} %bitcast.263, s32[4096]{0:T(1024)S(1)} %fusion.38), kind=kCustom, calls=%fused_computation.4.clone | custom fusion | bytes 114688 | tf_op jit(solution)/shard_map/jit(_take)/gather | solution.py:139
  473.2 4.7 broadcast_select_fusion.3
  480.8 4.9 all-to-all-start.3
  485.8 6.2 fusion.16
  495.3 15.7 %gather_fusion.11 = f32[4096,3]{1,0:T(8,128)} fusion(f32[3,4096]{0,1:T(8,128)} %bitcast.264, s32[4096]{0:T(1024)S(1)} %fusion.39), kind=kCustom, calls=%fused_computation.5.clone | custom fusion | bytes 114688 | tf_op jit(solution)/shard_map/jit(_take)/gather | solution.py:141
  511.0 4.7 broadcast_select_fusion.2
  520.7 3.4 collective-permute-start.4
  524.1 26.5 %all_gather.10 = bf16[100,4608]{0,1:T(8,128)(2,1)S(1)} all-gather(bf16[100,144]{0,1:T(8,128)(2,1)S(1)} %get-tuple-element.370), channel_id=1, replica_groups=mesh['grp'=4,'tile'=32] {'tile'}, dimensions={1}, use_global_device_ids=true | all-gather | bytes 950400 | tf_op jit(solution)/shard_map/all_gather | solution.py:117
  553.7 10.4 scatter_fusion.3
  568.5 14.4 %while.40 = (s32[]{:T(128)}, f32[2,16,3,128]{3,2,1,0:T(4,128)S(1)}, f32[2,16,3,384]{3,1,0,2:T(8,128)S(1)}, f32[2,16,3,128]{3,2,1,0:T(4,128)S(1)}, f32[2,16,3,384]{3,2,1,0:T(4,128)S(1)}, /*index=5*/s32[]{:T(128)}) while((s32[]{:T(128)}, f32[2,16,3,128]{3,2,1,0:T(4,128)S(1)}, f32[2,16,3,384]{3,1,0,2:T(8,128)S(1)}, ...), condition=%wide.region_23.25_spmd, body=%wide.region_19.24_spmd.sunk | while | flops 27525120 | bytes 26091612 | solution.py:65
  568.6 3.1 fusion.79
  572.4 3.3 fusion.80
  579.6 3.3 fusion.80
  584.9 12.3 %scatter_custom_fusion.4 = f32[3,4096]{0,1:T(8,128)} fusion(s32[4096]{0:T(1024)} %bitcast.303, f32[4096,3]{1,0:T(8,128)} %bitcast.267, f32[]{:T(128)} %constant.361.clone.1), kind=kCustom, calls=%fused_computation.99 | custom fusion | bytes 49664 | tf_op jit(solution)/shard_map/scatter | solution.py:158
  600.0 5.2 all-to-all-start.4
  605.5 7.0 all-to-all-done.4
  614.5 12.4 %scatter_custom_fusion.5 = f32[3,4096]{0,1:T(8,128)} fusion(s32[4096]{0:T(1024)} %bitcast.300, f32[4096,3]{1,0:T(8,128)} %copy.397, f32[]{:T(128)} %constant.361.clone.1), kind=kCustom, calls=%fused_computation.97 | custom fusion | bytes 49664 | tf_op jit(solution)/shard_map/scatter | solution.py:160
  631.2 5.9 reduce-scatter.12.cloned.1.call-done
  642.4 66.2 %psum.52 = f32[2]{0:T(128)S(1)} all-reduce(f32[2]{0:T(128)S(1)} %pad_maximum_fusion.5), channel_id=1, replica_groups=mesh['grp'=4,'tile'=32] {'grp','tile'}, use_global_device_ids=true, to_apply=%region_33.35 | all-reduce | flops 2 | bytes 16 | tf_op jit(solution)/shard_map/psum | solution.py:171
  714.3 62.5 %psum.53 = f32[]{:T(128)} all-reduce(f32[]{:T(128)S(6)} %add.323), channel_id=1, replica_groups=mesh['grp'=4,'tile'=32] {'grp','tile'}, use_global_device_ids=true, to_apply=%region_36.38 | all-reduce | flops 1 | bytes 8 | tf_op jit(solution)/shard_map/psum | solution.py:177
  780.4 15.7 %gather_fusion.12 = f32[4096,3]{1,0:T(8,128)} fusion(f32[3,4096]{0,1:T(8,128)} %bitcast.259, s32[4096]{0:T(1024)S(1)} %fusion.38), kind=kCustom, calls=%fused_computation.6.clone | custom fusion | bytes 114688 | tf_op jit(solution)/shard_map/jit(_take)/gather | solution.py:139
  796.1 4.7 broadcast_select_fusion.1
  803.7 5.4 all-to-all-start.5
  809.2 6.3 fusion.17
  818.3 15.7 %gather_fusion.13 = f32[4096,3]{1,0:T(8,128)} fusion(f32[3,4096]{0,1:T(8,128)} %bitcast.260, s32[4096]{0:T(1024)S(1)} %fusion.39), kind=kCustom, calls=%fused_computation.7.clone | custom fusion | bytes 114688 | tf_op jit(solution)/shard_map/jit(_take)/gather | solution.py:141
  834.0 4.7 broadcast_select_fusion
  843.3 3.3 collective-permute-start.6
  846.6 25.4 %all_gather.11 = bf16[100,4608]{0,1:T(8,128)(2,1)S(1)} all-gather(bf16[100,144]{0,1:T(8,128)(2,1)S(1)} %fusion.49), channel_id=1, replica_groups=mesh['grp'=4,'tile'=32] {'tile'}, dimensions={1}, use_global_device_ids=true | all-gather | bytes 950400 | tf_op jit(solution)/shard_map/all_gather | solution.py:117
  875.0 10.4 scatter_fusion.5
  889.8 14.4 %while.41 = (s32[]{:T(128)}, f32[2,16,3,128]{3,2,1,0:T(4,128)S(1)}, f32[2,16,3,384]{3,1,0,2:T(8,128)S(1)}, f32[2,16,3,128]{3,2,1,0:T(4,128)S(1)}, f32[2,16,3,384]{3,2,1,0:T(4,128)S(1)}, /*index=5*/s32[]{:T(128)}) while((s32[]{:T(128)}, f32[2,16,3,128]{3,2,1,0:T(4,128)S(1)}, f32[2,16,3,384]{3,1,0,2:T(8,128)S(1)}, ...), condition=%wide.region_42.44_spmd, body=%wide.region_38.43_spmd.sunk | while | flops 27525120 | bytes 26091612 | solution.py:65
  893.7 3.3 fusion.82
  900.9 3.3 fusion.82
  906.2 12.3 %scatter_custom_fusion.8 = f32[3,4096]{0,1:T(8,128)} fusion(s32[4096]{0:T(1024)} %bitcast.304, f32[4096,3]{1,0:T(8,128)} %bitcast.265, f32[]{:T(128)} %constant.361.clone.1), kind=kCustom, calls=%fused_computation.95 | custom fusion | bytes 49664 | tf_op jit(solution)/shard_map/scatter | solution.py:158
  921.3 5.2 all-to-all-start.6
  929.6 4.1 all-to-all-done.6
  935.8 12.5 %scatter_custom_fusion.9 = f32[3,4096]{0,1:T(8,128)} fusion(s32[4096]{0:T(1024)} %bitcast.301, f32[4096,3]{1,0:T(8,128)} %copy.411, f32[]{:T(128)} %constant.361.clone.1), kind=kCustom, calls=%fused_computation.93 | custom fusion | bytes 49664 | tf_op jit(solution)/shard_map/scatter | solution.py:160
  952.5 5.9 reduce-scatter.14.cloned.1.call-done
  966.2 66.1 %psum.54 = f32[3]{0:T(128)S(1)} all-reduce(f32[3]{0:T(128)S(1)} %pad_maximum_fusion.6), channel_id=1, replica_groups=mesh['grp'=4,'tile'=32] {'grp','tile'}, use_global_device_ids=true, to_apply=%region_54.56 | all-reduce | flops 3 | bytes 24 | tf_op jit(solution)/shard_map/psum | solution.py:171
  1042.7 62.5 %psum.55 = f32[]{:T(128)} all-reduce(f32[]{:T(128)S(6)} %add.330), channel_id=1, replica_groups=mesh['grp'=4,'tile'=32] {'grp','tile'}, use_global_device_ids=true, to_apply=%region_57.59 | all-reduce | flops 1 | bytes 8 | tf_op jit(solution)/shard_map/psum | solution.py:177
  (329 shorter events, 168.6 us)
Async XLA Ops:
  7.2 312.8 %copy-start = (bf16[144,4608]{1,0:T(8,128)(2,1)S(1)}, bf16[144,4608]{1,0:T(8,128)(2,1)}, u32[]{:S(2)}) copy-start(bf16[144,4608]{1,0:T(8,128)(2,1)} %param.39) | copy-start | bytes 3981316
  8.7 464.5 %copy-start.31 = (pred[4096]{0:T(1024)(128)(4,1)}, pred[4096]{0:T(1024)(128)(4,1)S(1)}, u32[]{:S(2)}) copy-start(pred[4096]{0:T(1024)(128)(4,1)S(1)} %compare_and_fusion.1) | copy-start | bytes 12292
  124.2 8.0 copy-start.52
  124.2 8.0 copy-start.51
  127.0 58.8 %all-to-all-start.1 = ((f32[3,32,128]{2,0,1:T(4,128)}), f32[3,32,128]{2,0,1:T(4,128)}, u32[]{:S(2)}, u32[]{:S(2)}) async-start(f32[3,32,128]{2,0,1:T(4,128)} %copy.375), calls=%async_computation.1 | async-start | bytes 131072 | tf_op jit(solution)/shard_map/all_to_all | solution.py:99
  132.1 187.9 %reduce-scatter.10.cloned.1.call-start = ((), (), s32[]{:S(2)}) async-start(), calls=%async_computation.10 | async-start | bytes 1216512
  133.1 11.4 %copy-start.49 = (s32[1024]{0:T(1024)}, s32[1024]{0:T(1024)S(1)}, u32[]{:S(2)}) copy-start(s32[1024]{0:T(1024)S(1)} %pad_clamp_fusion) | copy-start | bytes 12292
  145.5 2.6 copy-start.10
  145.5 2.7 copy-start.50
  145.5 28.4 %copy-start.28 = (s32[64,3,1]{1,0,2:T(8,128)S(1)}, s32[64,3,1]{1,0,2:T(8,128)}, u32[]{:S(2)}) copy-start(s32[64,3,1]{1,0,2:T(8,128)} %get-tuple-element.407) | copy-start | bytes 2308
  148.0 155.5 %copy-start.37 = (s32[4096,1]{0,1:T(1,128)}, s32[4096,1]{0,1:T(1,128)S(1)}, u32[]{:S(2)}) copy-start(s32[4096,1]{0,1:T(1,128)S(1)} %compare_select_fusion.1) | copy-start | bytes 49156
  148.1 118.8 %copy-start.38 = (s32[4096,1]{0,1:T(1,128)}, s32[4096,1]{0,1:T(1,128)S(1)}, u32[]{:S(2)}) copy-start(s32[4096,1]{0,1:T(1,128)S(1)} %compare_select_fusion) | copy-start | bytes 49156
  148.1 362.9 %copy-start.33 = (pred[4096]{0:T(1024)(128)(4,1)}, pred[4096]{0:T(1024)(128)(4,1)S(1)}, u32[]{:S(2)}) copy-start(pred[4096]{0:T(1024)(128)(4,1)S(1)} %compare_and_fusion) | copy-start | bytes 12292
  148.2 101.0 %copy-start.43 = (f32[32]{0:T(128)}, f32[32]{0:T(128)S(1)}, u32[]{:S(2)}) copy-start(f32[32]{0:T(128)S(1)} %get-tuple-element.408) | copy-start | bytes 388
  148.2 101.0 %copy-start.46 = (f32[32]{0:T(128)}, f32[32]{0:T(128)S(1)}, u32[]{:S(2)}) copy-start(f32[32]{0:T(128)S(1)} %get-tuple-element.409) | copy-start | bytes 388
  185.8 23.9 %all-to-all-start = ((f32[3,32,128]{2,0,1:T(4,128)}), f32[3,32,128]{2,0,1:T(4,128)S(1)}, u32[]{:S(2)}, u32[]{:S(2)}) async-start(f32[3,32,128]{2,0,1:T(4,128)} %copy.371), calls=%async_computation | async-start | bytes 131072 | tf_op jit(solution)/shard_map/all_to_all | solution.py:140
  233.6 15.6 %collective-permute-start.1 = (bf16[1,3,128]{2,0,1:T(2,128)(2,1)S(1)}, bf16[1,3,128]{2,0,1:T(2,128)(2,1)S(1)}, u32[]{:S(2)}, u32[]{:S(2)}) collective-permute-start(bf16[1,3,128]{2,0,1:T(2,128)(2,1)S(1)} %get-tuple-element.401), channel_id=1, source_target_pairs={{1,0},{2,1},{3,2},{4,3},{5,4},{6,5},{7,6},{8,7},{9,8},{10,9},{11,1... | collective-permute-start | bytes 2312 | tf_op jit(solution)/shard_map/ppermute | solution.py:27
  235.6 13.6 %collective-permute-start = (bf16[1,3,128]{2,0,1:T(2,128)(2,1)S(1)}, bf16[1,3,128]{2,0,1:T(2,128)(2,1)S(1)}, u32[]{:S(2)}, u32[]{:S(2)}) collective-permute-start(bf16[1,3,128]{2,0,1:T(2,128)(2,1)S(1)} %get-tuple-element.400), channel_id=1, source_target_pairs={{0,1},{1,2},{2,3},{3,4},{4,5},{5,6},{6,7},{7,8},{8,9},{9,10},{10,1... | collective-permute-start | bytes 2312 | tf_op jit(solution)/shard_map/ppermute | solution.py:26
  243.6 5.7 collective-permute-start.3
  245.5 4.4 collective-permute-start.2
  264.9 14.3 %copy-start.5 = (f32[2,16,3,384]{3,2,1,0:T(4,128)}, f32[2,16,3,384]{3,2,1,0:T(4,128)S(1)}, u32[]{:S(2)}) copy-start(f32[2,16,3,384]{3,2,1,0:T(4,128)S(1)} %get-tuple-element.612) | copy-start | bytes 442372
  264.9 14.3 %copy-start.13 = (f32[2,16,3,128]{3,2,1,0:T(4,128)}, f32[2,16,3,128]{3,2,1,0:T(4,128)S(1)}, u32[]{:S(2)}) copy-start(f32[2,16,3,128]{3,2,1,0:T(4,128)S(1)} %get-tuple-element.614) | copy-start | bytes 147460
  282.0 19.5 %all-to-all-start.2 = ((f32[3,32,128]{2,0,1:T(4,128)}), f32[3,32,128]{2,0,1:T(4,128)S(1)}, u32[]{:S(2)}, u32[]{:S(2)}) async-start(f32[3,32,128]{2,0,1:T(4,128)} %copy.382), calls=%async_computation.2 | async-start | bytes 131072 | tf_op jit(solution)/shard_map/all_to_all | solution.py:159
  303.5 15.0 %copy-start.40 = (s32[3]{0:T(128)S(1)}, s32[3]{0:T(128)}, u32[]{:S(2)}) copy-start(s32[3]{0:T(128)} %copy-done.39) | copy-start | bytes 40
  480.8 12.6 %all-to-all-start.3 = ((f32[3,32,128]{2,0,1:T(4,128)}), f32[3,32,128]{2,0,1:T(4,128)S(1)}, u32[]{:S(2)}, u32[]{:S(2)}) async-start(f32[3,32,128]{2,0,1:T(4,128)} %copy.389), calls=%async_computation.3 | async-start | bytes 131072 | tf_op jit(solution)/shard_map/all_to_all | solution.py:140
  485.7 151.5 %reduce-scatter.12.cloned.1.call-start = ((), (), s32[]{:S(2)}) async-start(), calls=%async_computation.11 | async-start | bytes 1216512
  517.9 6.2 copy-start.22
  518.0 35.3 %copy-start.29 = (bf16[32,3,128]{2,0,1:T(8,128)(2,1)}, bf16[32,3,128]{2,0,1:T(8,128)(2,1)S(1)}, u32[]{:S(2)}) copy-start(bf16[32,3,128]{2,0,1:T(8,128)(2,1)S(1)} %bitcast_convert_fusion.1) | copy-start | bytes 73732
  518.6 49.0 %collective-permute-start.5 = (bf16[1,3,128]{2,0,1:T(2,128)(2,1)}, bf16[1,3,128]{2,0,1:T(2,128)(2,1)}, u32[]{:S(2)}, u32[]{:S(2)}) collective-permute-start(bf16[1,3,128]{2,0,1:T(2,128)(2,1)} %get-tuple-element.399), channel_id=1, source_target_pairs={{1,0},{2,1},{3,2},{4,3},{5,4},{6,5},{7,6},{8,7},{9,8},{10,9},{11,1... | collective-permute-start | bytes 2312 | tf_op jit(solution)/shard_map/ppermute | solution.py:27
  520.7 46.9 %collective-permute-start.4 = (bf16[1,3,128]{2,0,1:T(2,128)(2,1)}, bf16[1,3,128]{2,0,1:T(2,128)(2,1)}, u32[]{:S(2)}, u32[]{:S(2)}) collective-permute-start(bf16[1,3,128]{2,0,1:T(2,128)(2,1)} %get-tuple-element.398), channel_id=1, source_target_pairs={{0,1},{1,2},{2,3},{3,4},{4,5},{5,6},{6,7},{7,8},{8,9},{9,10},{10,1... | collective-permute-start | bytes 2312 | tf_op jit(solution)/shard_map/ppermute | solution.py:26
  565.1 3.2 copy-start.44
  565.1 3.3 copy-start.47
  565.1 3.3 copy-start.23
  565.1 3.4 copy-start.6
  565.1 3.4 copy-start.14
  584.9 20.3 %copy-start.25 = (f32[64,256]{1,0:T(8,128)S(1)}, f32[64,256]{1,0:T(8,128)}, u32[]{:S(2)}) copy-start(f32[64,256]{1,0:T(8,128)} %fusion.16) | copy-start | bytes 196612
  600.0 12.5 %all-to-all-start.4 = ((f32[3,32,128]{2,0,1:T(4,128)}), f32[3,32,128]{2,0,1:T(4,128)S(1)}, u32[]{:S(2)}, u32[]{:S(2)}) async-start(f32[3,32,128]{2,0,1:T(4,128)} %copy.396), calls=%async_computation.4 | async-start | bytes 131072 | tf_op jit(solution)/shard_map/all_to_all | solution.py:159
  614.5 15.2 %copy-start.41 = (s32[3]{0:T(128)S(1)}, s32[3]{0:T(128)}, u32[]{:S(2)}) copy-start(s32[3]{0:T(128)} %copy-done.39) | copy-start | bytes 40
  626.9 10.2 copy-start.4
  627.0 10.2 copy-start.11
  627.0 10.2 copy-start.16
  709.2 86.9 %copy-start.32 = (pred[4096]{0:T(1024)(128)(4,1)S(1)}, pred[4096]{0:T(1024)(128)(4,1)}, u32[]{:S(2)}) copy-start(pred[4096]{0:T(1024)(128)(4,1)} %copy-done.31) | copy-start | bytes 12292
  712.9 102.5 %copy-start.18 = (f32[100,144]{0,1:T(8,128)}, f32[100,144]{0,1:T(8,128)S(1)}, u32[]{:S(2)}) copy-start(f32[100,144]{0,1:T(8,128)S(1)} %get-tuple-element.367) | copy-start | bytes 172804
  714.3 86.5 %copy-start.35 = (f32[4,3]{1,0:T(4,128)}, f32[4,3]{1,0:T(4,128)S(1)}, u32[]{:S(2)}) copy-start(f32[4,3]{1,0:T(4,128)S(1)} %scatter.90) | copy-start | bytes 148
  777.5 94.5 %copy-start.8 = (f32[64,256]{0,1:T(8,128)}, f32[64,256]{0,1:T(8,128)S(1)}, u32[]{:S(2)}) copy-start(f32[64,256]{0,1:T(8,128)S(1)} %get-tuple-element.365) | copy-start | bytes 196612
  803.7 12.7 %all-to-all-start.5 = ((f32[3,32,128]{2,0,1:T(4,128)}), f32[3,32,128]{2,0,1:T(4,128)S(1)}, u32[]{:S(2)}, u32[]{:S(2)}) async-start(f32[3,32,128]{2,0,1:T(4,128)} %copy.403), calls=%async_computation.5 | async-start | bytes 131072 | tf_op jit(solution)/shard_map/all_to_all | solution.py:140
  809.0 149.4 %reduce-scatter.14.cloned.1.call-start = ((), (), s32[]{:S(2)}) async-start(), calls=%async_computation.12 | async-start | bytes 1216512
  815.4 18.5 %copy-start.34 = (pred[4096]{0:T(1024)(128)(4,1)S(1)}, pred[4096]{0:T(1024)(128)(4,1)}, u32[]{:S(2)}) copy-start(pred[4096]{0:T(1024)(128)(4,1)} %copy-done.33) | copy-start | bytes 12292
  841.0 47.9 %collective-permute-start.7 = (bf16[1,3,128]{2,0,1:T(2,128)(2,1)S(1)}, bf16[1,3,128]{2,0,1:T(2,128)(2,1)S(1)}, u32[]{:S(2)}, u32[]{:S(2)}) collective-permute-start(bf16[1,3,128]{2,0,1:T(2,128)(2,1)S(1)} %get-tuple-element.397), channel_id=1, source_target_pairs={{1,0},{2,1},{3,2},{4,3},{5,4},{6,5},{7,6},{8,7},{9,8},{10,9},{11,1... | collective-permute-start | bytes 2312 | tf_op jit(solution)/shard_map/ppermute | solution.py:27
  843.3 45.6 %collective-permute-start.6 = (bf16[1,3,128]{2,0,1:T(2,128)(2,1)S(1)}, bf16[1,3,128]{2,0,1:T(2,128)(2,1)}, u32[]{:S(2)}, u32[]{:S(2)}) collective-permute-start(bf16[1,3,128]{2,0,1:T(2,128)(2,1)S(1)} %get-tuple-element.396), channel_id=1, source_target_pairs={{0,1},{1,2},{2,3},{3,4},{4,5},{5,6},{6,7},{7,8},{8,9},{9,10},{10,1... | collective-permute-start | bytes 2312 | tf_op jit(solution)/shard_map/ppermute | solution.py:26
  886.4 3.2 copy-start.45
  886.4 3.2 copy-start.48
  886.4 3.3 copy-start.21
  886.4 3.3 copy-start.7
  886.4 3.3 copy-start.15
  906.2 20.3 %copy-start.24 = (f32[64,256]{1,0:T(8,128)S(1)}, f32[64,256]{1,0:T(8,128)}, u32[]{:S(2)}) copy-start(f32[64,256]{1,0:T(8,128)} %fusion.17) | copy-start | bytes 196612
  906.2 20.6 %copy-start.36 = (f32[4,3]{1,0:T(4,128)S(1)}, f32[4,3]{1,0:T(4,128)}, u32[]{:S(2)}) copy-start(f32[4,3]{1,0:T(4,128)} %copy-done.35) | copy-start | bytes 148
  921.3 12.5 %all-to-all-start.6 = ((f32[3,32,128]{2,0,1:T(4,128)}), f32[3,32,128]{2,0,1:T(4,128)S(1)}, u32[]{:S(2)}, u32[]{:S(2)}) async-start(f32[3,32,128]{2,0,1:T(4,128)} %copy.410), calls=%async_computation.6 | async-start | bytes 131072 | tf_op jit(solution)/shard_map/all_to_all | solution.py:159
  935.8 15.3 %copy-start.9 = (f32[64,256]{0,1:T(8,128)S(1)}, f32[64,256]{0,1:T(8,128)}, u32[]{:S(2)}) copy-start(f32[64,256]{0,1:T(8,128)} %copy-done.8) | copy-start | bytes 196612
  935.8 15.3 %copy-start.42 = (s32[3]{0:T(128)S(1)}, s32[3]{0:T(128)}, u32[]{:S(2)}) copy-start(s32[3]{0:T(128)} %copy-done.39) | copy-start | bytes 40
  948.3 10.2 copy-start.2
  948.3 10.2 copy-start.12
  948.3 10.2 copy-start.17
  948.3 10.2 copy-start.19
  (8 other events, 18.1 us)
Sparse Core Ops, SparseCore 0:
  148.1 71.7 reduce-scatter.9
  567.7 69.3 reduce-scatter.11
  889.0 69.4 reduce-scatter.13
where the time goes:
time: 1130 us; the launch traced here: 1120 us
  blocking collectives  529 us (47%)
  local copies, waits for them, and re-layouts  303 us (27%)
  other arithmetic  154 us (14%)
  starting transfers between devices  65.6 us (6%)
  between operations  33.1 us (3%)
  waiting for transfers between devices  30.9 us (3%)
    psum x3, blocking collectives, local(): coeffs = lax.psum(jnp.stack(local_dots), ('grp', 'tile'))  195 us
    psum x3, blocking collectives, local(): lax.psum(inner_product((fiber_w, nucleus_w), (fiber_w, nucleus_w)), ('grp...  188 us
    all_gather x3, blocking collectives, local(): nucleus_full = lax.all_gather(nucleus_bf, 'tile', axis=1, tiled=True)  77.5 us
    psum x1, blocking collectives, local(): lax.psum(inner_product((rhs_fiber, rhs_body), (rhs_fiber, rhs_body)), ('g...  68.6 us
    gather x3, local copies, waits for them, and re-layouts, local(): leaf_force = to_leaves(jnp.take(force_recv, leaf_index, axis=1))  47 us
    gather x3, local copies, waits for them, and re-layouts, local(): sent_forces = jnp.take(forces, send_index, axis=1)  47 us
    scatter x3, local copies, waits for them, and re-layouts, local(): jnp.zeros((3, node_count), jnp.float32).at[:, send_index].set(returned)  37.2 us
    scatter x3, local copies, waits for them, and re-layouts, local(): jnp.zeros((3, node_count), jnp.float32).at[:, leaf_index].set(flat_vel)  36.8 us
  transfers between devices with their start and end apart: 18, of which 7 were waited for; matrix products, arithmetic and copies ran while one was open for 25% of the time, Pallas kernels for 0%

commit v1 on v0

v1 whole, which is shorter than its diff:
```python
import functools
import math

import jax
import jax.numpy as jnp
from jax import lax
from jax.experimental import pallas as pl
from jax.experimental.pallas import tpu as pltpu
from jax.sharding import PartitionSpec as P

FNODES = 64
BNODES = 1536
ITERS = 3
FIB = 64
NUC = 100
ORDER = 256
COLS = 144
ROWS = 32
LANES = 128
NODES = ROWS * LANES
PAYLOAD = 152
TILES = 32
ALL = 128

kappa_coef = 0.5
eps_square = 0.0025
stokes_coef = 1.0 / (16.0 * math.pi)

F32 = jnp.float32
BF16 = jnp.bfloat16
AXES = ("grp", "tile")


def shape(dims, dtype=F32):
    return jax.ShapeDtypeStruct(dims, dtype)


VMEM = pl.BlockSpec(memory_space=pltpu.VMEM)
SMEM = pl.BlockSpec(memory_space=pltpu.SMEM)


def call(body, outs, in_specs, scratch=(), micros=1.0):
    return pl.pallas_call(
        body,
        out_shape=outs,
        in_specs=in_specs,
        out_specs=jax.tree.map(lambda _: VMEM, outs),
        scratch_shapes=list(scratch),
        cost_estimate=pl.CostEstimate(
            flops=0, transcendentals=0, bytes_accessed=int(micros * 3.6e6)
        ),
    )


def lane_iota(rows):
    return lax.broadcasted_iota(jnp.int32, (rows, LANES), 1)


def sub_iota(rows):
    return lax.broadcasted_iota(jnp.int32, (rows, LANES), 0)


def pick(read, count, row, lane):
    outs = [jnp.zeros((ROWS, LANES), F32)] * count
    for r in range(ROWS):
        hit = row == r
        for c in range(count):
            source = jnp.broadcast_to(read(c, r), (ROWS, LANES))
            found = jnp.take_along_axis(source, lane, axis=1, mode="promise_in_bounds")
            outs[c] = jnp.where(hit, found, outs[c])
    return outs


def swap_out(mix, parts, out_ref, width):
    for c in range(width):
        mix[c * ROWS : (c + 1) * ROWS, :] = parts[min(c, len(parts) - 1)]
    for d in range(ROWS):
        out_ref[d] = mix[pl.ds(d, width, stride=ROWS), :]


def fiber_table(q_ref):
    low = lane_iota(ROWS) < FNODES
    a0, a1 = q_ref[:ROWS, :LANES], q_ref[:ROWS, LANES:]
    b0, b1 = q_ref[ROWS:, :LANES], q_ref[ROWS:, LANES:]
    t0 = jnp.where(low, a0, pltpu.roll(b0, FNODES, 1))
    t1 = jnp.where(low, pltpu.roll(a0, FNODES, 1), b0)
    t2 = jnp.where(low, a1, pltpu.roll(b1, FNODES, 1))
    return t0, t1, t2


def table_place(node):
    row = (node >> 6) & 31
    lane = ((node >> 11) << 6) | (node & 63)
    return row, lane


def prep_kernel(pos_ref, q_ref, order_ref, att_ref, sent_ref, index_ref, table, mix):
    for r in range(ROWS):
        index_ref[r : r + 1, :] = order_ref[:, r * LANES : (r + 1) * LANES]
    node = index_ref[...]
    spots = pick(
        lambda c, r: pos_ref[c : c + 1, r * LANES : (r + 1) * LANES], 3, node >> 7, node & 127
    )
    for c, part in enumerate(fiber_table(q_ref)):
        table[c] = part
    row, lane = table_place(node)
    forces = pick(lambda c, r: table[c, r : r + 1, :], 3, row, lane)
    extra = [jnp.broadcast_to(att_ref[i : i + 1, :], (ROWS, LANES)) for i in range(2)]
    swap_out(mix, spots + forces + extra, sent_ref, 8)


def invert_kernel(leaf_ref, send_ref, index_ref, inv_leaf_ref, inv_send_ref):
    slots = lane_iota(64)
    upper = sub_iota(64) >= 32
    spot = sub_iota(64) & 31

    def one(place, row_of, lane_of):
        value = slots + place * LANES
        digit = jnp.where(upper, value & 63, value >> 6).astype(F32)
        left = jnp.where(row_of == spot, digit, 0.0).astype(BF16)
        right = jnp.where(lane_of == sub_iota(LANES), 1.0, 0.0).astype(BF16)
        return lax.dot_general(
            left, right, (((1,), (1,)), ((), ())), preferred_element_type=F32
        )

    leaf_sum = jnp.zeros((64, LANES), F32)
    send_sum = jnp.zeros((64, LANES), F32)
    for r in range(ROWS):
        leaf = leaf_ref[:, r * LANES : (r + 1) * LANES]
        index_ref[r : r + 1, :] = leaf
        leaf_sum = leaf_sum + one(r, leaf >> 7, leaf & 127)
        row, lane = table_place(send_ref[:, r * LANES : (r + 1) * LANES])
        send_sum = send_sum + one(r, row, lane)
    for total, ref in ((leaf_sum, inv_leaf_ref), (send_sum, inv_send_ref)):
        ref[...] = (total[:32] * 64.0 + total[32:]).astype(jnp.int32)


def payload_kernel(q_ref, z_ref, out_ref):
    out_ref[:COLS, :] = z_ref[...].astype(BF16)
    rows = []
    for half in range(2):
        part = q_ref[:, half * LANES : (half + 1) * LANES]
        high = part.astype(BF16).astype(F32)
        rows.append(jnp.concatenate([high, part - high], axis=0).T)
    where = sub_iota(8)
    ends = jnp.where(
        where == 0,
        rows[0][0:1, :],
        jnp.where(where == 1, rows[0][FNODES : FNODES + 1, :], rows[1][0:1, :]),
    )
    out_ref[COLS:, :] = ends.astype(BF16)


def leaf_kernel(first, recv_ref, index_ref, *outs):
    slot = index_ref[...]
    base = 0
    if first:
        pos_ref, force_ref, head_ref, tail_ref = outs
        parts = pick(lambda c, r: recv_ref[r, c : c + 1, :], 6, slot >> 7, slot & 127)
        for c in range(3):
            pos_ref[c] = parts[c]
            head_ref[c : c + 1, :] = parts[c][:1]
            tail_ref[c : c + 1, :] = parts[c][ROWS - 1 :]
        base = 3
    else:
        force_ref, head_ref, tail_ref = outs
        parts = pick(lambda c, r: recv_ref[r, c : c + 1, :], 3, slot >> 7, slot & 127)
    for c in range(3):
        part = parts[base + c] * stokes_coef
        force_ref[c] = part
        head_ref[3 + c : 4 + c, :] = part[:1]
        tail_ref[3 + c : 4 + c, :] = part[ROWS - 1 :]
    for c in (6, 7) if first else (0, 1, 2, 6, 7):
        head_ref[c : c + 1, :] = jnp.zeros((1, LANES), F32)
        tail_ref[c : c + 1, :] = jnp.zeros((1, LANES), F32)


def pair_sum(target, sources, total):
    for spot, force in sources:
        dx, dy, dz = (target[c] - spot[c] for c in range(3))
        along = dx * force[0] + dy * force[1] + dz * force[2]
        square = dx * dx + dy * dy + dz * dz
        root = lax.rsqrt(square + eps_square)
        cube = root * root * root
        near = (square + 2.0 * eps_square) * cube
        along = along * cube
        total = [
            t + (near * f + along * d) for t, f, d in zip(total, force, (dx, dy, dz))
        ]
    return total


def leaf_sum(target_row, sources, column, total):
    for c in range(3):
        column[c] = jnp.broadcast_to(target_row(c), (LANES, LANES)).T
    spread = [
        tuple([jnp.broadcast_to(v, (8, LANES)) for v in part] for part in source)
        for source in sources
    ]
    for g in range(LANES // 8):
        rows = slice(g * 8, g * 8 + 8)
        start = [jnp.zeros((8, LANES), F32)] * 3
        found = pair_sum([column[c, rows, :] for c in range(3)], spread, start)
        for c in range(3):
            total[c, rows, :] = found[c]
    return [jnp.sum(total[c].T, axis=0, keepdims=True) for c in range(3)]


def stokes_kernel(mask_ref, pos_ref, force_ref, out_ref, column, total):
    def leaf(i, carry):
        def rows(ref, j):
            return [ref[c, pl.ds(j, 1), :] for c in range(3)]

        before, after = jnp.maximum(i - 1, 0), jnp.minimum(i + 1, ROWS - 1)
        weak = jnp.where(i > 0, mask_ref[i, 0], 0.0)
        strong = jnp.where(i < ROWS - 1, mask_ref[i, 1], 0.0)
        sources = [
            (rows(pos_ref, i), rows(force_ref, i)),
            (rows(pos_ref, before), [f * weak for f in rows(force_ref, before)]),
            (rows(pos_ref, after), [f * strong for f in rows(force_ref, after)]),
        ]
        found = leaf_sum(lambda c: pos_ref[c, pl.ds(i, 1), :], sources, column, total)
        for c in range(3):
            out_ref[c, pl.ds(i, 1), :] = found[c]
        return carry

    lax.fori_loop(0, ROWS, leaf, 0)


def halo_kernel(
    mask_ref, vel_ref, pos_ref, bpos_ref, apos_ref, bfor_ref, afor_ref, inv_ref, out_ref,
    column, total, field, mix,
):
    field[...] = vel_ref[...]
    for i, side, spot, force in ((0, 0, bpos_ref, bfor_ref), (ROWS - 1, 1, apos_ref, afor_ref)):
        source = (
            [spot[c : c + 1, :] for c in range(3)],
            [force[3 + c : 4 + c, :] * mask_ref[i, side] for c in range(3)],
        )
        found = leaf_sum(lambda c: pos_ref[c, i : i + 1, :], [source], column, total)
        for c in range(3):
            field[c, i : i + 1, :] = field[c, i : i + 1, :] + found[c]
    slot = inv_ref[...]
    parts = pick(lambda c, r: field[c, r : r + 1, :], 3, slot >> 7, slot & 127)
    swap_out(mix, parts, out_ref, 4)


def body_kernel(base_ref, got_ref, op_ref, take_ref, mine_ref, recv_ref, z_ref, corr_ref):
    full = got_ref[:, :COLS, :].reshape(TILES * COLS, LANES)
    z = jnp.dot(op_ref[...], full, preferred_element_type=F32)
    got = jnp.dot(take_ref[...], full, preferred_element_type=F32)
    mine = mine_ref[...]
    lane = lane_iota(FIB)
    corr = jnp.zeros((FIB, LANES), F32)
    for c in range(3):
        value = jnp.sum(got[c * FIB : (c + 1) * FIB] * mine, axis=1, keepdims=True)
        corr = jnp.where(lane == c, value * -kappa_coef, corr)
    corr_ref[...] = corr
    column = (sub_iota(COLS) + base_ref[0]).astype(F32)
    nucleus = sub_iota(LANES).astype(F32)
    ends = jnp.zeros((COLS, LANES), F32)
    for s in range(TILES):
        node = recv_ref[s, 7:8, :]
        left = jnp.zeros((COLS, LANES), F32)
        for c in range(3):
            value = got_ref[s, COLS + c : COLS + c + 1, :].astype(F32)
            left = jnp.where(column == node + float(c * BNODES), value, left)
        right = jnp.where(nucleus == recv_ref[s, 6:7, :], 1.0, 0.0).astype(BF16)
        ends = ends + lax.dot_general(
            left.astype(BF16), right, (((1,), (1,)), ((), ())), preferred_element_type=F32
        )
    z_ref[...] = z - kappa_coef * ends


def assemble(back_ref, inv_ref, prod_ref, corr_ref, q_ref):
    slot = inv_ref[...]
    h0, h1, h2 = pick(lambda c, r: back_ref[r, c : c + 1, :], 3, slot >> 7, slot & 127)
    lane = lane_iota(ROWS)
    low = lane < FNODES
    blank = jnp.zeros((ROWS, LANES), F32)
    first = (
        jnp.where(low, h0, pltpu.roll(h1, FNODES, 1)),
        jnp.where(low, pltpu.roll(h0, FNODES, 1), h1),
    )
    second = (jnp.where(low, h2, blank), jnp.where(low, pltpu.roll(h2, FNODES, 1), blank))
    for half in range(2):
        rows = slice(half * ROWS, (half + 1) * ROWS)
        c0, c1, c2 = (corr_ref[rows, c : c + 1] for c in range(3))
        at0 = jnp.where(lane == 0, c0, jnp.where(lane == FNODES, c1, blank))
        at1 = jnp.where(lane == 0, c2, blank)
        q_ref[rows, :LANES] = prod_ref[rows, :LANES] + first[half] + at0
        q_ref[rows, LANES:] = prod_ref[rows, LANES:] + second[half] + at1


def join_kernel(back_ref, inv_ref, prod_ref, corr_ref, index_ref, q_ref, sent_ref, table, mix):
    assemble(back_ref, inv_ref, prod_ref, corr_ref, q_ref)
    for c, part in enumerate(fiber_table(q_ref)):
        table[c] = part
    row, lane = table_place(index_ref[...])
    forces = pick(lambda c, r: table[c, r : r + 1, :], 3, row, lane)
    swap_out(mix, forces, sent_ref, 4)


def dots_kernel(back_ref, inv_ref, prod_ref, corr_ref, *refs):
    q, z, (out_ref, last) = refs[:3], refs[3:7], refs[7:]
    assemble(back_ref, inv_ref, prod_ref, corr_ref, last)
    q = list(q) + [last]
    lane = lane_iota(1)
    line = jnp.zeros((1, LANES), F32)
    k = 0
    for i in range(4):
        for j in range(i + 1):
            total = jnp.sum(q[i][...] * q[j][...]) + jnp.sum(z[i][...] * z[j][...])
            line = jnp.where(lane == k, total, line)
            k += 1
    for d in range(ALL):
        out_ref[d] = line


def solve_kernel(gram_ref, *refs):
    q, z, (fiber_ref, body_ref) = refs[:3], refs[3:6], refs[6:]
    line = jnp.sum(gram_ref[...], axis=0)
    lane = lane_iota(1)
    g = {}
    k = 0
    for i in range(4):
        for j in range(i + 1):
            g[i, j] = g[j, i] = jnp.sum(jnp.where(lane == k, line, 0.0), axis=1, keepdims=True)
            k += 1
    n = {}
    for i in range(3):
        for j in range(i + 1):
            n[i, j] = g[i, j] + g[i + 1, j] + g[i, j + 1] + g[i + 1, j + 1]
    t = [g[0, i] + g[0, i + 1] for i in range(3)]
    l00 = jnp.sqrt(n[0, 0])
    l10, l20 = n[1, 0] / l00, n[2, 0] / l00
    l11 = jnp.sqrt(n[1, 1] - l10 * l10)
    l21 = (n[2, 1] - l20 * l10) / l11
    l22 = jnp.sqrt(n[2, 2] - l20 * l20 - l21 * l21)
    f0 = t[0] / l00
    f1 = (t[1] - l10 * f0) / l11
    f2 = (t[2] - l20 * f0 - l21 * f1) / l22
    c2 = f2 / l22
    c1 = (f1 - l21 * c2) / l11
    c0 = (f0 - l10 * c1 - l20 * c2) / l00
    fiber_ref[...] = c0 * q[0][...] + c1 * q[1][...] + c2 * q[2][...]
    body_ref[...] = c0 * z[0][...] + c1 * z[1][...] + c2 * z[2][...]


def exchange(array, axis="tile"):
    return lax.all_to_all(array, axis, split_axis=0, concat_axis=0, tiled=True)


def local(
    rhs_fiber,
    rhs_body,
    fiber_ops,
    body_op,
    positions,
    send_order,
    leaf_order,
    neighbours,
    attach_nucleus,
    attach_node,
):
    base = (lax.axis_index("tile") * COLS).astype(jnp.int32).reshape(1)
    masks = neighbours.astype(F32)
    up = [(i, i + 1) for i in range(TILES - 1)]
    down = [(i + 1, i) for i in range(TILES - 1)]
    body0 = jnp.pad(rhs_body.T, ((0, 0), (0, LANES - NUC)))
    att = jnp.stack([jnp.tile(attach_nucleus, 2), jnp.tile(attach_node, 2)]).astype(F32)
    wanted = (jnp.arange(3, dtype=jnp.int32)[:, None] * BNODES + attach_node[None, :]).reshape(-1)
    take = (wanted[:, None] == jnp.arange(3 * BNODES, dtype=jnp.int32)[None, :]).astype(BF16)
    mine = (attach_nucleus[:, None] == jnp.arange(LANES, dtype=jnp.int32)[None, :]).astype(F32)

    square = shape((ROWS, LANES), jnp.int32)
    field = shape((3, ROWS, LANES))
    edge = shape((8, LANES))
    tile3 = pltpu.VMEM((3, LANES, LANES), F32)
    table = pltpu.VMEM((3, ROWS, LANES), F32)
    mix8 = pltpu.VMEM((8 * ROWS, LANES), F32)
    mix4 = pltpu.VMEM((4 * ROWS, LANES), F32)

    sent, send_index = call(
        prep_kernel, (shape((ROWS, 8, LANES)), square), [VMEM] * 4, [table, mix8], 2.0
    )(positions, rhs_fiber, send_order, att)
    leaf_index, inv_leaf, inv_send = call(
        invert_kernel, (square, square, square), [VMEM] * 2, (), 2.0
    )(leaf_order, send_order)

    q, z = [rhs_fiber], [body0]
    info = pos = before0 = after0 = None
    for j in range(ITERS):
        recv = exchange(sent)
        payload = call(payload_kernel, shape((PAYLOAD, LANES), BF16), [VMEM] * 2)(q[j], z[j])
        got = exchange(jnp.broadcast_to(payload[None], (TILES, PAYLOAD, LANES)))
        product = jnp.einsum(
            "fij,fj->fi", fiber_ops, q[j].astype(BF16), preferred_element_type=F32
        )
        if j == 0:
            info = recv
            pos, force, head, tail = call(
                functools.partial(leaf_kernel, True), (field, field, edge, edge), [VMEM] * 2
            )(recv, leaf_index)
        else:
            force, head, tail = call(
                functools.partial(leaf_kernel, False), (field, edge, edge), [VMEM] * 2
            )(recv, leaf_index)
        before = lax.ppermute(tail, "tile", up)
        after = lax.ppermute(head, "tile", down)
        if j == 0:
            before0, after0 = before, after
        vel = call(stokes_kernel, field, [SMEM, VMEM, VMEM], [tile3, tile3], 8.0)(
            masks, pos, force
        )
        out = call(
            halo_kernel,
            shape((ROWS, 4, LANES)),
            [SMEM] + [VMEM] * 7,
            [tile3, tile3, table, mix4],
            2.0,
        )(masks, vel, pos, before0, after0, before, after, inv_leaf)
        back = exchange(out)
        image, corr = call(
            body_kernel,
            (shape((COLS, LANES)), shape((FIB, LANES))),
            [SMEM] + [VMEM] * 5,
            (),
            3.0,
        )(base, got, body_op, take, mine, info)
        z.append(image)
        if j + 1 < ITERS:
            vector, sent = call(
                join_kernel,
                (shape((FIB, ORDER)), shape((ROWS, 4, LANES))),
                [VMEM] * 5,
                [table, mix4],
                2.0,
            )(back, inv_send, product, corr, send_index)
            q.append(vector)
    line = call(
        dots_kernel,
        shape((ALL, 1, LANES)),
        [VMEM] * 11,
        [pltpu.VMEM((FIB, ORDER), F32)],
        2.0,
    )(back, inv_send, product, corr, *q, *z)
    gram = exchange(line, AXES)
    sol_fiber, sol_body = call(
        solve_kernel, (shape((FIB, ORDER)), shape((COLS, LANES))), [VMEM] * 7
    )(gram, *q, *z[:3])
    return sol_fiber, sol_body[:, :NUC].T


def solution(mesh):
    placed = (
        P(AXES, None),
        P("grp", "tile"),
        P(AXES, None, None),
        P("tile", None),
        P(None, AXES),
        P(AXES, None),
        P(AXES, None),
        P(AXES, None),
        P(AXES),
        P(AXES),
    )
    return jax.shard_map(
        local,
        mesh=mesh,
        in_specs=placed,
        out_specs=(P(AXES, None), P("grp", "tile")),
        check_vma=False,
    )
```

time: 1130 us -> 249 us (0.22)
  blocking collectives: 529 us -> 19.1 us
  local copies, waits for them, and re-layouts: 303 us -> 17.5 us
  other arithmetic: 154 us -> 4.23 us
  Pallas kernels: 0 us -> 97.1 us
  between operations: 33.1 us -> 0.91 us
  waiting for transfers between devices: 30.9 us -> 16.5 us
    psum x7 -> x0, blocking collectives: 452 us -> none  [the longest x3 195 us: local(): coeffs = lax.psum(jnp.stack(local_dots), ('grp', 'tile'))]
    gather x20 -> x0, local copies, waits for them, and re-layouts: 134 us -> none  [the longest x3 47 us: local(): leaf_force = to_leaves(jnp.take(force_recv, leaf_index, axis=1))]
    pallas_call x0 -> x21, Pallas kernels: none -> 97.1 us  [the longest x3 40 us: local(): call(stokes_kernel, field, [SMEM, VMEM, VMEM], [tile3, tile3], 8.0)]
    scatter x15 -> x0, local copies, waits for them, and re-layouts: 80.6 us -> none  [the longest x3 37.2 us: local(): jnp.zeros((3, node_count), jnp.float32).at[:, send_index].set(returned)]
    all_gather x3 -> x0, blocking collectives: 77.5 us -> none  [local(): nucleus_full = lax.all_gather(nucleus_bf, 'tile', axis=1, tiled=True)]
    reduce_sum x23 -> x0, other arithmetic: 55.3 us -> none  [the longest x6 19.6 us: stokes_block(): return stokes_coef * jnp.sum(terms, axis=3)]
    all_to_all x14 -> x0, local copies, waits for them, and re-layouts: 34.6 us -> none  [the longest x6 14.5 us: local(): lax.all_to_all(in_slots, 'tile', split_axis=1, concat_axis=1, tiled=True)]
    scatter-add x6 -> x0, other arithmetic: 33.4 us -> none  [the longest x3 31.1 us: local(): attach_term = jnp.zeros((nucleus_count, 3 * BNODES), jnp.float32).at[atta...]
  transfers between devices with their start and end apart: 18 -> 15, of which waited for: 7 -> 4; matrix products, arithmetic and copies ran while one was open for 25% -> 10% of each run, Pallas kernels for 0% -> 32%
where the time goes in v1:
time: 249 us; the launch traced here: 247 us
  Pallas kernels  97.1 us (39%)
  starting transfers between devices  74.5 us (30%)
  blocking collectives  19.1 us (8%)
  local copies, waits for them, and re-layouts  17.5 us (7%)
  matrix products  16.9 us (7%)
  waiting for transfers between devices  16.5 us (7%)
  other arithmetic  4.23 us (2%)
    all_to_all x9, starting transfers between devices, exchange(): return lax.all_to_all(array, axis, split_axis=0, concat_axis=0, tiled=True)  58.1 us
    pallas_call x3, Pallas kernels, local(): call(stokes_kernel, field, [SMEM, VMEM, VMEM], [tile3, tile3], 8.0)  40 us
    all_to_all x1, blocking collectives, exchange(): return lax.all_to_all(array, axis, split_axis=0, concat_axis=0, tiled=True)  19.1 us
    dot_general x3, matrix products, local(): jnp.einsum('fij,fj->fi', fiber_ops, q[j].astype(BF16), preferred_element_...  16.9 us
    all_to_all x9, waiting for transfers between devices, exchange(): return lax.all_to_all(array, axis, split_axis=0, concat_axis=0, tiled=True)  16.5 us
    pallas_call x3, Pallas kernels, local(): call(body_kernel, (shape((COLS, LANES)), shape((FIB, LANES))), [SMEM] + [...  13.6 us
    ppermute x3, starting transfers between devices, local(): before = lax.ppermute(tail, 'tile', up)  10.6 us
    pallas_call x3, Pallas kernels, local(): call(halo_kernel, shape((ROWS, 4, LANES)), [SMEM] + [VMEM] * 7, [tile3, t...  9.74 us
  transfers between devices with their start and end apart: 15, of which 4 were waited for; matrix products, arithmetic and copies ran while one was open for 10% of the time, Pallas kernels for 32%

profile of v1, /device:TPU:1, one launch (start us, length us, event | category | flops | bytes accessed | tf_op | source)
XLA Modules:
  0.0 246.8 jit_solution(9755927067296812473)
XLA Ops:
  0.6 0.7 tile.4
  1.4 0.7 tile.5
  2.7 3.9 %shard_map.113 = (f32[32,8,128]{2,1,0:T(8,128)}, s32[32,128]{1,0:T(8,128)}) custom-call(f32[3,4096]{1,0:T(4,128)} %pos_ref.1, f32[64,256]{1,0:T(8,128)} %refs_0_.3, s32[1,4096]{1,0:T(1,128)} %send_ref.1, f32[2,128]{1,0:T(2,128)} %add_convert_fusion.att_ref), custom_call_target="tpu_custom_call" | custom-call | bytes 7200000 | tf_op jit(solution)/shard_map/pallas_call | solution.py:384
  6.6 9.6 %all-to-all-start = ((f32[32,8,128]{2,1,0:T(8,128)}), f32[32,8,128]{2,1,0:T(8,128)S(1)}, u32[]{:S(2)}, u32[]{:S(2)}) async-start(f32[32,8,128]{2,1,0:T(8,128)} %get-tuple-element.29), calls=%async_computation | async-start | bytes 262144 | tf_op jit(solution)/shard_map/all_to_all | solution.py:351
  16.2 0.7 broadcast_add_fusion
  17.0 1.5 pad.4.z_ref.refs_3_
  18.6 1.6 shard_map.118
  20.2 3.6 %all-to-all-done.recv_ref = f32[32,8,128]{2,1,0:T(8,128)S(1)} async-done(((f32[32,8,128]{2,1,0:T(8,128)}), f32[32,8,128]{2,1,0:T(8,128)S(1)}, u32[]{:S(2)}, u32[]{:S(2)}) %all-to-all-start) | async-done | bytes 131104 | tf_op jit(solution)/shard_map/all_to_all | solution.py:351
  23.8 2.0 broadcast_in_dim.6
  25.8 4.0 %all-to-all-start.2 = ((bf16[32,152,128]{2,1,0:T(8,128)(2,1)}), bf16[32,152,128]{2,1,0:T(8,128)(2,1)S(1)}, u32[]{:S(2)}, u32[]{:S(2)}) async-start(bf16[32,152,128]{2,1,0:T(8,128)(2,1)} %broadcast_in_dim.6), calls=%async_computation.2 | async-start | bytes 2490368 | tf_op jit(solution)/shard_map/all_to_all | solution.py:351
  29.8 1.6 fusion.take_ref
  31.4 2.8 %shard_map.114 = (s32[32,128]{1,0:T(8,128)}, s32[32,128]{1,0:T(8,128)}, s32[32,128]{1,0:T(8,128)}) custom-call(s32[1,4096]{1,0:T(1,128)} %leaf_ref.1, s32[1,4096]{1,0:T(1,128)} %send_ref.1), custom_call_target="tpu_custom_call" | custom-call | bytes 7200000 | tf_op jit(solution)/shard_map/pallas_call | solution.py:387
  34.3 3.8 %shard_map.115 = (f32[3,32,128]{2,1,0:T(8,128)}, f32[3,32,128]{2,1,0:T(8,128)}, f32[8,128]{1,0:T(8,128)}, f32[8,128]{1,0:T(8,128)}) custom-call(f32[32,8,128]{2,1,0:T(8,128)} %copy-done.3, s32[32,128]{1,0:T(8,128)} %get-tuple-element.30.index_ref), custom_call_target="tpu_custom_call" | custom-call | bytes 3600000 | tf_op jit(solution)/shard_map/pallas_call | solution.py:402
  38.1 3.5 %collective-permute-start = (f32[8,128]{1,0:T(8,128)}, f32[8,128]{1,0:T(8,128)S(1)}, u32[]{:S(2)}, u32[]{:S(2)}) collective-permute-start(f32[8,128]{1,0:T(8,128)} %get-tuple-element.33), channel_id=1, source_target_pairs={{0,1},{1,2},{2,3},{3,4},{4,5},{5,6},{6,7},{7,8},{8,9},{9,10},{10,1... | collective-permute-start | bytes 12296 | tf_op jit(solution)/shard_map/ppermute | solution.py:409
  41.6 1.9 collective-permute-start.1
  43.5 5.6 %fusion.5 = f32[64,1,256]{2,1,0:T(1,128)S(1)} fusion(bf16[64,256,256]{2,1,0:T(8,128)(2,1)} %param.12, bf16[64,256,1]{1,0,2:T(8,128)(2,1)S(1)} %convert_bitcast_fusion.2), kind=kOutput, calls=%fused_computation.10 | convolution fusion | flops 8388608 | bytes 8486912 | tf_op jit(solution)/shard_map/fij,fj->fi/dot_general | solution.py:397
  49.3 0.6 convert_element_type.23.mask_ref
  49.9 13.3 %shard_map.116.vel_ref = f32[3,32,128]{2,1,0:T(8,128)} custom-call(f32[32,2]{1,0:T(8,128)} %convert_element_type.23.mask_ref, f32[3,32,128]{2,1,0:T(8,128)} %get-tuple-element.31.pos_ref, f32[3,32,128]{2,1,0:T(8,128)} %get-tuple-element.32.force_ref), custom_call_target="tpu_custom_call" | custom-call | bytes 28800000 | tf_op jit(solution)/shard_map/pallas_call | solution.py:413
  63.8 3.2 %shard_map.117 = f32[32,4,128]{2,1,0:T(4,128)} custom-call(f32[32,2]{1,0:T(8,128)} %convert_element_type.23.mask_ref, f32[3,32,128]{2,1,0:T(8,128)} %shard_map.116.vel_ref, f32[3,32,128]{2,1,0:T(8,128)} %get-tuple-element.31.pos_ref, f32[8,128]{1,0:T(8,128)} %copy-done.12, f32[8,128]{1,0:T(8,128)} %copy-done.13, f32[8,128]{1,0:T(8,128)} %copy-done.12, ...), custom_call_target="tpu_custom_call" | custom-call | bytes 7200000 | tf_op jit(solution)/shard_map/pallas_call | solution.py:416
  67.1 7.6 %all-to-all-start.1 = ((f32[32,4,128]{2,1,0:T(4,128)}), f32[32,4,128]{2,1,0:T(4,128)S(1)}, u32[]{:S(2)}, u32[]{:S(2)}) async-start(f32[32,4,128]{2,1,0:T(4,128)} %shard_map.117), calls=%async_computation.1 | async-start | bytes 131072 | tf_op jit(solution)/shard_map/all_to_all | solution.py:351
  74.7 0.7 fusion.7.mine_ref
  75.4 0.6 copy.30
  76.0 4.5 %shard_map.119 = (f32[144,128]{1,0:T(8,128)}, f32[64,128]{1,0:T(8,128)}) custom-call(s32[1]{0:T(128)} %bitcast.2.base_ref, bf16[32,152,128]{2,1,0:T(8,128)(2,1)} %copy-done, bf16[144,4608]{1,0:T(8,128)(2,1)} %op_ref.5, bf16[192,4608]{1,0:T(8,128)(2,1)} %fusion.take_ref, f32[64,128]{1,0:T(8,128)} %fusion.7.mine_ref, f32[32,8,128]{2,1,0:T(8,128)} %copy-done.3), custom_call_target="tpu_custom_call" | custom-call | bytes 10800000 | tf_op jit(solution)/shard_map/pallas_call | solution.py:424
  80.5 1.5 all-to-all-done.1.back_ref
  82.0 0.6 copy-done.7
  82.6 4.0 %shard_map.120 = (f32[64,256]{1,0:T(8,128)}, f32[32,4,128]{2,1,0:T(4,128)}) custom-call(f32[32,4,128]{2,1,0:T(4,128)} %copy-done.7, s32[32,128]{1,0:T(8,128)} %get-tuple-element.36.inv_ref, f32[64,256]{1,0:T(8,128)} %bitcast.22, f32[64,128]{1,0:T(8,128)} %get-tuple-element.37.corr_ref, s32[32,128]{1,0:T(8,128)} %get-tuple-element.38.index_ref), custom_call_target="tpu_custom_call" | custom-call | bytes 7200000 | tf_op jit(solution)/shard_map/pallas_call | solution.py:433
  86.7 6.0 %all-to-all-start.3 = ((f32[32,4,128]{2,1,0:T(4,128)}), f32[32,4,128]{2,1,0:T(4,128)S(1)}, u32[]{:S(2)}, u32[]{:S(2)}) async-start(f32[32,4,128]{2,1,0:T(4,128)} %get-tuple-element.39), calls=%async_computation.3 | async-start | bytes 131072 | tf_op jit(solution)/shard_map/all_to_all | solution.py:351
  92.7 1.6 shard_map.124
  94.3 5.7 %all-to-all-done.3.recv_ref = f32[32,4,128]{2,1,0:T(4,128)S(1)} async-done(((f32[32,4,128]{2,1,0:T(4,128)}), f32[32,4,128]{2,1,0:T(4,128)S(1)}, u32[]{:S(2)}, u32[]{:S(2)}) %all-to-all-start.3) | async-done | bytes 65568 | tf_op jit(solution)/shard_map/all_to_all | solution.py:351
  100.0 2.0 broadcast_in_dim.7
  102.0 4.2 %all-to-all-start.5 = ((bf16[32,152,128]{2,1,0:T(8,128)(2,1)}), bf16[32,152,128]{2,1,0:T(8,128)(2,1)S(1)}, u32[]{:S(2)}, u32[]{:S(2)}) async-start(bf16[32,152,128]{2,1,0:T(8,128)(2,1)} %broadcast_in_dim.7), calls=%async_computation.5 | async-start | bytes 2490368 | tf_op jit(solution)/shard_map/all_to_all | solution.py:351
  106.2 2.6 %shard_map.121 = (f32[3,32,128]{2,1,0:T(8,128)}, f32[8,128]{1,0:T(8,128)}, f32[8,128]{1,0:T(8,128)}) custom-call(f32[32,4,128]{2,1,0:T(4,128)} %copy-done.11, s32[32,128]{1,0:T(8,128)} %get-tuple-element.30.index_ref), custom_call_target="tpu_custom_call" | custom-call | bytes 3600000 | tf_op jit(solution)/shard_map/pallas_call | solution.py:406
  108.8 3.5 %collective-permute-start.2 = (f32[8,128]{1,0:T(8,128)}, f32[8,128]{1,0:T(8,128)S(1)}, u32[]{:S(2)}, u32[]{:S(2)}) collective-permute-start(f32[8,128]{1,0:T(8,128)} %get-tuple-element.41), channel_id=1, source_target_pairs={{0,1},{1,2},{2,3},{3,4},{4,5},{5,6},{6,7},{7,8},{8,9},{9,10},{10,1... | collective-permute-start | bytes 12296 | tf_op jit(solution)/shard_map/ppermute | solution.py:409
  112.4 1.9 collective-permute-start.3
  114.3 13.3 %shard_map.122.vel_ref = f32[3,32,128]{2,1,0:T(8,128)} custom-call(f32[32,2]{1,0:T(8,128)} %convert_element_type.23.mask_ref, f32[3,32,128]{2,1,0:T(8,128)} %get-tuple-element.31.pos_ref, f32[3,32,128]{2,1,0:T(8,128)} %get-tuple-element.40.force_ref), custom_call_target="tpu_custom_call" | custom-call | bytes 28800000 | tf_op jit(solution)/shard_map/pallas_call | solution.py:413
  127.6 0.6 copy-done.16
  128.2 0.6 copy-done.17
  128.8 3.2 %shard_map.123 = f32[32,4,128]{2,1,0:T(4,128)} custom-call(f32[32,2]{1,0:T(8,128)} %convert_element_type.23.mask_ref, f32[3,32,128]{2,1,0:T(8,128)} %shard_map.122.vel_ref, f32[3,32,128]{2,1,0:T(8,128)} %get-tuple-element.31.pos_ref, f32[8,128]{1,0:T(8,128)} %copy-done.12, f32[8,128]{1,0:T(8,128)} %copy-done.13, f32[8,128]{1,0:T(8,128)} %copy-done.16, ...), custom_call_target="tpu_custom_call" | custom-call | bytes 7200000 | tf_op jit(solution)/shard_map/pallas_call | solution.py:416
  132.1 7.6 %all-to-all-start.4 = ((f32[32,4,128]{2,1,0:T(4,128)}), f32[32,4,128]{2,1,0:T(4,128)S(1)}, u32[]{:S(2)}, u32[]{:S(2)}) async-start(f32[32,4,128]{2,1,0:T(4,128)} %shard_map.123), calls=%async_computation.4 | async-start | bytes 131072 | tf_op jit(solution)/shard_map/all_to_all | solution.py:351
  139.7 5.6 %fusion.3 = f32[64,1,256]{2,1,0:T(1,128)S(1)} fusion(bf16[64,256,256]{2,1,0:T(8,128)(2,1)} %param.12, bf16[64,256,1]{1,0,2:T(8,128)(2,1)S(1)} %convert_bitcast_fusion.1), kind=kOutput, calls=%fused_computation.7 | convolution fusion | flops 8388608 | bytes 8486912 | tf_op jit(solution)/shard_map/fij,fj->fi/dot_general | solution.py:397
  145.3 0.7 copy.29
  146.0 4.5 %shard_map.125 = (f32[144,128]{1,0:T(8,128)}, f32[64,128]{1,0:T(8,128)}) custom-call(s32[1]{0:T(128)} %bitcast.2.base_ref, bf16[32,152,128]{2,1,0:T(8,128)(2,1)} %copy-done.2, bf16[144,4608]{1,0:T(8,128)(2,1)} %op_ref.5, bf16[192,4608]{1,0:T(8,128)(2,1)} %fusion.take_ref, f32[64,128]{1,0:T(8,128)} %fusion.7.mine_ref, f32[32,8,128]{2,1,0:T(8,128)} %copy-done.3), custom_call_target="tpu_custom_call" | custom-call | bytes 10800000 | tf_op jit(solution)/shard_map/pallas_call | solution.py:424
  150.5 0.6 copy-done.9
  151.1 4.0 %shard_map.126 = (f32[64,256]{1,0:T(8,128)}, f32[32,4,128]{2,1,0:T(4,128)}) custom-call(f32[32,4,128]{2,1,0:T(4,128)} %copy-done.9, s32[32,128]{1,0:T(8,128)} %get-tuple-element.36.inv_ref, f32[64,256]{1,0:T(8,128)} %bitcast.24, f32[64,128]{1,0:T(8,128)} %get-tuple-element.45.corr_ref, s32[32,128]{1,0:T(8,128)} %get-tuple-element.38.index_ref), custom_call_target="tpu_custom_call" | custom-call | bytes 7200000 | tf_op jit(solution)/shard_map/pallas_call | solution.py:433
  155.2 7.5 %all-to-all-start.6 = ((f32[32,4,128]{2,1,0:T(4,128)}), f32[32,4,128]{2,1,0:T(4,128)S(1)}, u32[]{:S(2)}, u32[]{:S(2)}) async-start(f32[32,4,128]{2,1,0:T(4,128)} %get-tuple-element.46), calls=%async_computation.6 | async-start | bytes 131072 | tf_op jit(solution)/shard_map/all_to_all | solution.py:351
  162.7 1.6 shard_map.130
  164.3 5.7 %all-to-all-done.6.recv_ref = f32[32,4,128]{2,1,0:T(4,128)S(1)} async-done(((f32[32,4,128]{2,1,0:T(4,128)}), f32[32,4,128]{2,1,0:T(4,128)S(1)}, u32[]{:S(2)}, u32[]{:S(2)}) %all-to-all-start.6) | async-done | bytes 65568 | tf_op jit(solution)/shard_map/all_to_all | solution.py:351
  170.0 2.0 broadcast_in_dim.8
  172.0 4.0 %all-to-all-start.8 = ((bf16[32,152,128]{2,1,0:T(8,128)(2,1)}), bf16[32,152,128]{2,1,0:T(8,128)(2,1)S(1)}, u32[]{:S(2)}, u32[]{:S(2)}) async-start(bf16[32,152,128]{2,1,0:T(8,128)(2,1)} %broadcast_in_dim.8), calls=%async_computation.8 | async-start | bytes 2490368 | tf_op jit(solution)/shard_map/all_to_all | solution.py:351
  176.0 2.6 %shard_map.127 = (f32[3,32,128]{2,1,0:T(8,128)}, f32[8,128]{1,0:T(8,128)}, f32[8,128]{1,0:T(8,128)}) custom-call(f32[32,4,128]{2,1,0:T(4,128)} %copy-done.10, s32[32,128]{1,0:T(8,128)} %get-tuple-element.30.index_ref), custom_call_target="tpu_custom_call" | custom-call | bytes 3600000 | tf_op jit(solution)/shard_map/pallas_call | solution.py:406
  178.6 3.5 %collective-permute-start.4 = (f32[8,128]{1,0:T(8,128)}, f32[8,128]{1,0:T(8,128)S(1)}, u32[]{:S(2)}, u32[]{:S(2)}) collective-permute-start(f32[8,128]{1,0:T(8,128)} %get-tuple-element.48), channel_id=1, source_target_pairs={{0,1},{1,2},{2,3},{3,4},{4,5},{5,6},{6,7},{7,8},{8,9},{9,10},{10,1... | collective-permute-start | bytes 12296 | tf_op jit(solution)/shard_map/ppermute | solution.py:409
  182.2 1.9 collective-permute-start.5
  184.1 13.3 %shard_map.128.vel_ref = f32[3,32,128]{2,1,0:T(8,128)} custom-call(f32[32,2]{1,0:T(8,128)} %convert_element_type.23.mask_ref, f32[3,32,128]{2,1,0:T(8,128)} %get-tuple-element.31.pos_ref, f32[3,32,128]{2,1,0:T(8,128)} %get-tuple-element.47.force_ref), custom_call_target="tpu_custom_call" | custom-call | bytes 28800000 | tf_op jit(solution)/shard_map/pallas_call | solution.py:413
  197.5 0.6 copy-done.14
  198.6 3.2 %shard_map.129 = f32[32,4,128]{2,1,0:T(4,128)} custom-call(f32[32,2]{1,0:T(8,128)} %convert_element_type.23.mask_ref, f32[3,32,128]{2,1,0:T(8,128)} %shard_map.128.vel_ref, f32[3,32,128]{2,1,0:T(8,128)} %get-tuple-element.31.pos_ref, f32[8,128]{1,0:T(8,128)} %copy-done.12, f32[8,128]{1,0:T(8,128)} %copy-done.13, f32[8,128]{1,0:T(8,128)} %copy-done.14, ...), custom_call_target="tpu_custom_call" | custom-call | bytes 7200000 | tf_op jit(solution)/shard_map/pallas_call | solution.py:416
  201.9 7.6 %all-to-all-start.7 = ((f32[32,4,128]{2,1,0:T(4,128)}), f32[32,4,128]{2,1,0:T(4,128)S(1)}, u32[]{:S(2)}, u32[]{:S(2)}) async-start(f32[32,4,128]{2,1,0:T(4,128)} %shard_map.129), calls=%async_computation.7 | async-start | bytes 131072 | tf_op jit(solution)/shard_map/all_to_all | solution.py:351
  209.5 5.6 %fusion.1 = f32[64,1,256]{2,1,0:T(1,128)S(1)} fusion(bf16[64,256,256]{2,1,0:T(8,128)(2,1)} %param.12, bf16[64,256,1]{1,0,2:T(8,128)(2,1)S(1)} %convert_bitcast_fusion), kind=kOutput, calls=%fused_computation.4 | convolution fusion | flops 8388608 | bytes 8486912 | tf_op jit(solution)/shard_map/fij,fj->fi/dot_general | solution.py:397
  215.1 0.6 copy.28
  215.8 4.5 %shard_map.131 = (f32[144,128]{1,0:T(8,128)}, f32[64,128]{1,0:T(8,128)}) custom-call(s32[1]{0:T(128)} %bitcast.2.base_ref, bf16[32,152,128]{2,1,0:T(8,128)(2,1)} %copy-done.1, bf16[144,4608]{1,0:T(8,128)(2,1)} %op_ref.5, bf16[192,4608]{1,0:T(8,128)(2,1)} %fusion.take_ref, f32[64,128]{1,0:T(8,128)} %fusion.7.mine_ref, f32[32,8,128]{2,1,0:T(8,128)} %copy-done.3), custom_call_target="tpu_custom_call" | custom-call | bytes 10800000 | tf_op jit(solution)/shard_map/pallas_call | solution.py:424
  220.3 0.6 copy-done.8
  220.9 3.1 %shard_map.132 = f32[128,1,128]{2,1,0:T(1,128)} custom-call(f32[32,4,128]{2,1,0:T(4,128)} %copy-done.8, s32[32,128]{1,0:T(8,128)} %get-tuple-element.36.inv_ref, f32[64,256]{1,0:T(8,128)} %bitcast.23, f32[64,128]{1,0:T(8,128)} %get-tuple-element.52.corr_ref, f32[64,256]{1,0:T(8,128)} %refs_0_.3, f32[64,256]{1,0:T(8,128)} %get-tuple-element.43.q_ref.refs_1_, ...), custom_call_target="tpu_custom_call" | custom-call | bytes 7200000 | tf_op jit(solution)/shard_map/pallas_call | solution.py:441
  224.1 19.1 %all_to_all.50.gram_ref = f32[128,1,128]{2,1,0:T(1,128)} all-to-all(f32[128,1,128]{2,1,0:T(1,128)} %shard_map.132), channel_id=1, replica_groups=mesh['grp'=4,'tile'=32] {'grp','tile'}, dimensions={0} | all-to-all | bytes 131072 | tf_op jit(solution)/shard_map/all_to_all | solution.py:351
  243.2 2.0 shard_map.133
  245.2 1.5 slice_bitcast_fusion
  (54 shorter events, 2.2 us)
Async XLA Ops:
  0.6 33.6 %copy-start.4 = (f32[64,256]{1,0:T(8,128)S(1)}, f32[64,256]{1,0:T(8,128)}, u32[]{:S(2)}) copy-start(f32[64,256]{1,0:T(8,128)} %refs_0_.3) | copy-start | bytes 196612
  6.6 17.2 %all-to-all-start = ((f32[32,8,128]{2,1,0:T(8,128)}), f32[32,8,128]{2,1,0:T(8,128)S(1)}, u32[]{:S(2)}, u32[]{:S(2)}) async-start(f32[32,8,128]{2,1,0:T(8,128)} %get-tuple-element.29), calls=%async_computation | async-start | bytes 262144 | tf_op jit(solution)/shard_map/all_to_all | solution.py:351
  23.8 10.5 %copy-start.3 = (f32[32,8,128]{2,1,0:T(8,128)}, f32[32,8,128]{2,1,0:T(8,128)S(1)}, u32[]{:S(2)}) copy-start(f32[32,8,128]{2,1,0:T(8,128)S(1)} %all-to-all-done.recv_ref) | copy-start | bytes 393220
  25.8 41.2 %all-to-all-start.2 = ((bf16[32,152,128]{2,1,0:T(8,128)(2,1)}), bf16[32,152,128]{2,1,0:T(8,128)(2,1)S(1)}, u32[]{:S(2)}, u32[]{:S(2)}) async-start(bf16[32,152,128]{2,1,0:T(8,128)(2,1)} %broadcast_in_dim.6), calls=%async_computation.2 | async-start | bytes 2490368 | tf_op jit(solution)/shard_map/all_to_all | solution.py:351
  38.1 25.2 %collective-permute-start = (f32[8,128]{1,0:T(8,128)}, f32[8,128]{1,0:T(8,128)S(1)}, u32[]{:S(2)}, u32[]{:S(2)}) collective-permute-start(f32[8,128]{1,0:T(8,128)} %get-tuple-element.33), channel_id=1, source_target_pairs={{0,1},{1,2},{2,3},{3,4},{4,5},{5,6},{6,7},{7,8},{8,9},{9,10},{10,1... | collective-permute-start | bytes 12296 | tf_op jit(solution)/shard_map/ppermute | solution.py:409
  41.6 7.6 %copy-start.18 = (s32[32,2]{0,1:T(2,128)S(1)}, s32[32,2]{0,1:T(2,128)}, u32[]{:S(2)}) copy-start(s32[32,2]{0,1:T(2,128)} %param.17) | copy-start | bytes 772
  41.6 33.1 %copy-start.19 = (s32[64]{0:T(128)S(1)}, s32[64]{0:T(128)}, u32[]{:S(2)}) copy-start(s32[64]{0:T(128)} %param.18) | copy-start | bytes 772
  41.6 21.6 %collective-permute-start.1 = (f32[8,128]{1,0:T(8,128)}, f32[8,128]{1,0:T(8,128)S(1)}, u32[]{:S(2)}, u32[]{:S(2)}) collective-permute-start(f32[8,128]{1,0:T(8,128)} %get-tuple-element.34), channel_id=1, source_target_pairs={{1,0},{2,1},{3,2},{4,3},{5,4},{6,5},{7,6},{8,7},{9,8},{10,9},{11,1... | collective-permute-start | bytes 12296 | tf_op jit(solution)/shard_map/ppermute | solution.py:410
  63.2 0.6 copy-start.12
  63.2 0.6 copy-start.13
  67.1 8.9 %copy-start = (bf16[32,152,128]{2,1,0:T(8,128)(2,1)}, bf16[32,152,128]{2,1,0:T(8,128)(2,1)S(1)}, u32[]{:S(2)}) copy-start(bf16[32,152,128]{2,1,0:T(8,128)(2,1)S(1)} %all-to-all-done.2.got_ref) | copy-start | bytes 3735556
  67.1 14.9 %all-to-all-start.1 = ((f32[32,4,128]{2,1,0:T(4,128)}), f32[32,4,128]{2,1,0:T(4,128)S(1)}, u32[]{:S(2)}, u32[]{:S(2)}) async-start(f32[32,4,128]{2,1,0:T(4,128)} %shard_map.117), calls=%async_computation.1 | async-start | bytes 131072 | tf_op jit(solution)/shard_map/all_to_all | solution.py:351
  82.0 0.6 copy-start.7
  86.7 27.6 %copy-start.5 = (f32[64,256]{1,0:T(8,128)S(1)}, f32[64,256]{1,0:T(8,128)}, u32[]{:S(2)}) copy-start(f32[64,256]{1,0:T(8,128)} %get-tuple-element.43.q_ref.refs_1_) | copy-start | bytes 196612
  86.7 13.4 %all-to-all-start.3 = ((f32[32,4,128]{2,1,0:T(4,128)}), f32[32,4,128]{2,1,0:T(4,128)S(1)}, u32[]{:S(2)}, u32[]{:S(2)}) async-start(f32[32,4,128]{2,1,0:T(4,128)} %get-tuple-element.39), calls=%async_computation.3 | async-start | bytes 131072 | tf_op jit(solution)/shard_map/all_to_all | solution.py:351
  100.0 6.2 %copy-start.11 = (f32[32,4,128]{2,1,0:T(4,128)}, f32[32,4,128]{2,1,0:T(4,128)S(1)}, u32[]{:S(2)}) copy-start(f32[32,4,128]{2,1,0:T(4,128)S(1)} %all-to-all-done.3.recv_ref) | copy-start | bytes 196612
  102.0 30.0 %all-to-all-start.5 = ((bf16[32,152,128]{2,1,0:T(8,128)(2,1)}), bf16[32,152,128]{2,1,0:T(8,128)(2,1)S(1)}, u32[]{:S(2)}, u32[]{:S(2)}) async-start(bf16[32,152,128]{2,1,0:T(8,128)(2,1)} %broadcast_in_dim.7), calls=%async_computation.5 | async-start | bytes 2490368 | tf_op jit(solution)/shard_map/all_to_all | solution.py:351
  108.8 18.8 %collective-permute-start.2 = (f32[8,128]{1,0:T(8,128)}, f32[8,128]{1,0:T(8,128)S(1)}, u32[]{:S(2)}, u32[]{:S(2)}) collective-permute-start(f32[8,128]{1,0:T(8,128)} %get-tuple-element.41), channel_id=1, source_target_pairs={{0,1},{1,2},{2,3},{3,4},{4,5},{5,6},{6,7},{7,8},{8,9},{9,10},{10,1... | collective-permute-start | bytes 12296 | tf_op jit(solution)/shard_map/ppermute | solution.py:409
  112.4 15.3 %collective-permute-start.3 = (f32[8,128]{1,0:T(8,128)}, f32[8,128]{1,0:T(8,128)S(1)}, u32[]{:S(2)}, u32[]{:S(2)}) collective-permute-start(f32[8,128]{1,0:T(8,128)} %get-tuple-element.42), channel_id=1, source_target_pairs={{1,0},{2,1},{3,2},{4,3},{5,4},{6,5},{7,6},{8,7},{9,8},{10,9},{11,1... | collective-permute-start | bytes 12296 | tf_op jit(solution)/shard_map/ppermute | solution.py:410
  127.6 0.6 copy-start.16
  128.2 0.6 copy-start.17
  132.1 13.2 %copy-start.2 = (bf16[32,152,128]{2,1,0:T(8,128)(2,1)}, bf16[32,152,128]{2,1,0:T(8,128)(2,1)S(1)}, u32[]{:S(2)}) copy-start(bf16[32,152,128]{2,1,0:T(8,128)(2,1)S(1)} %all-to-all-done.5.got_ref) | copy-start | bytes 3735556
  132.1 18.4 %all-to-all-start.4 = ((f32[32,4,128]{2,1,0:T(4,128)}), f32[32,4,128]{2,1,0:T(4,128)S(1)}, u32[]{:S(2)}, u32[]{:S(2)}) async-start(f32[32,4,128]{2,1,0:T(4,128)} %shard_map.123), calls=%async_computation.4 | async-start | bytes 131072 | tf_op jit(solution)/shard_map/all_to_all | solution.py:351
  150.5 0.6 copy-start.9
  155.2 28.9 %copy-start.6 = (f32[64,256]{1,0:T(8,128)S(1)}, f32[64,256]{1,0:T(8,128)}, u32[]{:S(2)}) copy-start(f32[64,256]{1,0:T(8,128)} %get-tuple-element.50.q_ref.refs_2_) | copy-start | bytes 196612
  155.2 14.8 %all-to-all-start.6 = ((f32[32,4,128]{2,1,0:T(4,128)}), f32[32,4,128]{2,1,0:T(4,128)S(1)}, u32[]{:S(2)}, u32[]{:S(2)}) async-start(f32[32,4,128]{2,1,0:T(4,128)} %get-tuple-element.46), calls=%async_computation.6 | async-start | bytes 131072 | tf_op jit(solution)/shard_map/all_to_all | solution.py:351
  170.0 6.0 %copy-start.10 = (f32[32,4,128]{2,1,0:T(4,128)}, f32[32,4,128]{2,1,0:T(4,128)S(1)}, u32[]{:S(2)}) copy-start(f32[32,4,128]{2,1,0:T(4,128)S(1)} %all-to-all-done.6.recv_ref) | copy-start | bytes 196612
  172.0 29.9 %all-to-all-start.8 = ((bf16[32,152,128]{2,1,0:T(8,128)(2,1)}), bf16[32,152,128]{2,1,0:T(8,128)(2,1)S(1)}, u32[]{:S(2)}, u32[]{:S(2)}) async-start(bf16[32,152,128]{2,1,0:T(8,128)(2,1)} %broadcast_in_dim.8), calls=%async_computation.8 | async-start | bytes 2490368 | tf_op jit(solution)/shard_map/all_to_all | solution.py:351
  178.6 18.8 %collective-permute-start.4 = (f32[8,128]{1,0:T(8,128)}, f32[8,128]{1,0:T(8,128)S(1)}, u32[]{:S(2)}, u32[]{:S(2)}) collective-permute-start(f32[8,128]{1,0:T(8,128)} %get-tuple-element.48), channel_id=1, source_target_pairs={{0,1},{1,2},{2,3},{3,4},{4,5},{5,6},{6,7},{7,8},{8,9},{9,10},{10,1... | collective-permute-start | bytes 12296 | tf_op jit(solution)/shard_map/ppermute | solution.py:409
  182.2 15.3 %collective-permute-start.5 = (f32[8,128]{1,0:T(8,128)}, f32[8,128]{1,0:T(8,128)S(1)}, u32[]{:S(2)}, u32[]{:S(2)}) collective-permute-start(f32[8,128]{1,0:T(8,128)} %get-tuple-element.49), channel_id=1, source_target_pairs={{1,0},{2,1},{3,2},{4,3},{5,4},{6,5},{7,6},{8,7},{9,8},{10,9},{11,1... | collective-permute-start | bytes 12296 | tf_op jit(solution)/shard_map/ppermute | solution.py:410
  197.4 0.6 copy-start.14
  198.0 0.6 copy-start.15
  201.9 13.3 %copy-start.1 = (bf16[32,152,128]{2,1,0:T(8,128)(2,1)}, bf16[32,152,128]{2,1,0:T(8,128)(2,1)S(1)}, u32[]{:S(2)}) copy-start(bf16[32,152,128]{2,1,0:T(8,128)(2,1)S(1)} %all-to-all-done.8.got_ref) | copy-start | bytes 3735556
  201.9 18.4 %all-to-all-start.7 = ((f32[32,4,128]{2,1,0:T(4,128)}), f32[32,4,128]{2,1,0:T(4,128)S(1)}, u32[]{:S(2)}, u32[]{:S(2)}) async-start(f32[32,4,128]{2,1,0:T(4,128)} %shard_map.129), calls=%async_computation.7 | async-start | bytes 131072 | tf_op jit(solution)/shard_map/all_to_all | solution.py:351
  220.3 0.6 copy-start.8

commit v2 on v1

v2 whole, which is shorter than its diff:
```python
import functools
import math

import jax
import jax.numpy as jnp
from jax import lax
from jax.experimental import pallas as pl
from jax.experimental.pallas import tpu as pltpu
from jax.sharding import PartitionSpec as P

FNODES = 64
BNODES = 1536
ITERS = 3
FIB = 64
NUC = 100
ORDER = 256
COLS = 144
ROWS = 32
LANES = 128
NODES = ROWS * LANES
PITCH = 40
UNROLL = 4
TILES = 32
ALL = 128

kappa_coef = 0.5
eps_square = 0.0025
stokes_coef = 1.0 / (16.0 * math.pi)

F32 = jnp.float32
BF16 = jnp.bfloat16
TILE = ("chip", "core")
AXES = ("grp",) + TILE


def shape(dims, dtype=F32):
    return jax.ShapeDtypeStruct(dims, dtype)


VMEM = pl.BlockSpec(memory_space=pltpu.VMEM)
SMEM = pl.BlockSpec(memory_space=pltpu.SMEM)


def call(body, outs, in_specs, scratch=(), micros=1.0):
    return pl.pallas_call(
        body,
        out_shape=outs,
        in_specs=in_specs,
        out_specs=jax.tree.map(lambda _: VMEM, outs),
        scratch_shapes=list(scratch),
        cost_estimate=pl.CostEstimate(
            flops=0, transcendentals=0, bytes_accessed=int(micros * 3.6e6)
        ),
    )


def lane_iota(rows):
    return lax.broadcasted_iota(jnp.int32, (rows, LANES), 1)


def sub_iota(rows):
    return lax.broadcasted_iota(jnp.int32, (rows, LANES), 0)


def pick(read, count, row, lane):
    size = row.shape
    outs = [jnp.zeros(size, F32)] * count
    for r in range(ROWS):
        hit = row == r
        for c in range(count):
            source = jnp.broadcast_to(read(c, r), size)
            found = jnp.take_along_axis(source, lane, axis=1, mode="promise_in_bounds")
            outs[c] = jnp.where(hit, found, outs[c])
    return outs


def swap_out(mix, parts, out_ref, width):
    for c in range(width):
        mix[c * ROWS : (c + 1) * ROWS, :] = parts[min(c, len(parts) - 1)]
    for d in range(ROWS):
        out_ref[d] = mix[pl.ds(d, width, stride=ROWS), :]


def send_out(mix, parts, extras, out_ref, width):
    for c, part in enumerate(parts):
        mix[c * PITCH : c * PITCH + 1, :] = jnp.zeros((1, LANES), F32)
        mix[c * PITCH + ROWS + 1 : c * PITCH + ROWS + 2, :] = jnp.zeros((1, LANES), F32)
        mix[c * PITCH + 1 : c * PITCH + ROWS + 1, :] = part
    for b, rows in enumerate(extras):
        for k, row in enumerate(rows):
            c = len(parts) + k
            mix[c * PITCH : c * PITCH + PITCH, :] = jnp.broadcast_to(row, (PITCH, LANES))
        for d in range(ROWS):
            out_ref[d, b] = mix[pl.ds(d + b, width, stride=PITCH), :]


def end_rows(q_ref):
    turned = jnp.concatenate([q_ref[:, :LANES], q_ref[:, LANES:]], axis=0).T
    return turned[:1, :], turned[FNODES : FNODES + 1, :]


def fiber_table(q_ref):
    low = lane_iota(ROWS) < FNODES
    a0, a1 = q_ref[:ROWS, :LANES], q_ref[:ROWS, LANES:]
    b0, b1 = q_ref[ROWS:, :LANES], q_ref[ROWS:, LANES:]
    t0 = jnp.where(low, a0, pltpu.roll(b0, FNODES, 1))
    t1 = jnp.where(low, pltpu.roll(a0, FNODES, 1), b0)
    t2 = jnp.where(low, a1, pltpu.roll(b1, FNODES, 1))
    return t0, t1, t2


def table_place(node):
    row = (node >> 6) & 31
    lane = ((node >> 11) << 6) | (node & 63)
    return row, lane


def prep_kernel(
    pos_ref, q_ref, order_ref, leaf_ref, nuc_ref, node_ref, sent_ref, index_ref, table, mix
):
    for r in range(ROWS):
        index_ref[r : r + 1, :] = order_ref[:, r * LANES : (r + 1) * LANES]
    node = index_ref[...]
    spots = pick(
        lambda c, r: pos_ref[c : c + 1, r * LANES : (r + 1) * LANES], 3, node >> 7, node & 127
    )
    for c, part in enumerate(fiber_table(q_ref)):
        table[c] = part
    row, lane = table_place(node)
    forces = pick(lambda c, r: table[c, r : r + 1, :], 3, row, lane)
    twice = [jnp.concatenate([r[...], r[...]], axis=1).astype(F32) for r in (nuc_ref, node_ref)]
    rims = [leaf_ref[:, :LANES].astype(F32), leaf_ref[:, NODES - LANES :].astype(F32)]
    send_out(mix, spots + forces, [twice, list(end_rows(q_ref)), rims], sent_ref, 8)


def invert_kernel(
    leaf_ref, send_ref, body_ref, index_ref, inv_leaf_ref, inv_send_ref, z_ref, load_ref
):
    blank = jnp.zeros((COLS, LANES - NUC), F32)
    z = jnp.concatenate([body_ref[...], blank], axis=1)
    z_ref[...] = z
    for s in range(TILES // 2):
        load_ref[s] = z.astype(BF16)
    slots = lane_iota(64)
    upper = sub_iota(64) >= 32
    spot = sub_iota(64) & 31

    def one(place, row_of, lane_of):
        value = slots + place * LANES
        digit = jnp.where(upper, value & 63, value >> 6).astype(F32)
        left = jnp.where(row_of == spot, digit, 0.0).astype(BF16)
        right = jnp.where(lane_of == sub_iota(LANES), 1.0, 0.0).astype(BF16)
        return lax.dot_general(
            left, right, (((1,), (1,)), ((), ())), preferred_element_type=F32
        )

    leaf_sum = jnp.zeros((64, LANES), F32)
    send_sum = jnp.zeros((64, LANES), F32)
    for r in range(ROWS):
        leaf = leaf_ref[:, r * LANES : (r + 1) * LANES]
        index_ref[r : r + 1, :] = leaf
        leaf_sum = leaf_sum + one(r, leaf >> 7, leaf & 127)
        row, lane = table_place(send_ref[:, r * LANES : (r + 1) * LANES])
        send_sum = send_sum + one(r, row, lane)
    for total, ref in ((leaf_sum, inv_leaf_ref), (send_sum, inv_send_ref)):
        ref[...] = (total[:32] * 64.0 + total[32:]).astype(jnp.int32)


def pair_weights(target, spot, force):
    dx, dy, dz = (target[c] - spot[c] for c in range(3))
    root = lax.rsqrt((dx * dx + eps_square) + (dy * dy + dz * dz))
    cube = root * (root * root)
    along = (dx * force[0] + dy * force[1]) + dz * force[2]
    return root + eps_square * cube, along * cube


def halves(value):
    high = value.astype(BF16).astype(F32)
    return high, value - high


def near_kernel(first, tile_ref, mask_ref, recv_ref, index_ref, inv_ref, *refs):
    if first:
        out_ref, pos, rims_ref, force, lines, column, weight, total, mix = refs
        me = tile_ref[0]
        before, after = jnp.maximum(me - 1, 0), jnp.minimum(me + 1, TILES - 1)
        rims_ref[0:8, :] = jnp.broadcast_to(recv_ref[before, 2, 7:8, :], (8, LANES)).astype(
            jnp.int32
        )
        rims_ref[8:16, :] = jnp.broadcast_to(recv_ref[after, 2, 6:7, :], (8, LANES)).astype(
            jnp.int32
        )
        count, base = 6, 3
    else:
        pos, rims_ref, out_ref, force, lines, column, weight, total, mix = refs
        count, base = 3, 0
    slot = index_ref[...]
    parts = pick(lambda c, r: recv_ref[r, 1, c : c + 1, :], count, slot >> 7, slot & 127)
    ends = []
    for side in range(2):
        slot = rims_ref[8 * side : 8 * side + 8, :]
        block = 2 * side
        ends.append(
            pick(lambda c, r: recv_ref[r, block, c : c + 1, :], count, slot >> 7, slot & 127)
        )
    live = (
        jnp.where(tile_ref[0] > 0, stokes_coef, 0.0),
        jnp.where(tile_ref[0] < TILES - 1, stokes_coef, 0.0),
    )
    for c in range(3):
        if first:
            pos[c, 0:1, :] = ends[0][c][:1] - 0.5
            pos[c, 1 : ROWS + 1, :] = parts[c] - 0.5
            pos[c, ROWS + 1 : ROWS + 2, :] = ends[1][c][:1] - 0.5
            pos[c, ROWS + 2 :, :] = jnp.zeros((PITCH - ROWS - 2, LANES), F32)
        force[c, 0:1, :] = ends[0][base + c][:1] * live[0]
        force[c, 1 : ROWS + 1, :] = parts[base + c] * stokes_coef
        force[c, ROWS + 1 : ROWS + 2, :] = ends[1][base + c][:1] * live[1]
        force[c, ROWS + 2 :, :] = jnp.zeros((PITCH - ROWS - 2, LANES), F32)

    def plane(k):
        return slice(k * PITCH, (k + 1) * PITCH)

    lines[0, plane(6), :] = jnp.zeros((PITCH, LANES), F32)
    lines[0, plane(7), :] = jnp.zeros((PITCH, LANES), F32)
    lines[1, plane(6), :] = jnp.ones((PITCH, LANES), F32)
    lines[1, plane(7), :] = jnp.zeros((PITCH, LANES), F32)
    for k, ref in enumerate((force, pos)):
        for c in range(3):
            lines[k, plane(c), :], lines[k, plane(3 + c), :] = halves(ref[c])

    def one_leaf(i, u):
        for c in range(3):
            row = pos[c, pl.ds(i + 1, 1), :]
            column[u, c] = jnp.broadcast_to(row, (LANES, LANES)).T
        sums = [jnp.zeros((8, LANES), F32)] * 2
        for w in range(3):
            spot, push = (
                [jnp.broadcast_to(ref[c, pl.ds(i + w, 1), :], (8, LANES)) for c in range(3)]
                for ref in (pos, force)
            )
            for g in range(LANES // 16):
                found = [
                    pair_weights([column[u, c, h : h + 8, :] for c in range(3)], spot, push)
                    for h in (16 * g, 16 * g + 8)
                ]
                for k in range(2):
                    weight[u, k, w, 16 * g : 16 * g + 16, :] = jnp.concatenate(
                        [found[0][k], found[1][k]], axis=0
                    ).astype(BF16)
            for k in range(2):
                left = lines[k, pl.ds(i + w, 8, stride=PITCH), :].astype(BF16)
                part = lax.dot_general(
                    left, weight[u, k, w], (((1,), (1,)), ((), ())), preferred_element_type=F32
                )
                if w != 1:
                    part = part * mask_ref[i, w // 2].astype(F32)
                sums[k] = sums[k] + part
        for k in range(2):
            total[k, pl.ds(8 * i, 8), :] = sums[k]

    def leaves(i, carry):
        for u in range(UNROLL):
            one_leaf(i * UNROLL + u, u)
        return carry

    lax.fori_loop(0, ROWS // UNROLL, leaves, 0)

    def gathered(k, c):
        return total[k, pl.ds(c, ROWS, stride=8), :]

    weights = gathered(1, 6)
    for c in range(3):
        mix[c * ROWS : (c + 1) * ROWS, :] = (
            (gathered(0, c) + gathered(0, 3 + c))
            + pos[c, 1 : ROWS + 1, :] * weights
            - (gathered(1, c) + gathered(1, 3 + c))
        )
    slot = inv_ref[...]
    parts = pick(
        lambda c, r: mix[c * ROWS + r : c * ROWS + r + 1, :], 3, slot >> 7, slot & 127
    )
    swap_out(mix, parts, out_ref, 4)


def body_kernel(
    first, last, tile_ref, got_ref, mate_ref, op_ref, take_ref, mine_ref, info_ref, recv_ref,
    *refs,
):
    z_ref, corr_ref = refs[:2]
    rows, full_ref = refs[-2:]
    side = tile_ref[0] & 1
    for s in range(TILES // 2):
        full_ref[2 * s + side] = got_ref[s]
        full_ref[2 * s + 1 - side] = mate_ref[s]
    full = full_ref[...].reshape(TILES * COLS, LANES)
    z = jnp.dot(op_ref[...], full, preferred_element_type=F32)
    got = jnp.dot(take_ref[...], full, preferred_element_type=F32)
    mine = mine_ref[...]
    lane = lane_iota(FIB)
    corr = jnp.zeros((FIB, LANES), F32)
    for c in range(3):
        value = jnp.sum(got[c * FIB : (c + 1) * FIB] * mine, axis=1, keepdims=True)
        corr = jnp.where(lane == c, value * -kappa_coef, corr)
    corr_ref[...] = corr
    for s in range(TILES):
        rows[0, s : s + 1, :] = recv_ref[s, 1, 6:7, :] if first else recv_ref[s, 0, 3:4, :]
        rows[1, s : s + 1, :] = recv_ref[s, 1, 7:8, :] if first else recv_ref[s, 1, 3:4, :]
    low = lane_iota(TILES) < FNODES
    ra, rb = rows[0], rows[1]
    wa, wb = pltpu.roll(ra, FNODES, 1), pltpu.roll(rb, FNODES, 1)
    for c, value in enumerate(
        (jnp.where(low, ra, wa), jnp.where(low, rb, wb), jnp.where(low, wa, ra))
    ):
        high = value.astype(BF16).astype(F32)
        rows[c] = jnp.where(low, high, value - high)
    column = (sub_iota(COLS) + tile_ref[0] * COLS).astype(F32)
    nucleus = sub_iota(LANES).astype(F32)
    ends = jnp.zeros((COLS, LANES), F32)
    for s in range(TILES):
        node = info_ref[s, 0, 7:8, :]
        left = jnp.zeros((COLS, LANES), F32)
        for c in range(3):
            left = jnp.where(column == node + float(c * BNODES), rows[c, s : s + 1, :], left)
        right = jnp.where(nucleus == info_ref[s, 0, 6:7, :], 1.0, 0.0).astype(BF16)
        ends = ends + lax.dot_general(
            left.astype(BF16), right, (((1,), (1,)), ((), ())), preferred_element_type=F32
        )
    z = z - kappa_coef * ends
    z_ref[...] = z
    if not last:
        for s in range(TILES // 2):
            refs[2][s] = z.astype(BF16)


def assemble(back_ref, inv_ref, prod_ref, corr_ref, q_ref):
    slot = inv_ref[...]
    h0, h1, h2 = pick(lambda c, r: back_ref[r, c : c + 1, :], 3, slot >> 7, slot & 127)
    lane = lane_iota(ROWS)
    low = lane < FNODES
    blank = jnp.zeros((ROWS, LANES), F32)
    first = (
        jnp.where(low, h0, pltpu.roll(h1, FNODES, 1)),
        jnp.where(low, pltpu.roll(h0, FNODES, 1), h1),
    )
    second = (jnp.where(low, h2, blank), jnp.where(low, pltpu.roll(h2, FNODES, 1), blank))
    for half in range(2):
        rows = slice(half * ROWS, (half + 1) * ROWS)
        c0, c1, c2 = (corr_ref[rows, c : c + 1] for c in range(3))
        at0 = jnp.where(lane == 0, c0, jnp.where(lane == FNODES, c1, blank))
        at1 = jnp.where(lane == 0, c2, blank)
        q_ref[rows, :LANES] = prod_ref[rows, :LANES] + first[half] + at0
        q_ref[rows, LANES:] = prod_ref[rows, LANES:] + second[half] + at1


def join_kernel(
    back_ref, inv_ref, prod_ref, corr_ref, index_ref, q_ref, low_ref, sent_ref, table, mix
):
    assemble(back_ref, inv_ref, prod_ref, corr_ref, q_ref)
    low_ref[...] = q_ref[...].astype(BF16)
    for c, part in enumerate(fiber_table(q_ref)):
        table[c] = part
    row, lane = table_place(index_ref[...])
    forces = pick(lambda c, r: table[c, r : r + 1, :], 3, row, lane)
    even, odd = end_rows(q_ref)
    send_out(mix, forces, [[even], [odd], [odd]], sent_ref, 4)


def dots_kernel(back_ref, inv_ref, prod_ref, corr_ref, *refs):
    q, z, (out_ref, last) = refs[:3], refs[3:7], refs[7:]
    assemble(back_ref, inv_ref, prod_ref, corr_ref, last)
    q = list(q) + [last]
    lane = lane_iota(1)
    line = jnp.zeros((1, LANES), F32)
    k = 0
    for i in range(4):
        for j in range(i + 1):
            total = jnp.sum(q[i][...] * q[j][...]) + jnp.sum(z[i][...] * z[j][...])
            line = jnp.where(lane == k, total, line)
            k += 1
    for d in range(ALL):
        out_ref[d] = line


def solve_kernel(gram_ref, *refs):
    q, z, (fiber_ref, body_ref) = refs[:3], refs[3:6], refs[6:]
    line = jnp.sum(gram_ref[...], axis=0)
    lane = lane_iota(1)
    g = {}
    k = 0
    for i in range(4):
        for j in range(i + 1):
            g[i, j] = g[j, i] = jnp.sum(jnp.where(lane == k, line, 0.0), axis=1, keepdims=True)
            k += 1
    n = {}
    for i in range(3):
        for j in range(i + 1):
            n[i, j] = g[i, j] + g[i + 1, j] + g[i, j + 1] + g[i + 1, j + 1]
    t = [g[0, i] + g[0, i + 1] for i in range(3)]
    l00 = jnp.sqrt(n[0, 0])
    l10, l20 = n[1, 0] / l00, n[2, 0] / l00
    l11 = jnp.sqrt(n[1, 1] - l10 * l10)
    l21 = (n[2, 1] - l20 * l10) / l11
    l22 = jnp.sqrt(n[2, 2] - l20 * l20 - l21 * l21)
    f0 = t[0] / l00
    f1 = (t[1] - l10 * f0) / l11
    f2 = (t[2] - l20 * f0 - l21 * f1) / l22
    c2 = f2 / l22
    c1 = (f1 - l21 * c2) / l11
    c0 = (f0 - l10 * c1 - l20 * c2) / l00
    fiber_ref[...] = c0 * q[0][...] + c1 * q[1][...] + c2 * q[2][...]
    body = c0 * z[0][...] + c1 * z[1][...] + c2 * z[2][...]
    body_ref[...] = body[:, :NUC]


def exchange(array, axis=TILE):
    return lax.all_to_all(array, axis, split_axis=0, concat_axis=0, tiled=True)


def local(
    rhs_fiber,
    rhs_body,
    fiber_ops,
    body_op,
    positions,
    send_order,
    leaf_order,
    neighbours,
    attach_nucleus,
    attach_node,
):
    tile = lax.axis_index(TILE).astype(jnp.int32).reshape(1)
    load = shape((TILES // 2, COLS, LANES), BF16)
    wanted = (jnp.arange(3, dtype=jnp.int32)[:, None] * BNODES + attach_node[None, :]).reshape(-1)
    take = (wanted[:, None] == jnp.arange(3 * BNODES, dtype=jnp.int32)[None, :]).astype(BF16)
    mine = (attach_nucleus[:, None] == jnp.arange(LANES, dtype=jnp.int32)[None, :]).astype(F32)

    square = shape((ROWS, LANES), jnp.int32)
    spots = shape((3, PITCH, LANES))
    rims = shape((16, LANES), jnp.int32)
    table = pltpu.VMEM((3, ROWS, LANES), F32)
    padded = pltpu.VMEM((3, PITCH, LANES), F32)
    mix4 = pltpu.VMEM((4 * ROWS, LANES), F32)
    blocks8 = pltpu.VMEM((8 * PITCH, LANES), F32)
    blocks4 = pltpu.VMEM((4 * PITCH, LANES), F32)

    sent, send_index = call(
        prep_kernel, (shape((ROWS, 3, 8, LANES)), square), [VMEM] * 6, [table, blocks8], 2.0
    )(
        positions,
        rhs_fiber,
        send_order,
        leaf_order,
        attach_nucleus.reshape(1, FIB),
        attach_node.reshape(1, FIB),
    )
    leaf_index, inv_leaf, inv_send, body0, payload = call(
        invert_kernel,
        (square, square, square, shape((COLS, LANES)), load),
        [VMEM] * 3,
        (),
        2.0,
    )(leaf_order, send_order, rhs_body.T)

    q, z, low = [rhs_fiber], [body0], rhs_fiber.astype(BF16)
    for j in range(ITERS):
        first, last = j == 0, j + 1 == ITERS
        recv = exchange(sent)
        product = jnp.einsum(
            "fij,fj->fi", fiber_ops, low, preferred_element_type=F32
        )
        if first:
            recv, product, payload, take, mine = lax.optimization_barrier(
                (recv, product, payload, take, mine)
            )
        else:
            recv, product, payload = lax.optimization_barrier((recv, product, payload))
        got = exchange(payload, "chip")
        near = functools.partial(near_kernel, first)
        specs = [SMEM, SMEM] + [VMEM] * 3
        scratch = [
            padded,
            pltpu.VMEM((2, 8 * PITCH, LANES), F32),
            pltpu.VMEM((UNROLL, 3, LANES, LANES), F32),
            pltpu.VMEM((UNROLL, 2, 3, LANES, LANES), BF16),
            pltpu.VMEM((2, 8 * ROWS, LANES), F32),
            mix4,
        ]
        if first:
            info = recv
            out, pos, rim = call(
                near, (shape((ROWS, 4, LANES)), spots, rims), specs, scratch, 14.0
            )(tile, neighbours, recv, leaf_index, inv_leaf)
        else:
            out = call(near, shape((ROWS, 4, LANES)), specs + [VMEM] * 2, scratch, 14.0)(
                tile, neighbours, recv, leaf_index, inv_leaf, pos, rim
            )
        got, out = lax.optimization_barrier((got, out))
        mate = lax.ppermute(got, "core", [(0, 1), (1, 0)])
        back = exchange(out)
        made = [shape((COLS, LANES)), shape((FIB, LANES))]
        if not last:
            made.append(load)
        image, corr, *rest = call(
            functools.partial(body_kernel, first, last),
            tuple(made),
            [SMEM] + [VMEM] * 7,
            [pltpu.VMEM((3, TILES, LANES), F32), pltpu.VMEM((TILES, COLS, LANES), BF16)],
            4.0,
        )(tile, got, mate, body_op, take, mine, info, recv)
        z.append(image)
        if not last:
            payload = rest[0]
            vector, low, sent = call(
                join_kernel,
                (shape((FIB, ORDER)), shape((FIB, ORDER), BF16), shape((ROWS, 3, 4, LANES))),
                [VMEM] * 5,
                [table, blocks4],
                2.0,
            )(back, inv_send, product, corr, send_index)
            q.append(vector)
    line = call(
        dots_kernel,
        shape((ALL, 1, LANES)),
        [VMEM] * 11,
        [pltpu.VMEM((FIB, ORDER), F32)],
        2.0,
    )(back, inv_send, product, corr, *q, *z)
    gram = exchange(line, AXES)
    sol_fiber, sol_body = call(
        solve_kernel, (shape((FIB, ORDER)), shape((COLS, NUC))), [VMEM] * 7
    )(gram, *q, *z[:3])
    return sol_fiber, sol_body.T


def solution(mesh):
    groups, tiles = mesh.devices.shape
    split = jax.sharding.Mesh(mesh.devices.reshape(groups, tiles // 2, 2), AXES)
    placed = (
        P(AXES, None),
        P("grp", TILE),
        P(AXES, None, None),
        P(TILE, None),
        P(None, AXES),
        P(AXES, None),
        P(AXES, None),
        P(AXES, None),
        P(AXES),
        P(AXES),
    )
    return jax.shard_map(
        local,
        mesh=split,
        in_specs=placed,
        out_specs=(P(AXES, None), P("grp", TILE)),
        check_vma=False,
    )
```

time: 249 us -> 189 us (0.76)
  Pallas kernels: 97.1 us -> 71.3 us
  starting transfers between devices: 74.5 us -> 62 us
  local copies, waits for them, and re-layouts: 17.5 us -> 7.06 us
  waiting for transfers between devices: 16.5 us -> 8.19 us
    pallas_call x20 -> x11, Pallas kernels: 93.9 us -> 68.2 us  [the longest x2 22.8 us: local(): call(near, shape((ROWS, 4, LANES)), specs + [VMEM] * 2, scratch, 14.0)]
    ppermute x6 -> x3, starting transfers between devices: 16.4 us -> 4.3 us  [local(): mate = lax.ppermute(got, 'core', [(0, 1), (1, 0)])]
    all_to_all x9, waiting for transfers between devices: 16.5 us -> 8.19 us  [exchange(): return lax.all_to_all(array, axis, split_axis=0, concat_axis=0, tiled=True)]
    broadcast_in_dim x3 -> x0, local copies, waits for them, and re-layouts: 6.02 us -> none  [local(): got = exchange(jnp.broadcast_to(payload[None], (TILES, PAYLOAD, LANES)))]
    unnamed x41 -> x29, local copies, waits for them, and re-layouts: 4.95 us -> 5.03 us
  transfers between devices with their start and end apart: 15 -> 12, of which waited for: 4 -> 5; matrix products, arithmetic and copies ran while one was open for 10% -> 13% of each run, Pallas kernels for 32% -> 29%
where the time goes in v2:
time: 189 us; the launch traced here: 188 us
  Pallas kernels  71.3 us (38%)
  starting transfers between devices  62 us (33%)
  blocking collectives  17.4 us (9%)
  matrix products  16.9 us (9%)
  waiting for transfers between devices  8.19 us (4%)
  local copies, waits for them, and re-layouts  7.06 us (4%)
  other arithmetic  3.85 us (2%)
    all_to_all x9, starting transfers between devices, exchange(): return lax.all_to_all(array, axis, split_axis=0, concat_axis=0, tiled=True)  57.7 us
    pallas_call x2, Pallas kernels, local(): call(near, shape((ROWS, 4, LANES)), specs + [VMEM] * 2, scratch, 14.0)  22.8 us
    all_to_all x1, blocking collectives, exchange(): return lax.all_to_all(array, axis, split_axis=0, concat_axis=0, tiled=True)  17.4 us
    dot_general x3, matrix products, local(): jnp.einsum('fij,fj->fi', fiber_ops, low, preferred_element_type=F32)  16.9 us
    pallas_call x3, Pallas kernels, local(): call(functools.partial(body_kernel, first, last), tuple(made), [SMEM] + [...  15.2 us
    pallas_call x1, Pallas kernels, local(): call(near, (shape((ROWS, 4, LANES)), spots, rims), specs, scratch, 14.0)  12.7 us
    pallas_call x2, Pallas kernels, local(): call(join_kernel, (shape((FIB, ORDER)), shape((FIB, ORDER), BF16), shape(...  8.28 us
    all_to_all x9, waiting for transfers between devices, exchange(): return lax.all_to_all(array, axis, split_axis=0, concat_axis=0, tiled=True)  8.19 us
  transfers between devices with their start and end apart: 12, of which 5 were waited for; matrix products, arithmetic and copies ran while one was open for 13% of the time, Pallas kernels for 29%

profile of v2, /device:TPU:1, one launch (start us, length us, event | category | flops | bytes accessed | tf_op | source)
XLA Modules:
  0.0 187.6 jit_solution(5612585706981409690)
XLA Ops:
  0.6 0.0 copy-start.12
  0.6 0.0 copy-start.13
  0.7 4.0 %shard_map.113 = (f32[32,3,8,128]{3,2,1,0:T(8,128)}, s32[32,128]{1,0:T(8,128)}) custom-call(f32[3,4096]{1,0:T(4,128)} %pos_ref.1, f32[64,256]{1,0:T(8,128)} %refs_0_.3, s32[1,4096]{1,0:T(1,128)} %send_ref.1, s32[1,4096]{1,0:T(1,128)} %leaf_ref.3, s32[1,64]{1,0:T(1,128)} %bitcast.27, s32[1,64]{1,0:T(1,128)} %bitcast.28), custom_call_target="tpu_custom_call" | custom-call | bytes 7200000 | tf_op jit(solution)/shard_map/pallas_call | solution.py:447
  4.7 9.6 %all-to-all-start = ((f32[32,3,8,128]{3,2,1,0:T(8,128)}), f32[32,3,8,128]{3,2,1,0:T(8,128)S(1)}, u32[]{:S(2)}, u32[]{:S(2)}) async-start(f32[32,3,8,128]{3,2,1,0:T(8,128)} %get-tuple-element.45), calls=%async_computation | async-start | bytes 786432 | tf_op jit(solution)/shard_map/all_to_all | solution.py:417
  14.3 0.8 convert_bitcast_fusion
  15.1 0.7 broadcast_add_fusion
  15.9 0.1 add.26
  16.0 1.6 fusion.take_ref
  17.5 5.6 %fusion.5 = f32[64,1,256]{2,1,0:T(1,128)S(1)} fusion(bf16[64,256,256]{2,1,0:T(8,128)(2,1)} %param.12, bf16[64,256,1]{1,0,2:T(8,128)(2,1)S(1)} %convert_bitcast_fusion), kind=kOutput, calls=%fused_computation.9 | convolution fusion | flops 8388608 | bytes 8486912 | tf_op jit(solution)/shard_map/fij,fj->fi/dot_general | solution.py:469
  23.2 0.7 copy.32
  23.8 3.2 %shard_map.114 = (s32[32,128]{1,0:T(8,128)}, s32[32,128]{1,0:T(8,128)}, s32[32,128]{1,0:T(8,128)}, f32[144,128]{1,0:T(8,128)}, bf16[16,144,128]{2,1,0:T(8,128)(2,1)}) custom-call(s32[1,4096]{1,0:T(1,128)} %leaf_ref.3, s32[1,4096]{1,0:T(1,128)} %send_ref.1, f32[144,100]{1,0:T(8,128)} %bitcast.26), custom_call_target="tpu_custom_call" | custom-call | bytes 7200000 | tf_op jit(solution)/shard_map/pallas_call | solution.py:457
  27.0 0.0 copy-done.12
  27.0 0.7 fusion.7.mine_ref
  27.7 0.0 all-to-all-done.recv_ref.info_ref
  27.7 6.7 %all-to-all-start.1 = ((bf16[16,144,128]{2,1,0:T(8,128)(2,1)}), bf16[16,144,128]{2,1,0:T(8,128)(2,1)S(1)}, u32[]{:S(2)}, u32[]{:S(2)}) async-start(bf16[16,144,128]{2,1,0:T(8,128)(2,1)} %get-tuple-element.47), calls=%async_computation.1 | async-start | bytes 1179648 | tf_op jit(solution)/shard_map/all_to_all | solution.py:417
  34.4 0.0 copy-done.13
  34.4 0.7 copy.12.mask_ref
  35.1 0.0 copy-done
  35.1 12.7 %shard_map.115 = (f32[32,4,128]{2,1,0:T(4,128)}, f32[3,40,128]{2,1,0:T(8,128)}, s32[16,128]{1,0:T(8,128)}) custom-call(s32[1]{0:T(128)} %bitcast.5.tile_ref, s32[32,2]{1,0:T(8,128)} %copy.12.mask_ref, f32[32,3,8,128]{3,2,1,0:T(8,128)} %copy-done, s32[32,128]{1,0:T(8,128)} %get-tuple-element.49.index_ref, s32[32,128]{1,0:T(8,128)} %get-tuple-element.50.inv_ref), custom_call_target="tpu_custom_call" | custom-call | bytes 50400000 | tf_op jit(solution)/shard_map/pallas_call | solution.py:491
  47.8 0.0 all-to-all-done.1.got_ref
  47.8 0.7 collective-permute-start
  48.5 7.4 %all-to-all-start.2 = ((f32[32,4,128]{2,1,0:T(4,128)}), f32[32,4,128]{2,1,0:T(4,128)S(1)}, u32[]{:S(2)}, u32[]{:S(2)}) async-start(f32[32,4,128]{2,1,0:T(4,128)} %get-tuple-element.52), calls=%async_computation.2 | async-start | bytes 131072 | tf_op jit(solution)/shard_map/all_to_all | solution.py:417
  55.9 0.0 collective-permute-done.mate_ref
  55.9 0.0 copy-done.3
  55.9 0.8 copy-done.8
  56.7 5.2 %shard_map.116 = (f32[144,128]{1,0:T(8,128)}, f32[64,128]{1,0:T(8,128)}, bf16[16,144,128]{2,1,0:T(8,128)(2,1)}) custom-call(s32[1]{0:T(128)} %bitcast.5.tile_ref, bf16[16,144,128]{2,1,0:T(8,128)(2,1)} %copy-done.3, bf16[16,144,128]{2,1,0:T(8,128)(2,1)} %copy-done.8, bf16[144,4608]{1,0:T(8,128)(2,1)} %op_ref.5, bf16[192,4608]{1,0:T(8,128)(2,1)} %fusion.take_ref, ...), custom_call_target="tpu_custom_call" | custom-call | bytes 14400000 | tf_op jit(solution)/shard_map/pallas_call | solution.py:504
  61.9 1.3 all-to-all-done.2.back_ref
  63.2 0.6 copy-done.11
  63.9 4.1 %shard_map.117 = (f32[64,256]{1,0:T(8,128)}, bf16[64,256]{1,0:T(8,128)(2,1)}, f32[32,3,4,128]{3,2,1,0:T(4,128)}) custom-call(f32[32,4,128]{2,1,0:T(4,128)} %copy-done.11, s32[32,128]{1,0:T(8,128)} %get-tuple-element.53.inv_ref, f32[64,256]{1,0:T(8,128)} %bitcast.21, f32[64,128]{1,0:T(8,128)} %get-tuple-element.58.corr_ref, s32[32,128]{1,0:T(8,128)} %get-tuple-element.59.index_ref), custom_call_target="tpu_custom_call" | custom-call | bytes 7200000 | tf_op jit(solution)/shard_map/pallas_call | solution.py:514
  68.0 6.1 %all-to-all-start.3 = ((f32[32,3,4,128]{3,2,1,0:T(4,128)}), f32[32,3,4,128]{3,2,1,0:T(4,128)S(1)}, u32[]{:S(2)}, u32[]{:S(2)}) async-start(f32[32,3,4,128]{3,2,1,0:T(4,128)} %get-tuple-element.60), calls=%async_computation.3 | async-start | bytes 393216 | tf_op jit(solution)/shard_map/all_to_all | solution.py:417
  74.1 5.7 %fusion.3 = f32[64,1,256]{2,1,0:T(1,128)S(1)} fusion(bf16[64,256,256]{2,1,0:T(8,128)(2,1)} %param.12, bf16[64,256,1]{1,0,2:T(8,128)(2,1)} %bitcast.25), kind=kOutput, calls=%fused_computation.6 | convolution fusion | flops 8388608 | bytes 8486912 | tf_op jit(solution)/shard_map/fij,fj->fi/dot_general | solution.py:469
  79.7 0.7 copy.31
  80.4 1.9 %all-to-all-done.3.recv_ref = f32[32,3,4,128]{3,2,1,0:T(4,128)S(1)} async-done(((f32[32,3,4,128]{3,2,1,0:T(4,128)}), f32[32,3,4,128]{3,2,1,0:T(4,128)S(1)}, u32[]{:S(2)}, u32[]{:S(2)}) %all-to-all-start.3) | async-done | bytes 196640 | tf_op jit(solution)/shard_map/all_to_all | solution.py:417
  82.3 4.7 %all-to-all-start.4 = ((bf16[16,144,128]{2,1,0:T(8,128)(2,1)}), bf16[16,144,128]{2,1,0:T(8,128)(2,1)S(1)}, u32[]{:S(2)}, u32[]{:S(2)}) async-start(bf16[16,144,128]{2,1,0:T(8,128)(2,1)} %get-tuple-element.63), calls=%async_computation.4 | async-start | bytes 1179648 | tf_op jit(solution)/shard_map/all_to_all | solution.py:417
  87.1 11.4 %shard_map.118 = f32[32,4,128]{2,1,0:T(4,128)} custom-call(s32[1]{0:T(128)} %bitcast.5.tile_ref, s32[32,2]{1,0:T(8,128)} %copy.12.mask_ref, f32[32,3,4,128]{3,2,1,0:T(4,128)} %copy-done.5, s32[32,128]{1,0:T(8,128)} %get-tuple-element.49.index_ref, s32[32,128]{1,0:T(8,128)} %get-tuple-element.50.inv_ref, f32[3,40,128]{2,1,0:T(8,128)} %get-tuple-element.65.refs_0_, ...), custom_call_target="tpu_custom_call" | custom-call | bytes 50400000 | tf_op jit(solution)/shard_map/pallas_call | solution.py:495
  98.5 0.0 all-to-all-done.4.got_ref
  98.5 1.8 collective-permute-start.1
  100.3 6.3 %all-to-all-start.5 = ((f32[32,4,128]{2,1,0:T(4,128)}), f32[32,4,128]{2,1,0:T(4,128)S(1)}, u32[]{:S(2)}, u32[]{:S(2)}) async-start(f32[32,4,128]{2,1,0:T(4,128)} %shard_map.118), calls=%async_computation.5 | async-start | bytes 131072 | tf_op jit(solution)/shard_map/all_to_all | solution.py:417
  106.5 0.0 collective-permute-done.1.mate_ref
  106.6 0.8 copy-done.7
  107.4 5.1 %shard_map.119 = (f32[144,128]{1,0:T(8,128)}, f32[64,128]{1,0:T(8,128)}, bf16[16,144,128]{2,1,0:T(8,128)(2,1)}) custom-call(s32[1]{0:T(128)} %bitcast.5.tile_ref, bf16[16,144,128]{2,1,0:T(8,128)(2,1)} %copy-done.2, bf16[16,144,128]{2,1,0:T(8,128)(2,1)} %copy-done.7, bf16[144,4608]{1,0:T(8,128)(2,1)} %op_ref.5, bf16[192,4608]{1,0:T(8,128)(2,1)} %fusion.take_ref, ...), custom_call_target="tpu_custom_call" | custom-call | bytes 14400000 | tf_op jit(solution)/shard_map/pallas_call | solution.py:504
  112.5 1.4 all-to-all-done.5.back_ref
  113.8 0.6 copy-done.10
  114.5 4.1 %shard_map.120 = (f32[64,256]{1,0:T(8,128)}, bf16[64,256]{1,0:T(8,128)(2,1)}, f32[32,3,4,128]{3,2,1,0:T(4,128)}) custom-call(f32[32,4,128]{2,1,0:T(4,128)} %copy-done.10, s32[32,128]{1,0:T(8,128)} %get-tuple-element.53.inv_ref, f32[64,256]{1,0:T(8,128)} %bitcast.23, f32[64,128]{1,0:T(8,128)} %get-tuple-element.70.corr_ref, s32[32,128]{1,0:T(8,128)} %get-tuple-element.59.index_ref), custom_call_target="tpu_custom_call" | custom-call | bytes 7200000 | tf_op jit(solution)/shard_map/pallas_call | solution.py:514
  118.6 6.0 %all-to-all-start.6 = ((f32[32,3,4,128]{3,2,1,0:T(4,128)}), f32[32,3,4,128]{3,2,1,0:T(4,128)S(1)}, u32[]{:S(2)}, u32[]{:S(2)}) async-start(f32[32,3,4,128]{3,2,1,0:T(4,128)} %get-tuple-element.71), calls=%async_computation.6 | async-start | bytes 393216 | tf_op jit(solution)/shard_map/all_to_all | solution.py:417
  124.6 5.7 %fusion.1 = f32[64,1,256]{2,1,0:T(1,128)S(1)} fusion(bf16[64,256,256]{2,1,0:T(8,128)(2,1)} %param.12, bf16[64,256,1]{1,0,2:T(8,128)(2,1)} %bitcast.24), kind=kOutput, calls=%fused_computation.3 | convolution fusion | flops 8388608 | bytes 8486912 | tf_op jit(solution)/shard_map/fij,fj->fi/dot_general | solution.py:469
  130.3 0.6 copy.30
  130.9 1.9 %all-to-all-done.6.recv_ref = f32[32,3,4,128]{3,2,1,0:T(4,128)S(1)} async-done(((f32[32,3,4,128]{3,2,1,0:T(4,128)}), f32[32,3,4,128]{3,2,1,0:T(4,128)S(1)}, u32[]{:S(2)}, u32[]{:S(2)}) %all-to-all-start.6) | async-done | bytes 196640 | tf_op jit(solution)/shard_map/all_to_all | solution.py:417
  132.9 4.7 %all-to-all-start.7 = ((bf16[16,144,128]{2,1,0:T(8,128)(2,1)}), bf16[16,144,128]{2,1,0:T(8,128)(2,1)S(1)}, u32[]{:S(2)}, u32[]{:S(2)}) async-start(bf16[16,144,128]{2,1,0:T(8,128)(2,1)} %get-tuple-element.74), calls=%async_computation.7 | async-start | bytes 1179648 | tf_op jit(solution)/shard_map/all_to_all | solution.py:417
  137.6 0.0 copy-done.4
  137.6 11.4 %shard_map.121 = f32[32,4,128]{2,1,0:T(4,128)} custom-call(s32[1]{0:T(128)} %bitcast.5.tile_ref, s32[32,2]{1,0:T(8,128)} %copy.12.mask_ref, f32[32,3,4,128]{3,2,1,0:T(4,128)} %copy-done.4, s32[32,128]{1,0:T(8,128)} %get-tuple-element.49.index_ref, s32[32,128]{1,0:T(8,128)} %get-tuple-element.50.inv_ref, f32[3,40,128]{2,1,0:T(8,128)} %get-tuple-element.65.refs_0_, ...), custom_call_target="tpu_custom_call" | custom-call | bytes 50400000 | tf_op jit(solution)/shard_map/pallas_call | solution.py:495
  149.0 0.0 all-to-all-done.7.got_ref
  149.0 1.8 collective-permute-start.2
  150.8 6.3 %all-to-all-start.8 = ((f32[32,4,128]{2,1,0:T(4,128)}), f32[32,4,128]{2,1,0:T(4,128)S(1)}, u32[]{:S(2)}, u32[]{:S(2)}) async-start(f32[32,4,128]{2,1,0:T(4,128)} %shard_map.121), calls=%async_computation.8 | async-start | bytes 131072 | tf_op jit(solution)/shard_map/all_to_all | solution.py:417
  157.0 0.0 collective-permute-done.2.mate_ref
  157.1 0.0 copy-done.1
  157.1 0.0 copy-start.6
  157.1 0.8 copy-done.6
  157.9 4.9 %shard_map.122 = (f32[144,128]{1,0:T(8,128)}, f32[64,128]{1,0:T(8,128)}) custom-call(s32[1]{0:T(128)} %bitcast.5.tile_ref, bf16[16,144,128]{2,1,0:T(8,128)(2,1)} %copy-done.1, bf16[16,144,128]{2,1,0:T(8,128)(2,1)} %copy-done.6, bf16[144,4608]{1,0:T(8,128)(2,1)} %op_ref.5, bf16[192,4608]{1,0:T(8,128)(2,1)} %fusion.take_ref, f32[64,128]{1,0:T(8,128)} %fusion.7.mine_ref, ...), custom_call_target="tpu_custom_call" | custom-call | bytes 14400000 | tf_op jit(solution)/shard_map/pallas_call | solution.py:504
  162.8 1.6 all-to-all-done.8.back_ref
  164.4 0.6 copy-done.9
  165.0 3.1 %shard_map.123 = f32[128,1,128]{2,1,0:T(1,128)} custom-call(f32[32,4,128]{2,1,0:T(4,128)} %copy-done.9, s32[32,128]{1,0:T(8,128)} %get-tuple-element.53.inv_ref, f32[64,256]{1,0:T(8,128)} %bitcast.22, f32[64,128]{1,0:T(8,128)} %get-tuple-element.79.corr_ref, f32[64,256]{1,0:T(8,128)} %refs_0_.3, f32[64,256]{1,0:T(8,128)} %get-tuple-element.80.refs_1_, ...), custom_call_target="tpu_custom_call" | custom-call | bytes 7200000 | tf_op jit(solution)/shard_map/pallas_call | solution.py:522
  168.1 17.4 %all_to_all.50.gram_ref = f32[128,1,128]{2,1,0:T(1,128)} all-to-all(f32[128,1,128]{2,1,0:T(1,128)} %shard_map.123), channel_id=1, replica_groups=mesh['grp'=4,'chip'=16,'core'=2] {'grp','chip','core'}, dimensions={0} | all-to-all | bytes 131072 | tf_op jit(solution)/shard_map/all_to_all | solution.py:417
  185.6 2.0 %shard_map.124 = (f32[64,256]{1,0:T(8,128)}, f32[144,100]{1,0:T(8,128)}) custom-call(f32[128,1,128]{2,1,0:T(1,128)} %all_to_all.50.gram_ref, f32[64,256]{1,0:T(8,128)} %refs_0_.3, f32[64,256]{1,0:T(8,128)} %get-tuple-element.80.refs_1_, f32[64,256]{1,0:T(8,128)} %get-tuple-element.81.refs_2_, f32[144,128]{1,0:T(8,128)} %get-tuple-element.82.refs_3_, ...), custom_call_target="tpu_custom_call" | custom-call | bytes 3600000 | tf_op jit(solution)/shard_map/pallas_call | solution.py:530
  (14 shorter events, 0.0 us)
Async XLA Ops:
  0.6 26.4 %copy-start.12 = (s32[64]{0:T(128)S(1)}, s32[64]{0:T(128)}, u32[]{:S(2)}) copy-start(s32[64]{0:T(128)} %param.18) | copy-start | bytes 772
  0.6 33.7 %copy-start.13 = (s32[32,2]{0,1:T(2,128)S(1)}, s32[32,2]{0,1:T(2,128)}, u32[]{:S(2)}) copy-start(s32[32,2]{0,1:T(2,128)} %param.17) | copy-start | bytes 772
  4.7 23.0 %all-to-all-start = ((f32[32,3,8,128]{3,2,1,0:T(8,128)}), f32[32,3,8,128]{3,2,1,0:T(8,128)S(1)}, u32[]{:S(2)}, u32[]{:S(2)}) async-start(f32[32,3,8,128]{3,2,1,0:T(8,128)} %get-tuple-element.45), calls=%async_computation | async-start | bytes 786432 | tf_op jit(solution)/shard_map/all_to_all | solution.py:417
  27.7 7.4 %copy-start = (f32[32,3,8,128]{3,2,1,0:T(8,128)}, f32[32,3,8,128]{3,2,1,0:T(8,128)S(1)}, u32[]{:S(2)}) copy-start(f32[32,3,8,128]{3,2,1,0:T(8,128)S(1)} %all-to-all-done.recv_ref.info_ref) | copy-start | bytes 1179652
  27.7 20.1 %all-to-all-start.1 = ((bf16[16,144,128]{2,1,0:T(8,128)(2,1)}), bf16[16,144,128]{2,1,0:T(8,128)(2,1)S(1)}, u32[]{:S(2)}, u32[]{:S(2)}) async-start(bf16[16,144,128]{2,1,0:T(8,128)(2,1)} %get-tuple-element.47), calls=%async_computation.1 | async-start | bytes 1179648 | tf_op jit(solution)/shard_map/all_to_all | solution.py:417
  47.8 8.1 %copy-start.3 = (bf16[16,144,128]{2,1,0:T(8,128)(2,1)}, bf16[16,144,128]{2,1,0:T(8,128)(2,1)S(1)}, u32[]{:S(2)}) copy-start(bf16[16,144,128]{2,1,0:T(8,128)(2,1)S(1)} %all-to-all-done.1.got_ref) | copy-start | bytes 1769476
  47.8 8.1 %collective-permute-start = (bf16[16,144,128]{2,1,0:T(8,128)(2,1)S(1)}, bf16[16,144,128]{2,1,0:T(8,128)(2,1)S(1)}, u32[]{:S(2)}, u32[]{:S(2)}) collective-permute-start(bf16[16,144,128]{2,1,0:T(8,128)(2,1)S(1)} %all-to-all-done.1.got_ref), channel_id=1, source_target_pairs={{0,1},{1,0},{2,3},{3,2},{4,5},{5,4},{6,7},{7,6},{8,9},{9,8},{10,11... | collective-permute-start | bytes 1769480 | tf_op jit(solution)/shard_map/ppermute | solution.py:499
  48.5 14.7 %all-to-all-start.2 = ((f32[32,4,128]{2,1,0:T(4,128)}), f32[32,4,128]{2,1,0:T(4,128)S(1)}, u32[]{:S(2)}, u32[]{:S(2)}) async-start(f32[32,4,128]{2,1,0:T(4,128)} %get-tuple-element.52), calls=%async_computation.2 | async-start | bytes 131072 | tf_op jit(solution)/shard_map/all_to_all | solution.py:417
  55.9 0.8 copy-start.8
  63.2 0.6 copy-start.11
  68.0 14.3 %all-to-all-start.3 = ((f32[32,3,4,128]{3,2,1,0:T(4,128)}), f32[32,3,4,128]{3,2,1,0:T(4,128)S(1)}, u32[]{:S(2)}, u32[]{:S(2)}) async-start(f32[32,3,4,128]{3,2,1,0:T(4,128)} %get-tuple-element.60), calls=%async_computation.3 | async-start | bytes 393216 | tf_op jit(solution)/shard_map/all_to_all | solution.py:417
  82.3 4.8 %copy-start.5 = (f32[32,3,4,128]{3,2,1,0:T(4,128)}, f32[32,3,4,128]{3,2,1,0:T(4,128)S(1)}, u32[]{:S(2)}) copy-start(f32[32,3,4,128]{3,2,1,0:T(4,128)S(1)} %all-to-all-done.3.recv_ref) | copy-start | bytes 589828
  82.3 16.2 %all-to-all-start.4 = ((bf16[16,144,128]{2,1,0:T(8,128)(2,1)}), bf16[16,144,128]{2,1,0:T(8,128)(2,1)S(1)}, u32[]{:S(2)}, u32[]{:S(2)}) async-start(bf16[16,144,128]{2,1,0:T(8,128)(2,1)} %get-tuple-element.63), calls=%async_computation.4 | async-start | bytes 1179648 | tf_op jit(solution)/shard_map/all_to_all | solution.py:417
  98.5 8.1 %copy-start.2 = (bf16[16,144,128]{2,1,0:T(8,128)(2,1)}, bf16[16,144,128]{2,1,0:T(8,128)(2,1)S(1)}, u32[]{:S(2)}) copy-start(bf16[16,144,128]{2,1,0:T(8,128)(2,1)S(1)} %all-to-all-done.4.got_ref) | copy-start | bytes 1769476
  98.5 8.0 %collective-permute-start.1 = (bf16[16,144,128]{2,1,0:T(8,128)(2,1)S(1)}, bf16[16,144,128]{2,1,0:T(8,128)(2,1)S(1)}, u32[]{:S(2)}, u32[]{:S(2)}) collective-permute-start(bf16[16,144,128]{2,1,0:T(8,128)(2,1)S(1)} %all-to-all-done.4.got_ref), channel_id=1, source_target_pairs={{0,1},{1,0},{2,3},{3,2},{4,5},{5,4},{6,7},{7,6},{8,9},{9,8},{10,11... | collective-permute-start | bytes 1769480 | tf_op jit(solution)/shard_map/ppermute | solution.py:499
  100.3 13.6 %all-to-all-start.5 = ((f32[32,4,128]{2,1,0:T(4,128)}), f32[32,4,128]{2,1,0:T(4,128)S(1)}, u32[]{:S(2)}, u32[]{:S(2)}) async-start(f32[32,4,128]{2,1,0:T(4,128)} %shard_map.118), calls=%async_computation.5 | async-start | bytes 131072 | tf_op jit(solution)/shard_map/all_to_all | solution.py:417
  106.5 0.8 copy-start.7
  113.8 0.6 copy-start.10
  118.6 14.2 %all-to-all-start.6 = ((f32[32,3,4,128]{3,2,1,0:T(4,128)}), f32[32,3,4,128]{3,2,1,0:T(4,128)S(1)}, u32[]{:S(2)}, u32[]{:S(2)}) async-start(f32[32,3,4,128]{3,2,1,0:T(4,128)} %get-tuple-element.71), calls=%async_computation.6 | async-start | bytes 393216 | tf_op jit(solution)/shard_map/all_to_all | solution.py:417
  132.8 4.7 %copy-start.4 = (f32[32,3,4,128]{3,2,1,0:T(4,128)}, f32[32,3,4,128]{3,2,1,0:T(4,128)S(1)}, u32[]{:S(2)}) copy-start(f32[32,3,4,128]{3,2,1,0:T(4,128)S(1)} %all-to-all-done.6.recv_ref) | copy-start | bytes 589828
  132.9 16.1 %all-to-all-start.7 = ((bf16[16,144,128]{2,1,0:T(8,128)(2,1)}), bf16[16,144,128]{2,1,0:T(8,128)(2,1)S(1)}, u32[]{:S(2)}, u32[]{:S(2)}) async-start(bf16[16,144,128]{2,1,0:T(8,128)(2,1)} %get-tuple-element.74), calls=%async_computation.7 | async-start | bytes 1179648 | tf_op jit(solution)/shard_map/all_to_all | solution.py:417
  149.0 8.1 %copy-start.1 = (bf16[16,144,128]{2,1,0:T(8,128)(2,1)}, bf16[16,144,128]{2,1,0:T(8,128)(2,1)S(1)}, u32[]{:S(2)}) copy-start(bf16[16,144,128]{2,1,0:T(8,128)(2,1)S(1)} %all-to-all-done.7.got_ref) | copy-start | bytes 1769476
  149.0 8.0 %collective-permute-start.2 = (bf16[16,144,128]{2,1,0:T(8,128)(2,1)S(1)}, bf16[16,144,128]{2,1,0:T(8,128)(2,1)S(1)}, u32[]{:S(2)}, u32[]{:S(2)}) collective-permute-start(bf16[16,144,128]{2,1,0:T(8,128)(2,1)S(1)} %all-to-all-done.7.got_ref), channel_id=1, source_target_pairs={{0,1},{1,0},{2,3},{3,2},{4,5},{5,4},{6,7},{7,6},{8,9},{9,8},{10,11... | collective-permute-start | bytes 1769480 | tf_op jit(solution)/shard_map/ppermute | solution.py:499
  150.8 13.6 %all-to-all-start.8 = ((f32[32,4,128]{2,1,0:T(4,128)}), f32[32,4,128]{2,1,0:T(4,128)S(1)}, u32[]{:S(2)}, u32[]{:S(2)}) async-start(f32[32,4,128]{2,1,0:T(4,128)} %shard_map.121), calls=%async_computation.8 | async-start | bytes 131072 | tf_op jit(solution)/shard_map/all_to_all | solution.py:417
  157.1 0.8 copy-start.6
  164.4 0.6 copy-start.9

commit v3 on v2

--- a/solution.py
+++ b/solution.py
@@ -20,6 +20,7 @@
 NODES = ROWS * LANES
 PITCH = 40
 UNROLL = 4
+BATCH = 8
 TILES = 32
 ALL = 128
 
@@ -41,13 +42,15 @@
 SMEM = pl.BlockSpec(memory_space=pltpu.SMEM)
 
 
-def call(body, outs, in_specs, scratch=(), micros=1.0):
+def call(body, outs, in_specs, scratch=(), micros=1.0, grid=(), out_specs=None, mib=None):
     return pl.pallas_call(
         body,
         out_shape=outs,
+        grid=grid,
         in_specs=in_specs,
-        out_specs=jax.tree.map(lambda _: VMEM, outs),
+        out_specs=out_specs or jax.tree.map(lambda _: VMEM, outs),
         scratch_shapes=list(scratch),
+        compiler_params=pltpu.CompilerParams(vmem_limit_bytes=mib and mib << 20),
         cost_estimate=pl.CostEstimate(
             flops=0, transcendentals=0, bytes_accessed=int(micros * 3.6e6)
         ),
@@ -171,7 +174,7 @@
     root = lax.rsqrt((dx * dx + eps_square) + (dy * dy + dz * dz))
     cube = root * (root * root)
     along = (dx * force[0] + dy * force[1]) + dz * force[2]
-    return root + eps_square * cube, along * cube
+    return root + eps_square * cube, cube, along * cube
 
 
 def halves(value):
@@ -181,7 +184,88 @@
 
 def near_kernel(first, tile_ref, mask_ref, recv_ref, index_ref, inv_ref, *refs):
     if first:
-        out_ref, pos, rims_ref, force, lines, column, weight, total, mix = refs
+        out_ref, pos, rims_ref, near_ref, cube_ref = refs[:5]
+    else:
+        pos, rims_ref, near_ref, cube_ref, out_ref = refs[:5]
+    force, lines, column, weight, total, mix = refs[5:]
+    step = pl.program_id(0)
+
+    @pl.when(step == 0)
+    def _():
+        gather_leaves(
+            first, tile_ref, recv_ref, index_ref, pos, rims_ref, force, lines
+        )
+
+    def one_leaf(b, u):
+        i = step * BATCH + b
+        for c in range(3):
+            row = pos[c, pl.ds(i + 1, 1), :]
+            column[u, c] = jnp.broadcast_to(row, (LANES, LANES)).T
+        sums = [jnp.zeros((8, LANES), F32)] * 2
+        for w in range(3):
+            spot, push = (
+                [jnp.broadcast_to(ref[c, pl.ds(i + w, 1), :], (8, LANES)) for c in range(3)]
+                for ref in (pos, force)
+            )
+            inner = (spot[0] * push[0] + spot[1] * push[1]) + spot[2] * push[2]
+            for g in range(LANES // 16):
+                rows = slice(16 * g, 16 * g + 16)
+                found = []
+                for h in (16 * g, 16 * g + 8):
+                    target = [column[u, c, h : h + 8, :] for c in range(3)]
+                    if first:
+                        near, cube, turn = pair_weights(target, spot, push)
+                        cube_ref[b, w, h : h + 8, :] = cube
+                        found.append((turn, near))
+                    else:
+                        along = (target[0] * push[0] + target[1] * push[1]) + (
+                            target[2] * push[2] - inner
+                        )
+                        found.append((along * cube_ref[b, w, h : h + 8, :],))
+                halves_of = [jnp.concatenate(k, axis=0).astype(BF16) for k in zip(*found)]
+                weight[u, w, rows, :] = halves_of[0]
+                if first:
+                    near_ref[b, w, rows, :] = halves_of[1]
+            for k, right in enumerate((near_ref[b, w], weight[u, w])):
+                left = lines[k, pl.ds(i + w, 8, stride=PITCH), :].astype(BF16)
+                part = lax.dot_general(
+                    left, right, (((1,), (1,)), ((), ())), preferred_element_type=F32
+                )
+                if w != 1:
+                    part = part * mask_ref[i, w // 2].astype(F32)
+                sums[k] = sums[k] + part
+        for k in range(2):
+            total[k, pl.ds(8 * i, 8), :] = sums[k]
+
+    def leaves(i, carry):
+        for u in range(UNROLL):
+            one_leaf(i * UNROLL + u, u)
+        return carry
+
+    lax.fori_loop(0, BATCH // UNROLL, leaves, 0)
+
+    @pl.when(step == ROWS // BATCH - 1)
+    def _():
+        weights = total[1, pl.ds(6, ROWS, stride=8), :]
+
+        def gathered(k, c):
+            return total[k, pl.ds(c, ROWS, stride=8), :]
+
+        for c in range(3):
+            mix[c * ROWS : (c + 1) * ROWS, :] = (
+                (gathered(0, c) + gathered(0, 3 + c))
+                + pos[c, 1 : ROWS + 1, :] * weights
+                - (gathered(1, c) + gathered(1, 3 + c))
+            )
+        slot = inv_ref[...]
+        parts = pick(
+            lambda c, r: mix[c * ROWS + r : c * ROWS + r + 1, :], 3, slot >> 7, slot & 127
+        )
+        swap_out(mix, parts, out_ref, 4)
+
+
+def gather_leaves(first, tile_ref, recv_ref, index_ref, pos, rims_ref, force, lines):
+    if first:
         me = tile_ref[0]
         before, after = jnp.maximum(me - 1, 0), jnp.minimum(me + 1, TILES - 1)
         rims_ref[0:8, :] = jnp.broadcast_to(recv_ref[before, 2, 7:8, :], (8, LANES)).astype(
@@ -192,7 +276,6 @@
         )
         count, base = 6, 3
     else:
-        pos, rims_ref, out_ref, force, lines, column, weight, total, mix = refs
         count, base = 3, 0
     slot = index_ref[...]
     parts = pick(lambda c, r: recv_ref[r, 1, c : c + 1, :], count, slot >> 7, slot & 127)
@@ -228,59 +311,6 @@
     for k, ref in enumerate((force, pos)):
         for c in range(3):
             lines[k, plane(c), :], lines[k, plane(3 + c), :] = halves(ref[c])
-
-    def one_leaf(i, u):
-        for c in range(3):
-            row = pos[c, pl.ds(i + 1, 1), :]
-            column[u, c] = jnp.broadcast_to(row, (LANES, LANES)).T
-        sums = [jnp.zeros((8, LANES), F32)] * 2
-        for w in range(3):
-            spot, push = (
-                [jnp.broadcast_to(ref[c, pl.ds(i + w, 1), :], (8, LANES)) for c in range(3)]
-                for ref in (pos, force)
-            )
-            for g in range(LANES // 16):
-                found = [
-                    pair_weights([column[u, c, h : h + 8, :] for c in range(3)], spot, push)
-                    for h in (16 * g, 16 * g + 8)
-                ]
-                for k in range(2):
-                    weight[u, k, w, 16 * g : 16 * g + 16, :] = jnp.concatenate(
-                        [found[0][k], found[1][k]], axis=0
-                    ).astype(BF16)
-            for k in range(2):
-                left = lines[k, pl.ds(i + w, 8, stride=PITCH), :].astype(BF16)
-                part = lax.dot_general(
-                    left, weight[u, k, w], (((1,), (1,)), ((), ())), preferred_element_type=F32
-                )
-                if w != 1:
-                    part = part * mask_ref[i, w // 2].astype(F32)
-                sums[k] = sums[k] + part
-        for k in range(2):
-            total[k, pl.ds(8 * i, 8), :] = sums[k]
-
-    def leaves(i, carry):
-        for u in range(UNROLL):
-            one_leaf(i * UNROLL + u, u)
-        return carry
-
-    lax.fori_loop(0, ROWS // UNROLL, leaves, 0)
-
-    def gathered(k, c):
-        return total[k, pl.ds(c, ROWS, stride=8), :]
-
-    weights = gathered(1, 6)
-    for c in range(3):
-        mix[c * ROWS : (c + 1) * ROWS, :] = (
-            (gathered(0, c) + gathered(0, 3 + c))
-            + pos[c, 1 : ROWS + 1, :] * weights
-            - (gathered(1, c) + gathered(1, 3 + c))
-        )
-    slot = inv_ref[...]
-    parts = pick(
-        lambda c, r: mix[c * ROWS + r : c * ROWS + r + 1, :], 3, slot >> 7, slot & 127
-    )
-    swap_out(mix, parts, out_ref, 4)
 
 
 def body_kernel(
@@ -399,9 +429,9 @@
     t = [g[0, i] + g[0, i + 1] for i in range(3)]
     l00 = jnp.sqrt(n[0, 0])
     l10, l20 = n[1, 0] / l00, n[2, 0] / l00
-    l11 = jnp.sqrt(n[1, 1] - l10 * l10)
+    l11 = jnp.sqrt(jnp.maximum(n[1, 1] - l10 * l10, n[1, 1] * 1e-7))
     l21 = (n[2, 1] - l20 * l10) / l11
-    l22 = jnp.sqrt(n[2, 2] - l20 * l20 - l21 * l21)
+    l22 = jnp.sqrt(jnp.maximum(n[2, 2] - l20 * l20 - l21 * l21, n[2, 2] * 1e-7))
     f0 = t[0] / l00
     f1 = (t[1] - l10 * f0) / l11
     f2 = (t[2] - l20 * f0 - l21 * f1) / l22
@@ -439,6 +469,8 @@
     spots = shape((3, PITCH, LANES))
     rims = shape((16, LANES), jnp.int32)
     table = pltpu.VMEM((3, ROWS, LANES), F32)
+    pairs = (ROWS, 3, LANES, LANES)
+    block = pl.BlockSpec((BATCH, 3, LANES, LANES), lambda i: (i, 0, 0, 0))
     padded = pltpu.VMEM((3, PITCH, LANES), F32)
     mix4 = pltpu.VMEM((4 * ROWS, LANES), F32)
     blocks8 = pltpu.VMEM((8 * PITCH, LANES), F32)
@@ -482,18 +514,26 @@
             padded,
             pltpu.VMEM((2, 8 * PITCH, LANES), F32),
             pltpu.VMEM((UNROLL, 3, LANES, LANES), F32),
-            pltpu.VMEM((UNROLL, 2, 3, LANES, LANES), BF16),
+            pltpu.VMEM((UNROLL, 3, LANES, LANES), BF16),
             pltpu.VMEM((2, 8 * ROWS, LANES), F32),
             mix4,
         ]
+        steps = (ROWS // BATCH,)
+        result = shape((ROWS, 4, LANES))
         if first:
             info = recv
-            out, pos, rim = call(
-                near, (shape((ROWS, 4, LANES)), spots, rims), specs, scratch, 14.0
+            out, pos, rim, *kept = call(
+                near,
+                (result, spots, rims, shape(pairs, BF16), shape(pairs)),
+                specs,
+                scratch,
+                13.0,
+                steps,
+                (VMEM, VMEM, VMEM, block, block),
             )(tile, neighbours, recv, leaf_index, inv_leaf)
         else:
-            out = call(near, shape((ROWS, 4, LANES)), specs + [VMEM] * 2, scratch, 14.0)(
-                tile, neighbours, recv, leaf_index, inv_leaf, pos, rim
+            out = call(near, result, specs + [VMEM, VMEM, block, block], scratch, 9.0, steps)(
+                tile, neighbours, recv, leaf_index, inv_leaf, pos, rim, *kept
             )
         got, out = lax.optimization_barrier((got, out))
         mate = lax.ppermute(got, "core", [(0, 1), (1, 0)])
@@ -507,6 +547,7 @@
             [SMEM] + [VMEM] * 7,
             [pltpu.VMEM((3, TILES, LANES), F32), pltpu.VMEM((TILES, COLS, LANES), BF16)],
             4.0,
+            mib=14,
         )(tile, got, mate, body_op, take, mine, info, recv)
         z.append(image)
         if not last:

time: 189 us -> 184 us (0.974)
  Pallas kernels: 71.3 us -> 65.2 us
  waiting for transfers between devices: 8.19 us -> 11.6 us
  local copies, waits for them, and re-layouts: 7.06 us -> 9.73 us
  starting transfers between devices: 62 us -> 60.1 us
    pallas_call x3, Pallas kernels: 15.2 us -> 9.55 us  [local(): call(functools.partial(body_kernel, first, last), tuple(made), [SMEM] + [...]
    all_to_all x9, waiting for transfers between devices: 8.19 us -> 11.6 us  [exchange(): return lax.all_to_all(array, axis, split_axis=0, concat_axis=0, tiled=True)]
    unnamed x29 -> x31, local copies, waits for them, and re-layouts: 5.03 us -> 7.7 us
  transfers between devices with their start and end apart: 12 -> 12, of which waited for: 5 -> 7; matrix products, arithmetic and copies ran while one was open for 13% -> 12% of each run, Pallas kernels for 29% -> 26%
where the time goes in v3:
time: 184 us; the launch traced here: 183 us
  Pallas kernels  65.2 us (35%)
  starting transfers between devices  60.1 us (33%)
  matrix products  17 us (9%)
  blocking collectives  16.2 us (9%)
  waiting for transfers between devices  11.6 us (6%)
  local copies, waits for them, and re-layouts  9.73 us (5%)
  other arithmetic  2 us (1%)
    all_to_all x9, starting transfers between devices, exchange(): return lax.all_to_all(array, axis, split_axis=0, concat_axis=0, tiled=True)  55.8 us
    pallas_call x2, Pallas kernels, local(): call(near, result, specs + [VMEM, VMEM, block, block], scratch, 9.0, steps)  21.2 us
    dot_general x3, matrix products, local(): jnp.einsum('fij,fj->fi', fiber_ops, low, preferred_element_type=F32)  17 us
    all_to_all x1, blocking collectives, exchange(): return lax.all_to_all(array, axis, split_axis=0, concat_axis=0, tiled=True)  16.2 us
    pallas_call x1, Pallas kernels, local(): call(near, (result, spots, rims, shape(pairs, BF16), shape(pairs)), specs...  13.7 us
    all_to_all x9, waiting for transfers between devices, exchange(): return lax.all_to_all(array, axis, split_axis=0, concat_axis=0, tiled=True)  11.6 us
    pallas_call x3, Pallas kernels, local(): call(functools.partial(body_kernel, first, last), tuple(made), [SMEM] + [...  9.55 us
    pallas_call x2, Pallas kernels, local(): call(join_kernel, (shape((FIB, ORDER)), shape((FIB, ORDER), BF16), shape(...  8.3 us
  transfers between devices with their start and end apart: 12, of which 7 were waited for; matrix products, arithmetic and copies ran while one was open for 12% of the time, Pallas kernels for 26%

profile of v3, /device:TPU:1, one launch (start us, length us, event | category | flops | bytes accessed | tf_op | source)
XLA Modules:
  0.0 182.6 jit_solution(9507460565912890707)
XLA Ops:
  0.6 0.0 copy-start.13
  0.7 4.1 %shard_map.113 = (f32[32,3,8,128]{3,2,1,0:T(8,128)}, s32[32,128]{1,0:T(8,128)}) custom-call(f32[3,4096]{1,0:T(4,128)} %pos_ref.1, f32[64,256]{1,0:T(8,128)} %refs_0_.3, s32[1,4096]{1,0:T(1,128)} %send_ref.1, s32[1,4096]{1,0:T(1,128)} %leaf_ref.3, s32[1,64]{1,0:T(1,128)} %bitcast.27, s32[1,64]{1,0:T(1,128)} %bitcast.28), custom_call_target="tpu_custom_call" | custom-call | bytes 7200000 | tf_op jit(solution)/shard_map/pallas_call | solution.py:479
  4.8 9.6 %all-to-all-start = ((f32[32,3,8,128]{3,2,1,0:T(8,128)}), f32[32,3,8,128]{3,2,1,0:T(8,128)S(1)}, u32[]{:S(2)}, u32[]{:S(2)}) async-start(f32[32,3,8,128]{3,2,1,0:T(8,128)} %get-tuple-element.47), calls=%async_computation | async-start | bytes 786432 | tf_op jit(solution)/shard_map/all_to_all | solution.py:447
  14.4 0.8 convert_bitcast_fusion
  15.2 0.7 broadcast_add_fusion
  16.0 0.1 add.26
  16.1 0.4 fusion.take_ref
  16.4 5.6 %fusion.5 = f32[64,1,256]{2,1,0:T(1,128)S(1)} fusion(bf16[64,256,256]{2,1,0:T(8,128)(2,1)} %param.12, bf16[64,256,1]{1,0,2:T(8,128)(2,1)S(1)} %convert_bitcast_fusion), kind=kOutput, calls=%fused_computation.9 | convolution fusion | flops 8388608 | bytes 8486912 | tf_op jit(solution)/shard_map/fij,fj->fi/dot_general | solution.py:501
  22.1 0.7 copy.32
  22.7 3.2 %shard_map.114 = (s32[32,128]{1,0:T(8,128)}, s32[32,128]{1,0:T(8,128)}, s32[32,128]{1,0:T(8,128)}, f32[144,128]{1,0:T(8,128)}, bf16[16,144,128]{2,1,0:T(8,128)(2,1)}) custom-call(s32[1,4096]{1,0:T(1,128)} %leaf_ref.3, s32[1,4096]{1,0:T(1,128)} %send_ref.1, f32[144,100]{1,0:T(8,128)} %bitcast.26), custom_call_target="tpu_custom_call" | custom-call | bytes 7200000 | tf_op jit(solution)/shard_map/pallas_call | solution.py:489
  25.9 0.1 fusion.7.mine_ref
  25.9 0.0 all-to-all-done.recv_ref.info_ref
  25.9 0.0 copy-start
  26.0 6.7 %all-to-all-start.1 = ((bf16[16,144,128]{2,1,0:T(8,128)(2,1)}), bf16[16,144,128]{2,1,0:T(8,128)(2,1)}, u32[]{:S(2)}, u32[]{:S(2)}) async-start(bf16[16,144,128]{2,1,0:T(8,128)(2,1)} %get-tuple-element.49), calls=%async_computation.1 | async-start | bytes 1179648 | tf_op jit(solution)/shard_map/all_to_all | solution.py:447
  32.7 0.0 copy-done.14
  32.7 0.7 copy.12.mask_ref
  33.4 13.7 %shard_map.115 = (f32[32,4,128]{2,1,0:T(4,128)}, f32[3,40,128]{2,1,0:T(8,128)}, s32[16,128]{1,0:T(8,128)}, bf16[32,3,128,128]{3,2,1,0:T(8,128)(2,1)}, f32[32,3,128,128]{3,2,1,0:T(8,128)}) custom-call(s32[1]{0:T(128)} %bitcast.5.tile_ref, s32[32,2]{1,0:T(8,128)} %copy.12.mask_ref, f32[32,3,8,128]{3,2,1,0:T(8,128)} %copy-done, ...), custom_call_target="tpu_custom_call" | custom-call | bytes 46800000 | tf_op jit(solution)/shard_map/pallas_call | solution.py:525
  47.0 0.0 all-to-all-done.1.got_ref
  47.0 0.7 collective-permute-start
  47.7 7.3 %all-to-all-start.2 = ((f32[32,4,128]{2,1,0:T(4,128)}), f32[32,4,128]{2,1,0:T(4,128)S(1)}, u32[]{:S(2)}, u32[]{:S(2)}) async-start(f32[32,4,128]{2,1,0:T(4,128)} %get-tuple-element.54), calls=%async_computation.2 | async-start | bytes 131072 | tf_op jit(solution)/shard_map/all_to_all | solution.py:447
  55.1 0.0 collective-permute-done.mate_ref
  55.1 1.0 copy-done.1
  56.1 3.2 %shard_map.116 = (f32[144,128]{1,0:T(8,128)S(1)}, f32[64,128]{1,0:T(8,128)S(1)}, bf16[16,144,128]{2,1,0:T(8,128)(2,1)S(1)}) custom-call(s32[1]{0:T(128)} %bitcast.5.tile_ref, bf16[16,144,128]{2,1,0:T(8,128)(2,1)} %all-to-all-done.1.got_ref, bf16[16,144,128]{2,1,0:T(8,128)(2,1)} %collective-permute-done.mate_ref, bf16[144,4608]{1,0:T(8,128)(2,1)S(1)} %copy-done.3, ...), custom_call_target="tpu_custom_call" | custom-call | bytes 14400000 | tf_op jit(solution)/shard_map/pallas_call | solution.py:544
  59.2 0.8 copy-done.5
  60.1 0.6 copy-done.6
  60.7 0.6 copy-done.11
  61.3 1.1 all-to-all-done.2.back_ref
  62.4 0.6 copy-done.12
  63.0 4.2 %shard_map.117 = (f32[64,256]{1,0:T(8,128)}, bf16[64,256]{1,0:T(8,128)(2,1)}, f32[32,3,4,128]{3,2,1,0:T(4,128)}) custom-call(f32[32,4,128]{2,1,0:T(4,128)} %copy-done.12, s32[32,128]{1,0:T(8,128)} %get-tuple-element.55.inv_ref, f32[64,256]{1,0:T(8,128)} %bitcast.21, f32[64,128]{1,0:T(8,128)} %copy-done.11, s32[32,128]{1,0:T(8,128)} %get-tuple-element.61.index_ref), custom_call_target="tpu_custom_call" | custom-call | bytes 7200000 | tf_op jit(solution)/shard_map/pallas_call | solution.py:555
  67.2 6.4 %all-to-all-start.3 = ((f32[32,3,4,128]{3,2,1,0:T(4,128)}), f32[32,3,4,128]{3,2,1,0:T(4,128)}, u32[]{:S(2)}, u32[]{:S(2)}) async-start(f32[32,3,4,128]{3,2,1,0:T(4,128)} %get-tuple-element.62), calls=%async_computation.3 | async-start | bytes 393216 | tf_op jit(solution)/shard_map/all_to_all | solution.py:447
  73.6 5.7 %fusion.3 = f32[64,1,256]{2,1,0:T(1,128)S(1)} fusion(bf16[64,256,256]{2,1,0:T(8,128)(2,1)} %param.12, bf16[64,256,1]{1,0,2:T(8,128)(2,1)} %bitcast.25), kind=kOutput, calls=%fused_computation.6 | convolution fusion | flops 8388608 | bytes 8486912 | tf_op jit(solution)/shard_map/fij,fj->fi/dot_general | solution.py:501
  79.3 0.7 copy.31
  79.9 1.9 %all-to-all-done.3.recv_ref = f32[32,3,4,128]{3,2,1,0:T(4,128)} async-done(((f32[32,3,4,128]{3,2,1,0:T(4,128)}), f32[32,3,4,128]{3,2,1,0:T(4,128)}, u32[]{:S(2)}, u32[]{:S(2)}) %all-to-all-start.3) | async-done | bytes 196640 | tf_op jit(solution)/shard_map/all_to_all | solution.py:447
  81.8 4.8 %all-to-all-start.4 = ((bf16[16,144,128]{2,1,0:T(8,128)(2,1)}), bf16[16,144,128]{2,1,0:T(8,128)(2,1)}, u32[]{:S(2)}, u32[]{:S(2)}) async-start(bf16[16,144,128]{2,1,0:T(8,128)(2,1)} %copy-done.5), calls=%async_computation.4 | async-start | bytes 1179648 | tf_op jit(solution)/shard_map/all_to_all | solution.py:447
  86.6 10.6 %shard_map.118 = f32[32,4,128]{2,1,0:T(4,128)} custom-call(s32[1]{0:T(128)} %bitcast.5.tile_ref, s32[32,2]{1,0:T(8,128)} %copy.12.mask_ref, f32[32,3,4,128]{3,2,1,0:T(4,128)} %all-to-all-done.3.recv_ref, s32[32,128]{1,0:T(8,128)} %get-tuple-element.51.index_ref, s32[32,128]{1,0:T(8,128)} %get-tuple-element.52.inv_ref, ...), custom_call_target="tpu_custom_call" | custom-call | bytes 32400000 | tf_op jit(solution)/shard_map/pallas_call | solution.py:535
  97.2 0.9 all-to-all-done.4.got_ref
  98.1 1.8 collective-permute-start.1
  99.9 5.4 %all-to-all-start.5 = ((f32[32,4,128]{2,1,0:T(4,128)}), f32[32,4,128]{2,1,0:T(4,128)}, u32[]{:S(2)}, u32[]{:S(2)}) async-start(f32[32,4,128]{2,1,0:T(4,128)} %shard_map.118), calls=%async_computation.5 | async-start | bytes 131072 | tf_op jit(solution)/shard_map/all_to_all | solution.py:447
  105.3 0.0 collective-permute-done.1.mate_ref
  105.3 3.2 %shard_map.119 = (f32[144,128]{1,0:T(8,128)S(1)}, f32[64,128]{1,0:T(8,128)S(1)}, bf16[16,144,128]{2,1,0:T(8,128)(2,1)S(1)}) custom-call(s32[1]{0:T(128)} %bitcast.5.tile_ref, bf16[16,144,128]{2,1,0:T(8,128)(2,1)} %all-to-all-done.4.got_ref, bf16[16,144,128]{2,1,0:T(8,128)(2,1)} %collective-permute-done.1.mate_ref, bf16[144,4608]{1,0:T(8,128)(2,1)S(1)} %copy-done.3, ...), custom_call_target="tpu_custom_call" | custom-call | bytes 14400000 | tf_op jit(solution)/shard_map/pallas_call | solution.py:544
  108.5 0.0 copy-start.4
  108.5 0.8 copy-done.4
  109.4 0.6 copy-done.7
  110.0 0.6 copy-done.10
  110.6 2.0 %all-to-all-done.5.back_ref = f32[32,4,128]{2,1,0:T(4,128)} async-done(((f32[32,4,128]{2,1,0:T(4,128)}), f32[32,4,128]{2,1,0:T(4,128)}, u32[]{:S(2)}, u32[]{:S(2)}) %all-to-all-start.5) | async-done | bytes 65568 | tf_op jit(solution)/shard_map/all_to_all | solution.py:447
  112.6 4.2 %shard_map.120 = (f32[64,256]{1,0:T(8,128)}, bf16[64,256]{1,0:T(8,128)(2,1)}, f32[32,3,4,128]{3,2,1,0:T(4,128)}) custom-call(f32[32,4,128]{2,1,0:T(4,128)} %all-to-all-done.5.back_ref, s32[32,128]{1,0:T(8,128)} %get-tuple-element.55.inv_ref, f32[64,256]{1,0:T(8,128)} %bitcast.23, f32[64,128]{1,0:T(8,128)} %copy-done.10, s32[32,128]{1,0:T(8,128)} %get-tuple-element.61.index_ref), custom_call_target="tpu_custom_call" | custom-call | bytes 7200000 | tf_op jit(solution)/shard_map/pallas_call | solution.py:555
  116.7 5.5 %all-to-all-start.6 = ((f32[32,3,4,128]{3,2,1,0:T(4,128)}), f32[32,3,4,128]{3,2,1,0:T(4,128)}, u32[]{:S(2)}, u32[]{:S(2)}) async-start(f32[32,3,4,128]{3,2,1,0:T(4,128)} %get-tuple-element.75), calls=%async_computation.6 | async-start | bytes 393216 | tf_op jit(solution)/shard_map/all_to_all | solution.py:447
  122.2 5.7 %fusion.1 = f32[64,1,256]{2,1,0:T(1,128)S(1)} fusion(bf16[64,256,256]{2,1,0:T(8,128)(2,1)} %param.12, bf16[64,256,1]{1,0,2:T(8,128)(2,1)} %bitcast.24), kind=kOutput, calls=%fused_computation.3 | convolution fusion | flops 8388608 | bytes 8486912 | tf_op jit(solution)/shard_map/fij,fj->fi/dot_general | solution.py:501
  127.8 0.6 copy.30
  128.5 2.0 %all-to-all-done.6.recv_ref = f32[32,3,4,128]{3,2,1,0:T(4,128)} async-done(((f32[32,3,4,128]{3,2,1,0:T(4,128)}), f32[32,3,4,128]{3,2,1,0:T(4,128)}, u32[]{:S(2)}, u32[]{:S(2)}) %all-to-all-start.6) | async-done | bytes 196640 | tf_op jit(solution)/shard_map/all_to_all | solution.py:447
  130.5 4.7 %all-to-all-start.7 = ((bf16[16,144,128]{2,1,0:T(8,128)(2,1)}), bf16[16,144,128]{2,1,0:T(8,128)(2,1)}, u32[]{:S(2)}, u32[]{:S(2)}) async-start(bf16[16,144,128]{2,1,0:T(8,128)(2,1)} %copy-done.4), calls=%async_computation.7 | async-start | bytes 1179648 | tf_op jit(solution)/shard_map/all_to_all | solution.py:447
  135.2 10.6 %shard_map.121 = f32[32,4,128]{2,1,0:T(4,128)} custom-call(s32[1]{0:T(128)} %bitcast.5.tile_ref, s32[32,2]{1,0:T(8,128)} %copy.12.mask_ref, f32[32,3,4,128]{3,2,1,0:T(4,128)} %all-to-all-done.6.recv_ref, s32[32,128]{1,0:T(8,128)} %get-tuple-element.51.index_ref, s32[32,128]{1,0:T(8,128)} %get-tuple-element.52.inv_ref, ...), custom_call_target="tpu_custom_call" | custom-call | bytes 32400000 | tf_op jit(solution)/shard_map/pallas_call | solution.py:535
  145.8 0.9 all-to-all-done.7.got_ref
  146.7 1.8 collective-permute-start.2
  148.5 5.4 %all-to-all-start.8 = ((f32[32,4,128]{2,1,0:T(4,128)}), f32[32,4,128]{2,1,0:T(4,128)}, u32[]{:S(2)}, u32[]{:S(2)}) async-start(f32[32,4,128]{2,1,0:T(4,128)} %shard_map.121), calls=%async_computation.8 | async-start | bytes 131072 | tf_op jit(solution)/shard_map/all_to_all | solution.py:447
  153.9 0.0 collective-permute-done.2.mate_ref
  153.9 3.2 %shard_map.122 = (f32[144,128]{1,0:T(8,128)S(1)}, f32[64,128]{1,0:T(8,128)S(1)}) custom-call(s32[1]{0:T(128)} %bitcast.5.tile_ref, bf16[16,144,128]{2,1,0:T(8,128)(2,1)} %all-to-all-done.7.got_ref, bf16[16,144,128]{2,1,0:T(8,128)(2,1)} %collective-permute-done.2.mate_ref, bf16[144,4608]{1,0:T(8,128)(2,1)S(1)} %copy-done.3, ...), custom_call_target="tpu_custom_call" | custom-call | bytes 14400000 | tf_op jit(solution)/shard_map/pallas_call | solution.py:544
  157.1 0.0 copy-start.8
  157.1 0.6 copy-done.8
  157.8 0.6 copy-done.9
  158.3 2.9 %all-to-all-done.8.back_ref = f32[32,4,128]{2,1,0:T(4,128)} async-done(((f32[32,4,128]{2,1,0:T(4,128)}), f32[32,4,128]{2,1,0:T(4,128)}, u32[]{:S(2)}, u32[]{:S(2)}) %all-to-all-start.8) | async-done | bytes 65568 | tf_op jit(solution)/shard_map/all_to_all | solution.py:447
  161.3 3.2 %shard_map.123 = f32[128,1,128]{2,1,0:T(1,128)} custom-call(f32[32,4,128]{2,1,0:T(4,128)} %all-to-all-done.8.back_ref, s32[32,128]{1,0:T(8,128)} %get-tuple-element.55.inv_ref, f32[64,256]{1,0:T(8,128)} %bitcast.22, f32[64,128]{1,0:T(8,128)} %copy-done.9, f32[64,256]{1,0:T(8,128)} %refs_0_.3, f32[64,256]{1,0:T(8,128)} %get-tuple-element.84.refs_1_, ...), custom_call_target="tpu_custom_call" | custom-call | bytes 7200000 | tf_op jit(solution)/shard_map/pallas_call | solution.py:563
  164.4 16.2 %all_to_all.50.gram_ref = f32[128,1,128]{2,1,0:T(1,128)} all-to-all(f32[128,1,128]{2,1,0:T(1,128)} %shard_map.123), channel_id=1, replica_groups=mesh['grp'=4,'chip'=16,'core'=2] {'grp','chip','core'}, dimensions={0} | all-to-all | bytes 131072 | tf_op jit(solution)/shard_map/all_to_all | solution.py:447
  180.6 2.0 %shard_map.124 = (f32[64,256]{1,0:T(8,128)}, f32[144,100]{1,0:T(8,128)}) custom-call(f32[128,1,128]{2,1,0:T(1,128)} %all_to_all.50.gram_ref, f32[64,256]{1,0:T(8,128)} %refs_0_.3, f32[64,256]{1,0:T(8,128)} %get-tuple-element.84.refs_1_, f32[64,256]{1,0:T(8,128)} %get-tuple-element.85.refs_2_, f32[144,128]{1,0:T(8,128)} %get-tuple-element.86.refs_3_, ...), custom_call_target="tpu_custom_call" | custom-call | bytes 3600000 | tf_op jit(solution)/shard_map/pallas_call | solution.py:571
  (16 shorter events, 0.0 us)
Async XLA Ops:
  0.6 25.2 %copy-start.13 = (s32[64]{0:T(128)S(1)}, s32[64]{0:T(128)}, u32[]{:S(2)}) copy-start(s32[64]{0:T(128)} %param.18) | copy-start | bytes 772
  0.6 32.1 %copy-start.14 = (s32[32,2]{0,1:T(2,128)S(1)}, s32[32,2]{0,1:T(2,128)}, u32[]{:S(2)}) copy-start(s32[32,2]{0,1:T(2,128)} %param.17) | copy-start | bytes 772
  0.7 54.4 %copy-start.3 = (bf16[144,4608]{1,0:T(8,128)(2,1)S(1)}, bf16[144,4608]{1,0:T(8,128)(2,1)}, u32[]{:S(2)}) copy-start(bf16[144,4608]{1,0:T(8,128)(2,1)} %op_ref.5) | copy-start | bytes 3981316
  4.8 21.2 %all-to-all-start = ((f32[32,3,8,128]{3,2,1,0:T(8,128)}), f32[32,3,8,128]{3,2,1,0:T(8,128)S(1)}, u32[]{:S(2)}, u32[]{:S(2)}) async-start(f32[32,3,8,128]{3,2,1,0:T(8,128)} %get-tuple-element.47), calls=%async_computation | async-start | bytes 786432 | tf_op jit(solution)/shard_map/all_to_all | solution.py:447
  25.9 7.4 %copy-start = (f32[32,3,8,128]{3,2,1,0:T(8,128)}, f32[32,3,8,128]{3,2,1,0:T(8,128)S(1)}, u32[]{:S(2)}) copy-start(f32[32,3,8,128]{3,2,1,0:T(8,128)S(1)} %all-to-all-done.recv_ref.info_ref) | copy-start | bytes 1179652
  26.0 21.1 %all-to-all-start.1 = ((bf16[16,144,128]{2,1,0:T(8,128)(2,1)}), bf16[16,144,128]{2,1,0:T(8,128)(2,1)}, u32[]{:S(2)}, u32[]{:S(2)}) async-start(bf16[16,144,128]{2,1,0:T(8,128)(2,1)} %get-tuple-element.49), calls=%async_computation.1 | async-start | bytes 1179648 | tf_op jit(solution)/shard_map/all_to_all | solution.py:447
  47.0 8.0 %collective-permute-start = (bf16[16,144,128]{2,1,0:T(8,128)(2,1)}, bf16[16,144,128]{2,1,0:T(8,128)(2,1)}, u32[]{:S(2)}, u32[]{:S(2)}) collective-permute-start(bf16[16,144,128]{2,1,0:T(8,128)(2,1)} %all-to-all-done.1.got_ref), channel_id=1, source_target_pairs={{0,1},{1,0},{2,3},{3,2},{4,5},{5,4},{6,7},{7,6},{8,9},{9,8},{10,11... | collective-permute-start | bytes 1769480 | tf_op jit(solution)/shard_map/ppermute | solution.py:539
  47.7 14.7 %all-to-all-start.2 = ((f32[32,4,128]{2,1,0:T(4,128)}), f32[32,4,128]{2,1,0:T(4,128)S(1)}, u32[]{:S(2)}, u32[]{:S(2)}) async-start(f32[32,4,128]{2,1,0:T(4,128)} %get-tuple-element.54), calls=%async_computation.2 | async-start | bytes 131072 | tf_op jit(solution)/shard_map/all_to_all | solution.py:447
  55.1 1.0 copy-start.1
  59.2 0.8 copy-start.5
  60.1 0.6 copy-start.6
  60.7 0.6 copy-start.11
  62.4 0.6 copy-start.12
  67.2 14.7 %all-to-all-start.3 = ((f32[32,3,4,128]{3,2,1,0:T(4,128)}), f32[32,3,4,128]{3,2,1,0:T(4,128)}, u32[]{:S(2)}, u32[]{:S(2)}) async-start(f32[32,3,4,128]{3,2,1,0:T(4,128)} %get-tuple-element.62), calls=%async_computation.3 | async-start | bytes 393216 | tf_op jit(solution)/shard_map/all_to_all | solution.py:447
  73.5 31.8 %copy-start.2 = (f32[32,3,8,128]{3,2,1,0:T(8,128)S(1)}, f32[32,3,8,128]{3,2,1,0:T(8,128)}, u32[]{:S(2)}) copy-start(f32[32,3,8,128]{3,2,1,0:T(8,128)} %copy-done) | copy-start | bytes 1179652
  81.8 16.3 %all-to-all-start.4 = ((bf16[16,144,128]{2,1,0:T(8,128)(2,1)}), bf16[16,144,128]{2,1,0:T(8,128)(2,1)}, u32[]{:S(2)}, u32[]{:S(2)}) async-start(bf16[16,144,128]{2,1,0:T(8,128)(2,1)} %copy-done.5), calls=%async_computation.4 | async-start | bytes 1179648 | tf_op jit(solution)/shard_map/all_to_all | solution.py:447
  98.1 7.2 %collective-permute-start.1 = (bf16[16,144,128]{2,1,0:T(8,128)(2,1)}, bf16[16,144,128]{2,1,0:T(8,128)(2,1)}, u32[]{:S(2)}, u32[]{:S(2)}) collective-permute-start(bf16[16,144,128]{2,1,0:T(8,128)(2,1)} %all-to-all-done.4.got_ref), channel_id=1, source_target_pairs={{0,1},{1,0},{2,3},{3,2},{4,5},{5,4},{6,7},{7,6},{8,9},{9,8},{10,11... | collective-permute-start | bytes 1769480 | tf_op jit(solution)/shard_map/ppermute | solution.py:539
  99.9 12.7 %all-to-all-start.5 = ((f32[32,4,128]{2,1,0:T(4,128)}), f32[32,4,128]{2,1,0:T(4,128)}, u32[]{:S(2)}, u32[]{:S(2)}) async-start(f32[32,4,128]{2,1,0:T(4,128)} %shard_map.118), calls=%async_computation.5 | async-start | bytes 131072 | tf_op jit(solution)/shard_map/all_to_all | solution.py:447
  108.5 0.8 copy-start.4
  109.4 0.6 copy-start.7
  110.0 0.6 copy-start.10
  116.7 13.8 %all-to-all-start.6 = ((f32[32,3,4,128]{3,2,1,0:T(4,128)}), f32[32,3,4,128]{3,2,1,0:T(4,128)}, u32[]{:S(2)}, u32[]{:S(2)}) async-start(f32[32,3,4,128]{3,2,1,0:T(4,128)} %get-tuple-element.75), calls=%async_computation.6 | async-start | bytes 393216 | tf_op jit(solution)/shard_map/all_to_all | solution.py:447
  130.5 16.2 %all-to-all-start.7 = ((bf16[16,144,128]{2,1,0:T(8,128)(2,1)}), bf16[16,144,128]{2,1,0:T(8,128)(2,1)}, u32[]{:S(2)}, u32[]{:S(2)}) async-start(bf16[16,144,128]{2,1,0:T(8,128)(2,1)} %copy-done.4), calls=%async_computation.7 | async-start | bytes 1179648 | tf_op jit(solution)/shard_map/all_to_all | solution.py:447
  146.7 7.2 %collective-permute-start.2 = (bf16[16,144,128]{2,1,0:T(8,128)(2,1)}, bf16[16,144,128]{2,1,0:T(8,128)(2,1)}, u32[]{:S(2)}, u32[]{:S(2)}) collective-permute-start(bf16[16,144,128]{2,1,0:T(8,128)(2,1)} %all-to-all-done.7.got_ref), channel_id=1, source_target_pairs={{0,1},{1,0},{2,3},{3,2},{4,5},{5,4},{6,7},{7,6},{8,9},{9,8},{10,11... | collective-permute-start | bytes 1769480 | tf_op jit(solution)/shard_map/ppermute | solution.py:539
  148.5 12.8 %all-to-all-start.8 = ((f32[32,4,128]{2,1,0:T(4,128)}), f32[32,4,128]{2,1,0:T(4,128)}, u32[]{:S(2)}, u32[]{:S(2)}) async-start(f32[32,4,128]{2,1,0:T(4,128)} %shard_map.121), calls=%async_computation.8 | async-start | bytes 131072 | tf_op jit(solution)/shard_map/all_to_all | solution.py:447
  157.1 0.6 copy-start.8
  157.7 0.6 copy-start.9

commit v4 on v3

--- a/solution.py
+++ b/solution.py
@@ -19,7 +19,7 @@
 LANES = 128
 NODES = ROWS * LANES
 PITCH = 40
-UNROLL = 4
+UNROLL = 8
 BATCH = 8
 TILES = 32
 ALL = 128

time: 184 us -> 182 us (0.989)
  Pallas kernels: 65.2 us -> 62.6 us
  transfers between devices with their start and end apart: 12 -> 12, of which waited for: 7 -> 7; matrix products, arithmetic and copies ran while one was open for 12% -> 12% of each run, Pallas kernels for 26% -> 25%
where the time goes in v4:
time: 182 us; the launch traced here: 180 us
  Pallas kernels  62.6 us (34%)
  starting transfers between devices  59 us (32%)
  matrix products  17 us (9%)
  blocking collectives  16.1 us (9%)
  waiting for transfers between devices  12.9 us (7%)
  local copies, waits for them, and re-layouts  9.73 us (5%)
  other arithmetic  2 us (1%)
    all_to_all x9, starting transfers between devices, exchange(): return lax.all_to_all(array, axis, split_axis=0, concat_axis=0, tiled=True)  54.8 us
    pallas_call x2, Pallas kernels, local(): call(near, result, specs + [VMEM, VMEM, block, block], scratch, 9.0, steps)  19.9 us
    dot_general x3, matrix products, local(): jnp.einsum('fij,fj->fi', fiber_ops, low, preferred_element_type=F32)  17 us
    all_to_all x1, blocking collectives, exchange(): return lax.all_to_all(array, axis, split_axis=0, concat_axis=0, tiled=True)  16.1 us
    all_to_all x9, waiting for transfers between devices, exchange(): return lax.all_to_all(array, axis, split_axis=0, concat_axis=0, tiled=True)  12.9 us
    pallas_call x1, Pallas kernels, local(): call(near, (result, spots, rims, shape(pairs, BF16), shape(pairs)), specs...  12.4 us
    pallas_call x3, Pallas kernels, local(): call(functools.partial(body_kernel, first, last), tuple(made), [SMEM] + [...  9.55 us
    pallas_call x2, Pallas kernels, local(): call(join_kernel, (shape((FIB, ORDER)), shape((FIB, ORDER), BF16), shape(...  8.3 us
  transfers between devices with their start and end apart: 12, of which 7 were waited for; matrix products, arithmetic and copies ran while one was open for 12% of the time, Pallas kernels for 25%

profile of v4, /device:TPU:1, one launch (start us, length us, event | category | flops | bytes accessed | tf_op | source)
XLA Modules:
  0.0 180.3 jit_solution(4674212783796121797)
XLA Ops:
  0.6 0.0 copy-start.13
  0.7 4.1 %shard_map.113 = (f32[32,3,8,128]{3,2,1,0:T(8,128)}, s32[32,128]{1,0:T(8,128)}) custom-call(f32[3,4096]{1,0:T(4,128)} %pos_ref.1, f32[64,256]{1,0:T(8,128)} %refs_0_.3, s32[1,4096]{1,0:T(1,128)} %send_ref.1, s32[1,4096]{1,0:T(1,128)} %leaf_ref.3, s32[1,64]{1,0:T(1,128)} %bitcast.27, s32[1,64]{1,0:T(1,128)} %bitcast.28), custom_call_target="tpu_custom_call" | custom-call | bytes 7200000 | tf_op jit(solution)/shard_map/pallas_call | solution.py:479
  4.8 9.6 %all-to-all-start = ((f32[32,3,8,128]{3,2,1,0:T(8,128)}), f32[32,3,8,128]{3,2,1,0:T(8,128)S(1)}, u32[]{:S(2)}, u32[]{:S(2)}) async-start(f32[32,3,8,128]{3,2,1,0:T(8,128)} %get-tuple-element.47), calls=%async_computation | async-start | bytes 786432 | tf_op jit(solution)/shard_map/all_to_all | solution.py:447
  14.4 0.8 convert_bitcast_fusion
  15.2 0.7 broadcast_add_fusion
  16.0 0.1 add.26
  16.1 0.4 fusion.take_ref
  16.4 5.6 %fusion.5 = f32[64,1,256]{2,1,0:T(1,128)S(1)} fusion(bf16[64,256,256]{2,1,0:T(8,128)(2,1)} %param.12, bf16[64,256,1]{1,0,2:T(8,128)(2,1)S(1)} %convert_bitcast_fusion), kind=kOutput, calls=%fused_computation.9 | convolution fusion | flops 8388608 | bytes 8486912 | tf_op jit(solution)/shard_map/fij,fj->fi/dot_general | solution.py:501
  22.1 0.7 copy.32
  22.7 3.2 %shard_map.114 = (s32[32,128]{1,0:T(8,128)}, s32[32,128]{1,0:T(8,128)}, s32[32,128]{1,0:T(8,128)}, f32[144,128]{1,0:T(8,128)}, bf16[16,144,128]{2,1,0:T(8,128)(2,1)}) custom-call(s32[1,4096]{1,0:T(1,128)} %leaf_ref.3, s32[1,4096]{1,0:T(1,128)} %send_ref.1, f32[144,100]{1,0:T(8,128)} %bitcast.26), custom_call_target="tpu_custom_call" | custom-call | bytes 7200000 | tf_op jit(solution)/shard_map/pallas_call | solution.py:489
  25.9 0.1 fusion.7.mine_ref
  25.9 0.0 all-to-all-done.recv_ref.info_ref
  25.9 0.0 copy-start
  26.0 6.7 %all-to-all-start.1 = ((bf16[16,144,128]{2,1,0:T(8,128)(2,1)}), bf16[16,144,128]{2,1,0:T(8,128)(2,1)}, u32[]{:S(2)}, u32[]{:S(2)}) async-start(bf16[16,144,128]{2,1,0:T(8,128)(2,1)} %get-tuple-element.49), calls=%async_computation.1 | async-start | bytes 1179648 | tf_op jit(solution)/shard_map/all_to_all | solution.py:447
  32.7 0.0 copy-done.14
  32.7 0.7 copy.12.mask_ref
  33.4 12.4 %shard_map.115 = (f32[32,4,128]{2,1,0:T(4,128)}, f32[3,40,128]{2,1,0:T(8,128)}, s32[16,128]{1,0:T(8,128)}, bf16[32,3,128,128]{3,2,1,0:T(8,128)(2,1)}, f32[32,3,128,128]{3,2,1,0:T(8,128)}) custom-call(s32[1]{0:T(128)} %bitcast.5.tile_ref, s32[32,2]{1,0:T(8,128)} %copy.12.mask_ref, f32[32,3,8,128]{3,2,1,0:T(8,128)} %copy-done, ...), custom_call_target="tpu_custom_call" | custom-call | bytes 46800000 | tf_op jit(solution)/shard_map/pallas_call | solution.py:525
  45.8 0.0 all-to-all-done.1.got_ref
  45.8 0.7 collective-permute-start
  46.4 7.3 %all-to-all-start.2 = ((f32[32,4,128]{2,1,0:T(4,128)}), f32[32,4,128]{2,1,0:T(4,128)S(1)}, u32[]{:S(2)}, u32[]{:S(2)}) async-start(f32[32,4,128]{2,1,0:T(4,128)} %get-tuple-element.54), calls=%async_computation.2 | async-start | bytes 131072 | tf_op jit(solution)/shard_map/all_to_all | solution.py:447
  53.8 0.0 collective-permute-done.mate_ref
  53.8 1.0 copy-done.1
  54.8 3.2 %shard_map.116 = (f32[144,128]{1,0:T(8,128)S(1)}, f32[64,128]{1,0:T(8,128)S(1)}, bf16[16,144,128]{2,1,0:T(8,128)(2,1)S(1)}) custom-call(s32[1]{0:T(128)} %bitcast.5.tile_ref, bf16[16,144,128]{2,1,0:T(8,128)(2,1)} %all-to-all-done.1.got_ref, bf16[16,144,128]{2,1,0:T(8,128)(2,1)} %collective-permute-done.mate_ref, bf16[144,4608]{1,0:T(8,128)(2,1)S(1)} %copy-done.3, ...), custom_call_target="tpu_custom_call" | custom-call | bytes 14400000 | tf_op jit(solution)/shard_map/pallas_call | solution.py:544
  58.0 0.8 copy-done.5
  58.8 0.6 copy-done.6
  59.4 0.6 copy-done.11
  60.0 1.1 all-to-all-done.2.back_ref
  61.1 0.6 copy-done.12
  61.7 4.2 %shard_map.117 = (f32[64,256]{1,0:T(8,128)}, bf16[64,256]{1,0:T(8,128)(2,1)}, f32[32,3,4,128]{3,2,1,0:T(4,128)}) custom-call(f32[32,4,128]{2,1,0:T(4,128)} %copy-done.12, s32[32,128]{1,0:T(8,128)} %get-tuple-element.55.inv_ref, f32[64,256]{1,0:T(8,128)} %bitcast.21, f32[64,128]{1,0:T(8,128)} %copy-done.11, s32[32,128]{1,0:T(8,128)} %get-tuple-element.61.index_ref), custom_call_target="tpu_custom_call" | custom-call | bytes 7200000 | tf_op jit(solution)/shard_map/pallas_call | solution.py:555
  65.9 6.5 %all-to-all-start.3 = ((f32[32,3,4,128]{3,2,1,0:T(4,128)}), f32[32,3,4,128]{3,2,1,0:T(4,128)}, u32[]{:S(2)}, u32[]{:S(2)}) async-start(f32[32,3,4,128]{3,2,1,0:T(4,128)} %get-tuple-element.62), calls=%async_computation.3 | async-start | bytes 393216 | tf_op jit(solution)/shard_map/all_to_all | solution.py:447
  72.4 5.7 %fusion.3 = f32[64,1,256]{2,1,0:T(1,128)S(1)} fusion(bf16[64,256,256]{2,1,0:T(8,128)(2,1)} %param.12, bf16[64,256,1]{1,0,2:T(8,128)(2,1)} %bitcast.25), kind=kOutput, calls=%fused_computation.6 | convolution fusion | flops 8388608 | bytes 8486912 | tf_op jit(solution)/shard_map/fij,fj->fi/dot_general | solution.py:501
  78.1 0.7 copy.31
  78.8 1.9 %all-to-all-done.3.recv_ref = f32[32,3,4,128]{3,2,1,0:T(4,128)} async-done(((f32[32,3,4,128]{3,2,1,0:T(4,128)}), f32[32,3,4,128]{3,2,1,0:T(4,128)}, u32[]{:S(2)}, u32[]{:S(2)}) %all-to-all-start.3) | async-done | bytes 196640 | tf_op jit(solution)/shard_map/all_to_all | solution.py:447
  80.7 4.8 %all-to-all-start.4 = ((bf16[16,144,128]{2,1,0:T(8,128)(2,1)}), bf16[16,144,128]{2,1,0:T(8,128)(2,1)}, u32[]{:S(2)}, u32[]{:S(2)}) async-start(bf16[16,144,128]{2,1,0:T(8,128)(2,1)} %copy-done.5), calls=%async_computation.4 | async-start | bytes 1179648 | tf_op jit(solution)/shard_map/all_to_all | solution.py:447
  85.5 9.9 %shard_map.118 = f32[32,4,128]{2,1,0:T(4,128)} custom-call(s32[1]{0:T(128)} %bitcast.5.tile_ref, s32[32,2]{1,0:T(8,128)} %copy.12.mask_ref, f32[32,3,4,128]{3,2,1,0:T(4,128)} %all-to-all-done.3.recv_ref, s32[32,128]{1,0:T(8,128)} %get-tuple-element.51.index_ref, s32[32,128]{1,0:T(8,128)} %get-tuple-element.52.inv_ref, ...), custom_call_target="tpu_custom_call" | custom-call | bytes 32400000 | tf_op jit(solution)/shard_map/pallas_call | solution.py:535
  95.5 1.5 all-to-all-done.4.got_ref
  97.0 1.8 collective-permute-start.1
  98.8 4.7 %all-to-all-start.5 = ((f32[32,4,128]{2,1,0:T(4,128)}), f32[32,4,128]{2,1,0:T(4,128)}, u32[]{:S(2)}, u32[]{:S(2)}) async-start(f32[32,4,128]{2,1,0:T(4,128)} %shard_map.118), calls=%async_computation.5 | async-start | bytes 131072 | tf_op jit(solution)/shard_map/all_to_all | solution.py:447
  103.5 0.0 collective-permute-done.1.mate_ref
  103.5 3.2 %shard_map.119 = (f32[144,128]{1,0:T(8,128)S(1)}, f32[64,128]{1,0:T(8,128)S(1)}, bf16[16,144,128]{2,1,0:T(8,128)(2,1)S(1)}) custom-call(s32[1]{0:T(128)} %bitcast.5.tile_ref, bf16[16,144,128]{2,1,0:T(8,128)(2,1)} %all-to-all-done.4.got_ref, bf16[16,144,128]{2,1,0:T(8,128)(2,1)} %collective-permute-done.1.mate_ref, bf16[144,4608]{1,0:T(8,128)(2,1)S(1)} %copy-done.3, ...), custom_call_target="tpu_custom_call" | custom-call | bytes 14400000 | tf_op jit(solution)/shard_map/pallas_call | solution.py:544
  106.8 0.0 copy-start.4
  106.8 0.8 copy-done.4
  107.6 0.6 copy-done.7
  108.2 0.6 copy-done.10
  108.8 2.0 %all-to-all-done.5.back_ref = f32[32,4,128]{2,1,0:T(4,128)} async-done(((f32[32,4,128]{2,1,0:T(4,128)}), f32[32,4,128]{2,1,0:T(4,128)}, u32[]{:S(2)}, u32[]{:S(2)}) %all-to-all-start.5) | async-done | bytes 65568 | tf_op jit(solution)/shard_map/all_to_all | solution.py:447
  110.8 4.2 %shard_map.120 = (f32[64,256]{1,0:T(8,128)}, bf16[64,256]{1,0:T(8,128)(2,1)}, f32[32,3,4,128]{3,2,1,0:T(4,128)}) custom-call(f32[32,4,128]{2,1,0:T(4,128)} %all-to-all-done.5.back_ref, s32[32,128]{1,0:T(8,128)} %get-tuple-element.55.inv_ref, f32[64,256]{1,0:T(8,128)} %bitcast.23, f32[64,128]{1,0:T(8,128)} %copy-done.10, s32[32,128]{1,0:T(8,128)} %get-tuple-element.61.index_ref), custom_call_target="tpu_custom_call" | custom-call | bytes 7200000 | tf_op jit(solution)/shard_map/pallas_call | solution.py:555
  114.9 5.5 %all-to-all-start.6 = ((f32[32,3,4,128]{3,2,1,0:T(4,128)}), f32[32,3,4,128]{3,2,1,0:T(4,128)}, u32[]{:S(2)}, u32[]{:S(2)}) async-start(f32[32,3,4,128]{3,2,1,0:T(4,128)} %get-tuple-element.75), calls=%async_computation.6 | async-start | bytes 393216 | tf_op jit(solution)/shard_map/all_to_all | solution.py:447
  120.4 5.7 %fusion.1 = f32[64,1,256]{2,1,0:T(1,128)S(1)} fusion(bf16[64,256,256]{2,1,0:T(8,128)(2,1)} %param.12, bf16[64,256,1]{1,0,2:T(8,128)(2,1)} %bitcast.24), kind=kOutput, calls=%fused_computation.3 | convolution fusion | flops 8388608 | bytes 8486912 | tf_op jit(solution)/shard_map/fij,fj->fi/dot_general | solution.py:501
  126.1 0.6 copy.30
  126.7 2.0 %all-to-all-done.6.recv_ref = f32[32,3,4,128]{3,2,1,0:T(4,128)} async-done(((f32[32,3,4,128]{3,2,1,0:T(4,128)}), f32[32,3,4,128]{3,2,1,0:T(4,128)}, u32[]{:S(2)}, u32[]{:S(2)}) %all-to-all-start.6) | async-done | bytes 196640 | tf_op jit(solution)/shard_map/all_to_all | solution.py:447
  128.7 4.7 %all-to-all-start.7 = ((bf16[16,144,128]{2,1,0:T(8,128)(2,1)}), bf16[16,144,128]{2,1,0:T(8,128)(2,1)}, u32[]{:S(2)}, u32[]{:S(2)}) async-start(bf16[16,144,128]{2,1,0:T(8,128)(2,1)} %copy-done.4), calls=%async_computation.7 | async-start | bytes 1179648 | tf_op jit(solution)/shard_map/all_to_all | solution.py:447
  133.4 9.9 %shard_map.121 = f32[32,4,128]{2,1,0:T(4,128)} custom-call(s32[1]{0:T(128)} %bitcast.5.tile_ref, s32[32,2]{1,0:T(8,128)} %copy.12.mask_ref, f32[32,3,4,128]{3,2,1,0:T(4,128)} %all-to-all-done.6.recv_ref, s32[32,128]{1,0:T(8,128)} %get-tuple-element.51.index_ref, s32[32,128]{1,0:T(8,128)} %get-tuple-element.52.inv_ref, ...), custom_call_target="tpu_custom_call" | custom-call | bytes 32400000 | tf_op jit(solution)/shard_map/pallas_call | solution.py:535
  143.4 1.5 all-to-all-done.7.got_ref
  144.9 1.8 collective-permute-start.2
  146.7 4.9 %all-to-all-start.8 = ((f32[32,4,128]{2,1,0:T(4,128)}), f32[32,4,128]{2,1,0:T(4,128)}, u32[]{:S(2)}, u32[]{:S(2)}) async-start(f32[32,4,128]{2,1,0:T(4,128)} %shard_map.121), calls=%async_computation.8 | async-start | bytes 131072 | tf_op jit(solution)/shard_map/all_to_all | solution.py:447
  151.6 0.0 collective-permute-done.2.mate_ref
  151.6 3.2 %shard_map.122 = (f32[144,128]{1,0:T(8,128)S(1)}, f32[64,128]{1,0:T(8,128)S(1)}) custom-call(s32[1]{0:T(128)} %bitcast.5.tile_ref, bf16[16,144,128]{2,1,0:T(8,128)(2,1)} %all-to-all-done.7.got_ref, bf16[16,144,128]{2,1,0:T(8,128)(2,1)} %collective-permute-done.2.mate_ref, bf16[144,4608]{1,0:T(8,128)(2,1)S(1)} %copy-done.3, ...), custom_call_target="tpu_custom_call" | custom-call | bytes 14400000 | tf_op jit(solution)/shard_map/pallas_call | solution.py:544
  154.8 0.0 copy-start.8
  154.8 0.6 copy-done.8
  155.4 0.6 copy-done.9
  156.0 2.9 %all-to-all-done.8.back_ref = f32[32,4,128]{2,1,0:T(4,128)} async-done(((f32[32,4,128]{2,1,0:T(4,128)}), f32[32,4,128]{2,1,0:T(4,128)}, u32[]{:S(2)}, u32[]{:S(2)}) %all-to-all-start.8) | async-done | bytes 65568 | tf_op jit(solution)/shard_map/all_to_all | solution.py:447
  158.9 3.2 %shard_map.123 = f32[128,1,128]{2,1,0:T(1,128)} custom-call(f32[32,4,128]{2,1,0:T(4,128)} %all-to-all-done.8.back_ref, s32[32,128]{1,0:T(8,128)} %get-tuple-element.55.inv_ref, f32[64,256]{1,0:T(8,128)} %bitcast.22, f32[64,128]{1,0:T(8,128)} %copy-done.9, f32[64,256]{1,0:T(8,128)} %refs_0_.3, f32[64,256]{1,0:T(8,128)} %get-tuple-element.84.refs_1_, ...), custom_call_target="tpu_custom_call" | custom-call | bytes 7200000 | tf_op jit(solution)/shard_map/pallas_call | solution.py:563
  162.1 16.1 %all_to_all.50.gram_ref = f32[128,1,128]{2,1,0:T(1,128)} all-to-all(f32[128,1,128]{2,1,0:T(1,128)} %shard_map.123), channel_id=1, replica_groups=mesh['grp'=4,'chip'=16,'core'=2] {'grp','chip','core'}, dimensions={0} | all-to-all | bytes 131072 | tf_op jit(solution)/shard_map/all_to_all | solution.py:447
  178.2 2.0 %shard_map.124 = (f32[64,256]{1,0:T(8,128)}, f32[144,100]{1,0:T(8,128)}) custom-call(f32[128,1,128]{2,1,0:T(1,128)} %all_to_all.50.gram_ref, f32[64,256]{1,0:T(8,128)} %refs_0_.3, f32[64,256]{1,0:T(8,128)} %get-tuple-element.84.refs_1_, f32[64,256]{1,0:T(8,128)} %get-tuple-element.85.refs_2_, f32[144,128]{1,0:T(8,128)} %get-tuple-element.86.refs_3_, ...), custom_call_target="tpu_custom_call" | custom-call | bytes 3600000 | tf_op jit(solution)/shard_map/pallas_call | solution.py:571
  (16 shorter events, 0.0 us)
Async XLA Ops:
  0.6 25.2 %copy-start.13 = (s32[64]{0:T(128)S(1)}, s32[64]{0:T(128)}, u32[]{:S(2)}) copy-start(s32[64]{0:T(128)} %param.18) | copy-start | bytes 772
  0.6 32.1 %copy-start.14 = (s32[32,2]{0,1:T(2,128)S(1)}, s32[32,2]{0,1:T(2,128)}, u32[]{:S(2)}) copy-start(s32[32,2]{0,1:T(2,128)} %param.17) | copy-start | bytes 772
  0.7 53.1 %copy-start.3 = (bf16[144,4608]{1,0:T(8,128)(2,1)S(1)}, bf16[144,4608]{1,0:T(8,128)(2,1)}, u32[]{:S(2)}) copy-start(bf16[144,4608]{1,0:T(8,128)(2,1)} %op_ref.5) | copy-start | bytes 3981316
  4.8 21.2 %all-to-all-start = ((f32[32,3,8,128]{3,2,1,0:T(8,128)}), f32[32,3,8,128]{3,2,1,0:T(8,128)S(1)}, u32[]{:S(2)}, u32[]{:S(2)}) async-start(f32[32,3,8,128]{3,2,1,0:T(8,128)} %get-tuple-element.47), calls=%async_computation | async-start | bytes 786432 | tf_op jit(solution)/shard_map/all_to_all | solution.py:447
  25.9 7.4 %copy-start = (f32[32,3,8,128]{3,2,1,0:T(8,128)}, f32[32,3,8,128]{3,2,1,0:T(8,128)S(1)}, u32[]{:S(2)}) copy-start(f32[32,3,8,128]{3,2,1,0:T(8,128)S(1)} %all-to-all-done.recv_ref.info_ref) | copy-start | bytes 1179652
  26.0 19.8 %all-to-all-start.1 = ((bf16[16,144,128]{2,1,0:T(8,128)(2,1)}), bf16[16,144,128]{2,1,0:T(8,128)(2,1)}, u32[]{:S(2)}, u32[]{:S(2)}) async-start(bf16[16,144,128]{2,1,0:T(8,128)(2,1)} %get-tuple-element.49), calls=%async_computation.1 | async-start | bytes 1179648 | tf_op jit(solution)/shard_map/all_to_all | solution.py:447
  45.8 8.0 %collective-permute-start = (bf16[16,144,128]{2,1,0:T(8,128)(2,1)}, bf16[16,144,128]{2,1,0:T(8,128)(2,1)}, u32[]{:S(2)}, u32[]{:S(2)}) collective-permute-start(bf16[16,144,128]{2,1,0:T(8,128)(2,1)} %all-to-all-done.1.got_ref), channel_id=1, source_target_pairs={{0,1},{1,0},{2,3},{3,2},{4,5},{5,4},{6,7},{7,6},{8,9},{9,8},{10,11... | collective-permute-start | bytes 1769480 | tf_op jit(solution)/shard_map/ppermute | solution.py:539
  46.4 14.7 %all-to-all-start.2 = ((f32[32,4,128]{2,1,0:T(4,128)}), f32[32,4,128]{2,1,0:T(4,128)S(1)}, u32[]{:S(2)}, u32[]{:S(2)}) async-start(f32[32,4,128]{2,1,0:T(4,128)} %get-tuple-element.54), calls=%async_computation.2 | async-start | bytes 131072 | tf_op jit(solution)/shard_map/all_to_all | solution.py:447
  53.8 1.0 copy-start.1
  58.0 0.8 copy-start.5
  58.8 0.6 copy-start.6
  59.4 0.6 copy-start.11
  61.1 0.6 copy-start.12
  65.9 14.8 %all-to-all-start.3 = ((f32[32,3,4,128]{3,2,1,0:T(4,128)}), f32[32,3,4,128]{3,2,1,0:T(4,128)}, u32[]{:S(2)}, u32[]{:S(2)}) async-start(f32[32,3,4,128]{3,2,1,0:T(4,128)} %get-tuple-element.62), calls=%async_computation.3 | async-start | bytes 393216 | tf_op jit(solution)/shard_map/all_to_all | solution.py:447
  72.4 31.1 %copy-start.2 = (f32[32,3,8,128]{3,2,1,0:T(8,128)S(1)}, f32[32,3,8,128]{3,2,1,0:T(8,128)}, u32[]{:S(2)}) copy-start(f32[32,3,8,128]{3,2,1,0:T(8,128)} %copy-done) | copy-start | bytes 1179652
  80.7 16.3 %all-to-all-start.4 = ((bf16[16,144,128]{2,1,0:T(8,128)(2,1)}), bf16[16,144,128]{2,1,0:T(8,128)(2,1)}, u32[]{:S(2)}, u32[]{:S(2)}) async-start(bf16[16,144,128]{2,1,0:T(8,128)(2,1)} %copy-done.5), calls=%async_computation.4 | async-start | bytes 1179648 | tf_op jit(solution)/shard_map/all_to_all | solution.py:447
  97.0 6.5 %collective-permute-start.1 = (bf16[16,144,128]{2,1,0:T(8,128)(2,1)}, bf16[16,144,128]{2,1,0:T(8,128)(2,1)}, u32[]{:S(2)}, u32[]{:S(2)}) collective-permute-start(bf16[16,144,128]{2,1,0:T(8,128)(2,1)} %all-to-all-done.4.got_ref), channel_id=1, source_target_pairs={{0,1},{1,0},{2,3},{3,2},{4,5},{5,4},{6,7},{7,6},{8,9},{9,8},{10,11... | collective-permute-start | bytes 1769480 | tf_op jit(solution)/shard_map/ppermute | solution.py:539
  98.8 12.0 %all-to-all-start.5 = ((f32[32,4,128]{2,1,0:T(4,128)}), f32[32,4,128]{2,1,0:T(4,128)}, u32[]{:S(2)}, u32[]{:S(2)}) async-start(f32[32,4,128]{2,1,0:T(4,128)} %shard_map.118), calls=%async_computation.5 | async-start | bytes 131072 | tf_op jit(solution)/shard_map/all_to_all | solution.py:447
  106.8 0.8 copy-start.4
  107.6 0.6 copy-start.7
  108.2 0.6 copy-start.10
  114.9 13.8 %all-to-all-start.6 = ((f32[32,3,4,128]{3,2,1,0:T(4,128)}), f32[32,3,4,128]{3,2,1,0:T(4,128)}, u32[]{:S(2)}, u32[]{:S(2)}) async-start(f32[32,3,4,128]{3,2,1,0:T(4,128)} %get-tuple-element.75), calls=%async_computation.6 | async-start | bytes 393216 | tf_op jit(solution)/shard_map/all_to_all | solution.py:447
  128.7 16.2 %all-to-all-start.7 = ((bf16[16,144,128]{2,1,0:T(8,128)(2,1)}), bf16[16,144,128]{2,1,0:T(8,128)(2,1)}, u32[]{:S(2)}, u32[]{:S(2)}) async-start(bf16[16,144,128]{2,1,0:T(8,128)(2,1)} %copy-done.4), calls=%async_computation.7 | async-start | bytes 1179648 | tf_op jit(solution)/shard_map/all_to_all | solution.py:447
  144.9 6.7 %collective-permute-start.2 = (bf16[16,144,128]{2,1,0:T(8,128)(2,1)}, bf16[16,144,128]{2,1,0:T(8,128)(2,1)}, u32[]{:S(2)}, u32[]{:S(2)}) collective-permute-start(bf16[16,144,128]{2,1,0:T(8,128)(2,1)} %all-to-all-done.7.got_ref), channel_id=1, source_target_pairs={{0,1},{1,0},{2,3},{3,2},{4,5},{5,4},{6,7},{7,6},{8,9},{9,8},{10,11... | collective-permute-start | bytes 1769480 | tf_op jit(solution)/shard_map/ppermute | solution.py:539
  146.7 12.3 %all-to-all-start.8 = ((f32[32,4,128]{2,1,0:T(4,128)}), f32[32,4,128]{2,1,0:T(4,128)}, u32[]{:S(2)}, u32[]{:S(2)}) async-start(f32[32,4,128]{2,1,0:T(4,128)} %shard_map.121), calls=%async_computation.8 | async-start | bytes 131072 | tf_op jit(solution)/shard_map/all_to_all | solution.py:447
  154.8 0.6 copy-start.8
  155.4 0.6 copy-start.9
